TPU v7x, 1024 devices: a whole 4x4x32 slice. The times are simulated.
1024 devices in a mesh: replica: 16 (over z_lo), fsdp: 8 (over y, z_hi), tensor: 8 (over x, core).
Axes of the slice: x: 4, y: 4, z: 32 (z_hi: 2, z_lo: 16; z = z_hi * 16 + z_lo), core: 2. Of those that a mesh axis runs over, the one named last changes fastest.
Arguments:
- activations: bfloat16 [16384, 8192], P(('replica', 'fsdp')), may hold values from -6 to 6
- value_grads: bfloat16 [16384, 2048], P(('replica', 'fsdp'), 'tensor'), may hold values from -6 to 6
- lengths: int32 [256], P(('replica', 'fsdp')), may hold values from 16 to 64, as said below
- master: float32 [8192, 2048], P('fsdp', 'tensor'), may hold values from -0.0625 to 0.0625
- moment_one: float32 [8192, 2048], P('fsdp', 'tensor'), may hold values from -0.078125 to 0.078125
- moment_two: float32 [8192, 2048], P('fsdp', 'tensor'), may hold values from 1e-06 to 0.0001
Outputs:
- input_grads: bfloat16 [16384, 8192], P(('replica', 'fsdp'), 'tensor')
- new_master: float32 [8192, 2048], P('fsdp', 'tensor')
- new_moment_one: float32 [8192, 2048], P('fsdp', 'tensor')
- new_moment_two: float32 [8192, 2048], P('fsdp', 'tensor')
Inputs may be any that keep to these rules, and one draw needn't show every extreme that they name: `lengths`: each sequence's live tokens form a prefix of its 64 positions.
All inputs are finite; a program needn't handle non-finite values.
Results may differ from a plain program's by a relative error of at most 0.014.
Values may be sent and summed in bfloat16 or wider, within the bound.
No kernel may reach another device: no remote copies, remote signals or barrier semaphores. Data moves between devices by JAX's collectives and lax.ppermute only.
A program may use at most 64 MiB of HBM per device.

v0:
```python
import jax
import jax.numpy as jnp
from jax import lax
from jax.sharding import Mesh
from jax.sharding import PartitionSpec as P

FSDP = ("fsdp_0", "fsdp_1")
REPLICA_FSDP = ("replica", "fsdp_0", "fsdp_1")


beta_one = 0.9
beta_two = 0.95
learn_rate = 0.001
weight_decay = 0.1
adam_step = 10
epsilon = 1e-08


def split_up(array, dim, count):
    shape = array.shape
    pieces = array.reshape(*shape[:dim], count, shape[dim] // count, *shape[dim + 1 :])
    return jnp.moveaxis(pieces, dim, 0)


def sent_and_summed(array, axis, dim):
    pieces = split_up(array, dim, lax.axis_size(axis))
    arrived = lax.all_to_all(pieces, axis, split_axis=0, concat_axis=0, tiled=True)
    return arrived.astype(jnp.float32).sum(axis=0)


def sum_by_axis(terms, axes):
    total = terms.astype(jnp.bfloat16)
    for axis in axes:
        total = lax.psum_scatter(total, axis, scatter_dimension=0, tiled=True)
    return total.astype(jnp.float32)


def sent_together(arrays, axis, dim, along):
    widths = [a.shape[along] for a in arrays]
    both = jnp.concatenate(arrays, axis=along)
    out = lax.all_gather(both, axis, axis=dim, tiled=True)
    return tuple(jnp.split(out, [sum(widths[:k]) for k in range(1, len(widths))], axis=along))


def adamw(grad, master, moment_one, moment_two):
    first = beta_one * moment_one + (1.0 - beta_one) * grad
    second = beta_two * moment_two + (1.0 - beta_two) * grad * grad
    first_hat = first / (1.0 - beta_one**adam_step)
    second_hat = second / (1.0 - beta_two**adam_step)
    updated = master - learn_rate * (
        first_hat / (jnp.sqrt(second_hat) + epsilon) + weight_decay * master
    )
    return (updated, first, second)


def local(activations, value_grads, lengths, master, moment_one, moment_two):
    tok_rows = activations.shape[0]
    seq_count = lengths.shape[0]
    seq_len = tok_rows // seq_count
    index = jnp.arange(tok_rows, dtype=jnp.int32)
    owner = index // seq_len
    pick = owner[:, None] == jnp.arange(seq_count, dtype=jnp.int32)[None, :]
    limit = jnp.sum(jnp.where(pick, lengths[None, :], 0), axis=1)
    masked = jnp.where((index % seq_len < limit)[:, None], value_grads, jnp.zeros_like(value_grads))
    weight = master.astype(jnp.bfloat16)
    terms = lax.dot_general(
        masked,
        lax.all_gather(weight, FSDP, axis=0, tiled=True),
        (((1,), (1,)), ((), ())),
        preferred_element_type=jnp.float32,
    )
    input_grads = sent_and_summed(terms.astype(jnp.bfloat16), "tensor", 1).astype(jnp.bfloat16)
    shard_rows = sum_by_axis(
        lax.dot_general(
            activations, masked, (((0,), (0,)), ((), ())), preferred_element_type=jnp.float32
        ),
        FSDP,
    )
    count = float(tok_rows * lax.axis_size("replica") * lax.axis_size(FSDP))
    share = sent_and_summed(shard_rows.astype(jnp.bfloat16), "replica", 0)
    rows = share.shape[0]
    begin = lax.axis_index("replica") * rows
    own_master = lax.dynamic_slice_in_dim(master, begin, rows, 0)
    own_one = lax.dynamic_slice_in_dim(moment_one, begin, rows, 0)
    own_two = lax.dynamic_slice_in_dim(moment_two, begin, rows, 0)
    part_master, part_one, part_two = adamw(share / count, own_master, own_one, own_two)
    new_master, new_one, new_two = tuple(
        (
            part.astype(jnp.float32)
            for part in sent_together(
                (
                    part_master.astype(jnp.bfloat16),
                    part_one.astype(jnp.bfloat16),
                    part_two.astype(jnp.bfloat16),
                ),
                "replica",
                0,
                1,
            )
        )
    )
    return (input_grads, new_master, new_one, new_two)


def solution(mesh):
    split = Mesh(
        mesh.devices.reshape(mesh.shape["replica"], 4, 2, mesh.shape["tensor"]),
        ("replica", "fsdp_0", "fsdp_1", "tensor"),
    )
    in_specs = (
        P(REPLICA_FSDP, None),
        P(REPLICA_FSDP, "tensor"),
        P(REPLICA_FSDP),
        P(FSDP, "tensor"),
        P(FSDP, "tensor"),
        P(FSDP, "tensor"),
    )
    out_specs = (P(REPLICA_FSDP, "tensor"), P(FSDP, "tensor"), P(FSDP, "tensor"), P(FSDP, "tensor"))
    return jax.shard_map(local, mesh=split, in_specs=in_specs, out_specs=out_specs, check_vma=False)
```

profile of v0, /device:TPU:4, one launch (start us, length us, event | category | flops | bytes accessed | tf_op | source)
XLA Modules:
  0.0 707.6 jit_solution(13584505713971137484)
XLA Ops:
  8.0 0.0 copy-start
  8.0 0.0 reduce-scatter.3.cloned.1.call-start
  8.1 0.9 fusion.3
  9.0 0.7 copy-done
  9.6 4.1 fusion
  13.7 0.0 copy-start.1
  13.7 0.0 reduce-scatter.3.cloned.1.call-update
  13.8 0.0 reduce-scatter.5.cloned.1.call-start
  13.8 72.3 %reduce-scatter.3.cloned.1.call-done = bf16[2048,256]{0,1:T(8,128)(2,1)} async-done(((bf16[8192,256]{0,1:T(8,128)(2,1)}), bf16[2048,256]{0,1:T(8,128)(2,1)}) %reduce-scatter.3.cloned.1.call-update) | async-done | bytes 1048592 | tf_op jit(solution)/shard_map/reduce_scatter | solution.py:34
  86.1 0.0 reduce-scatter.5.cloned.1.call-update
  86.2 0.0 all-gather.3.cloned.1.call-start
  86.2 0.0 copy-done.1
  86.2 0.8 convert_element_type.37
  87.1 0.0 copy-start.2
  87.1 0.0 all-gather.3.cloned.1.call-update
  87.1 95.9 %reduce-scatter.5.cloned.1.call-done = bf16[1024,256]{0,1:T(8,128)(2,1)} async-done(((bf16[2048,256]{0,1:T(8,128)(2,1)}), bf16[1024,256]{0,1:T(8,128)(2,1)}) %reduce-scatter.5.cloned.1.call-update) | async-done | bytes 524304 | tf_op jit(solution)/shard_map/reduce_scatter | solution.py:34
  183.0 2.0 copy.14
  185.1 86.6 %all-to-all-start.1 = ((bf16[16,64,256]{2,1,0:T(8,128)(2,1)}), bf16[16,64,256]{2,1,0:T(8,128)(2,1)S(1)}, u32[]{:S(2)}, u32[]{:S(2)}) async-start(bf16[16,64,256]{2,1,0:T(8,128)(2,1)} %bitcast.2), calls=%async_computation.3 | async-start | bytes 1048576 | tf_op jit(solution)/shard_map/all_to_all | solution.py:27
  271.7 0.0 all-gather.5.cloned.1.call-start
  271.8 195.2 %all-to-all-done.1 = bf16[16,64,256]{2,1,0:T(8,128)(2,1)S(1)} async-done(((bf16[16,64,256]{2,1,0:T(8,128)(2,1)}), bf16[16,64,256]{2,1,0:T(8,128)(2,1)S(1)}, u32[]{:S(2)}, u32[]{:S(2)}) %all-to-all-start.1) | async-done | bytes 524320 | tf_op jit(solution)/shard_map/all_to_all | solution.py:27
  467.0 0.1 convert_reduce_fusion
  467.1 1.0 subtract_convert_fusion
  468.0 0.6 pad_maximum_fusion
  468.7 0.0 all-gather.5.cloned.1.call-update
  468.7 0.0 all-gather.3.cloned.1.call-done
  468.7 0.0 copy-done.2
  468.8 3.7 convolution_convert_fusion.1
  472.4 0.2 copy.17
  472.6 29.0 %all_to_all.10 = bf16[8,128,1024]{2,1,0:T(8,128)(2,1)} all-to-all(bf16[8,128,1024]{2,1,0:T(8,128)(2,1)S(1)} %bitcast.13), channel_id=1, replica_groups=mesh['replica'=16,'fsdp_0'=4,'fsdp_1'=2,'tensor'=8] {'tensor'}, dimensions={0} | all-to-all | bytes 4194304 | tf_op jit(solution)/shard_map/all_to_all | solution.py:27
  501.7 2.7 reduce_sum.31
  504.4 192.6 %all-gather.5.cloned.1.call-done = bf16[1024,768]{1,0:T(8,128)(2,1)} async-done(((bf16[64,768]{1,0:T(8,128)(2,1)}), bf16[1024,768]{1,0:T(8,128)(2,1)}) %all-gather.5.cloned.1.call-update) | async-done | bytes 1572880 | tf_op jit(solution)/shard_map/all_gather | solution.py:41
  697.0 3.1 slice_convert_fusion
  (2 shorter events, 0.0 us)
Async XLA Ops:
  8.0 1.6 copy-start
  8.0 78.1 %reduce-scatter.3.cloned.1.call-start = ((), (), s32[]{:S(2)}) async-start(), calls=%async_computation.5 | async-start | bytes 5242880 | tf_op jit(solution)/shard_map/reduce_scatter | solution.py:34
  13.7 72.5 %copy-start.1 = (f32[1024,256]{1,0:T(8,128)S(1)}, f32[1024,256]{1,0:T(8,128)}, u32[]{:S(2)}) copy-start(f32[1024,256]{1,0:T(8,128)} %param.9) | copy-start | bytes 3145732
  13.8 169.3 %reduce-scatter.5.cloned.1.call-start = ((), (), s32[]{:S(2)}) async-start(), calls=%async_computation.6 | async-start | bytes 1572864 | tf_op jit(solution)/shard_map/reduce_scatter | solution.py:34
  86.2 382.6 %all-gather.3.cloned.1.call-start = ((), (), s32[]{:S(2)}) async-start(), calls=%async_computation.4 | async-start | bytes 4718592 | tf_op jit(solution)/shard_map/all_gather | solution.py:68
  87.1 381.7 %copy-start.2 = (bf16[128,256]{1,0:T(8,128)(2,1)S(1)}, bf16[128,256]{1,0:T(8,128)(2,1)}, u32[]{:S(2)}) copy-start(bf16[128,256]{1,0:T(8,128)(2,1)} %param.7) | copy-start | bytes 196612
  185.1 281.9 %all-to-all-start.1 = ((bf16[16,64,256]{2,1,0:T(8,128)(2,1)}), bf16[16,64,256]{2,1,0:T(8,128)(2,1)S(1)}, u32[]{:S(2)}, u32[]{:S(2)}) async-start(bf16[16,64,256]{2,1,0:T(8,128)(2,1)} %bitcast.2), calls=%async_computation.3 | async-start | bytes 1048576 | tf_op jit(solution)/shard_map/all_to_all | solution.py:27
  271.7 425.3 %all-gather.5.cloned.1.call-start = ((), (), s32[]{:S(2)}) async-start(), calls=%async_computation.7 | async-start | bytes 1671168 | tf_op jit(solution)/shard_map/all_gather | solution.py:41
Sparse Core Ops, SparseCore 0:
  13.9 72.2 reduce-scatter.2
  89.5 93.4 reduce-scatter.4
Sparse Core Ops, SparseCore 1:
  91.6 299.3 all-gather.2
  468.8 228.2 all-gather.4
where the time goes:
time: 708 us
  waiting for transfers between devices  556 us (79%)
  starting transfers between devices  86.8 us (12%)
  blocking collectives  29 us (4%)
  between operations  15.6 us (2%)
  other arithmetic  9.27 us (1%)
  matrix products  7.8 us (1%)
    all_to_all x1, waiting for transfers between devices, sent_and_summed(): lax.all_to_all(pieces, axis, split_axis=0, concat_axis=0, tiled=True)  195 us
    all_gather x1, waiting for transfers between devices, sent_together(): out = lax.all_gather(both, axis, axis=dim, tiled=True)  193 us
    reduce_scatter x2, waiting for transfers between devices, sum_by_axis(): total = lax.psum_scatter(total, axis, scatter_dimension=0, tiled=True)  168 us
    all_to_all x1, starting transfers between devices, sent_and_summed(): lax.all_to_all(pieces, axis, split_axis=0, concat_axis=0, tiled=True)  86.6 us
    all_to_all x1, blocking collectives, sent_and_summed(): lax.all_to_all(pieces, axis, split_axis=0, concat_axis=0, tiled=True)  29 us
  transfers between devices with their start and end apart: 5, of which 4 were waited for; matrix products, arithmetic and copies ran while one was open for 2% of the time, Pallas kernels for 0%

commit v1 on v0

v1 whole, which is shorter than its diff:
```python
import jax
import jax.numpy as jnp
from jax import lax
from jax.sharding import Mesh
from jax.sharding import PartitionSpec as P

AXES = ("za", "zb", "y", "h", "x", "c")
ROWS = ("y", "h")
COLS = ("x", "c")
TOKENS = ("za", "zb", "y", "h")
NEAR = ("zb", "y")

beta_one = 0.9
beta_two = 0.95
learn_rate = 0.001
weight_decay = 0.1
adam_step = 10
epsilon = 1e-08

F32 = jnp.float32
BF16 = jnp.bfloat16


def adamw(grad, master, moment_one, moment_two):
    first = beta_one * moment_one + (1.0 - beta_one) * grad
    second = beta_two * moment_two + (1.0 - beta_two) * grad * grad
    first_hat = first / (1.0 - beta_one**adam_step)
    second_hat = second / (1.0 - beta_two**adam_step)
    updated = master - learn_rate * (
        first_hat / (jnp.sqrt(second_hat) + epsilon) + weight_decay * master
    )
    return (updated, first, second)


def swapped(array, axis, bit=1):
    size = lax.axis_size(axis)
    return lax.ppermute(array, axis, [(k, k ^ bit) for k in range(size)])


def exchanged(pieces, axes):
    return lax.all_to_all(pieces, axes, split_axis=0, concat_axis=0, tiled=True)


def gathered(array, axes):
    count = lax.axis_size(axes)
    return exchanged(jnp.broadcast_to(array[None], (count, *array.shape)), axes)


def own_first(pair, index):
    flip = index == 0
    return jnp.where(flip, pair[0], pair[1]), jnp.where(flip, pair[1], pair[0])


def masked_grads(value_grads, lengths):
    tok_rows = value_grads.shape[0]
    seq_count = lengths.shape[0]
    seq_len = tok_rows // seq_count
    index = jnp.arange(tok_rows, dtype=jnp.int32)
    pick = (index // seq_len)[:, None] == jnp.arange(seq_count, dtype=jnp.int32)[None, :]
    limit = jnp.sum(jnp.where(pick, lengths[None, :], 0), axis=1)
    return jnp.where((index % seq_len < limit)[:, None], value_grads, jnp.zeros_like(value_grads))


def local(activations, value_grads, lengths, master, moment_one, moment_two):
    tok, width = activations.shape
    rows, cols = master.shape
    nzb, ny, nx = lax.axis_size("zb"), lax.axis_size("y"), lax.axis_size("x")
    near = nzb * ny
    shares = lax.axis_size(COLS)
    share = tok // shares
    part = rows // nzb
    h, c, zb = lax.axis_index("h"), lax.axis_index("c"), lax.axis_index("zb")

    weight = master.astype(BF16)
    other_weight = swapped(weight, "h")

    mine = lax.dynamic_slice_in_dim(activations, lax.axis_index(COLS) * share, share, 0)
    mine = mine.reshape(share, ny, 2, nzb, part).transpose(3, 1, 0, 2, 4)
    mine = mine.reshape(near, share, 2 * part)
    act_share = exchanged(mine, NEAR)
    act_own = gathered(act_share, "x")
    act_other = swapped(act_own, "c")

    masked = masked_grads(value_grads, lengths)
    grads = gathered(masked, NEAR)

    by_core = grads.reshape(near, nx, 2, share, cols).transpose(2, 1, 0, 3, 4)
    grads_own, grads_other = own_first((by_core[0], by_core[1]), c)

    def outer(a, g):
        return lax.dot_general(
            a.reshape(-1, 2 * part),
            g.reshape(-1, cols),
            (((0,), (0,)), ((), ())),
            preferred_element_type=F32,
        )

    partial = outer(act_own, grads_own) + outer(act_other, grads_other)
    partial = partial.astype(BF16).reshape(2, part, cols)
    keep, send = own_first((partial[0], partial[1]), h)
    total = (keep.astype(F32) + swapped(send, "h").astype(F32)).astype(BF16)
    for bit in (1, 2):
        if bit < lax.axis_size("za"):
            total = (total.astype(F32) + swapped(total, "za", bit).astype(F32)).astype(BF16)
    grad = gathered(total, "zb").reshape(rows, cols).astype(F32)
    count = float(tok * lax.axis_size(TOKENS))
    new_master, new_one, new_two = adamw(grad / count, master, moment_one, moment_two)

    tokens = lax.dynamic_slice_in_dim(grads, zb * ny, ny, 0).reshape(ny * tok, cols)
    weight_keep, weight_send = own_first((weight, other_weight), h ^ c)

    def product(w):
        return lax.dot_general(
            tokens, w, (((1,), (1,)), ((), ())), preferred_element_type=F32
        )

    sent = swapped(product(weight_send).astype(BF16), "c")
    summed = (product(weight_keep) + sent.astype(F32)).astype(BF16)
    arrived = exchanged(summed.reshape(nx, tok, rows), "x")
    block = arrived.astype(F32).sum(axis=0).astype(BF16)
    turn = [(y * nx + x, x * nx + y) for y in range(ny) for x in range(nx)]
    input_grads = lax.ppermute(block, ("y", "x"), turn)
    return (input_grads, new_master, new_one, new_two)


def solution(mesh):
    replica, fsdp, tensor = (mesh.shape[a] for a in ("replica", "fsdp", "tensor"))
    near = 4 if replica == 16 else 2
    split = Mesh(
        mesh.devices.reshape(replica // near, near, fsdp // 2, 2, tensor // 2, 2), AXES
    )
    in_specs = (
        P(TOKENS, None),
        P(TOKENS, COLS),
        P(TOKENS),
        P(ROWS, COLS),
        P(ROWS, COLS),
        P(ROWS, COLS),
    )
    out_specs = (P(TOKENS, COLS), P(ROWS, COLS), P(ROWS, COLS), P(ROWS, COLS))
    return jax.shard_map(local, mesh=split, in_specs=in_specs, out_specs=out_specs, check_vma=False)
```

time: 708 us -> 336 us (0.47)
  the two profiles are of different devices: /device:TPU:4 before, /device:TPU:71 now
where the time goes in v1:
time: 336 us; the launch traced here: 335 us
  waiting for transfers between devices  173 us (51%)
  starting transfers between devices  90.4 us (27%)
  blocking collectives  56 us (17%)
  local copies, waits for them, and re-layouts  6.55 us (2%)
  matrix products  5.22 us (2%)
    ppermute x6, waiting for transfers between devices, swapped(): return lax.ppermute(array, axis, [(k, k ^ bit) for k in range(size)])  139 us
    ppermute x6, starting transfers between devices, swapped(): return lax.ppermute(array, axis, [(k, k ^ bit) for k in range(size)])  75.2 us
    all_to_all x3, blocking collectives, exchanged(): return lax.all_to_all(pieces, axes, split_axis=0, concat_axis=0, tiled=True)  56 us
    all_to_all x2, waiting for transfers between devices, exchanged(): return lax.all_to_all(pieces, axes, split_axis=0, concat_axis=0, tiled=True)  20.9 us
    ppermute x1, waiting for transfers between devices, local(): input_grads = lax.ppermute(block, ('y', 'x'), turn)  12.6 us
    all_to_all x2, starting transfers between devices, exchanged(): return lax.all_to_all(pieces, axes, split_axis=0, concat_axis=0, tiled=True)  8.82 us
  transfers between devices with their start and end apart: 9, of which 8 were waited for; matrix products, arithmetic and copies ran while one was open for 0% of the time, Pallas kernels for 0%

profile of v1, /device:TPU:71, one launch (start us, length us, event | category | flops | bytes accessed | tf_op | source)
XLA Modules:
  0.0 335.1 jit_solution(3459667899260396145)
XLA Ops:
  0.6 0.0 copy-start
  0.7 1.6 copy-done
  2.2 0.2 reshape.76
  2.4 0.2 copy.15
  2.7 0.2 reshape.77
  2.9 0.0 copy-start.7
  2.9 0.0 copy-start.6
  2.9 16.7 %all_to_all.25 = bf16[16,16,512]{2,1,0:T(8,128)(2,1)S(1)} all-to-all(bf16[16,16,512]{2,1,0:T(8,128)(2,1)S(1)} %reshape.77), channel_id=1, replica_groups=mesh['za'=4,'zb'=4,'y'=4,'h'=2,'x'=4,'c'=2] {'zb','y'}, dimensions={0} | all-to-all | bytes 524288 | tf_op jit(solution)/shard_map/all_to_all | solution.py:41
  19.6 1.1 broadcast_in_dim.50
  20.7 4.2 %all-to-all-start.3 = ((bf16[4,16,16,512]{3,2,1,0:T(8,128)(2,1)}), bf16[4,16,16,512]{3,2,1,0:T(8,128)(2,1)S(1)}, u32[]{:S(2)}, u32[]{:S(2)}) async-start(bf16[4,16,16,512]{3,2,1,0:T(8,128)(2,1)} %broadcast_in_dim.50), calls=%async_computation.3 | async-start | bytes 2097152 | tf_op jit(solution)/shard_map/all_to_all | solution.py:41
  24.9 0.0 copy-done.7
  24.9 0.1 fusion.9
  25.0 0.0 copy-done.6
  25.0 0.1 broadcast_select_fusion.1
  25.1 7.8 %all-to-all-done.3 = bf16[4,16,16,512]{3,2,1,0:T(8,128)(2,1)S(1)} async-done(((bf16[4,16,16,512]{3,2,1,0:T(8,128)(2,1)}), bf16[4,16,16,512]{3,2,1,0:T(8,128)(2,1)S(1)}, u32[]{:S(2)}, u32[]{:S(2)}) %all-to-all-start.3) | async-done | bytes 1048608 | tf_op jit(solution)/shard_map/all_to_all | solution.py:41
  32.9 0.0 copy-start.4
  32.9 1.2 broadcast_in_dim.49
  34.1 0.1 copy-done.4
  34.2 4.6 %all-to-all-start = ((bf16[16,128,256]{2,1,0:T(8,128)(2,1)}), bf16[16,128,256]{2,1,0:T(8,128)(2,1)S(1)}, u32[]{:S(2)}, u32[]{:S(2)}) async-start(bf16[16,128,256]{2,1,0:T(8,128)(2,1)} %broadcast_in_dim.49), calls=%async_computation | async-start | bytes 2097152 | tf_op jit(solution)/shard_map/all_to_all | solution.py:41
  38.8 10.3 %collective-permute-start.3 = (bf16[4,16,16,512]{3,2,1,0:T(8,128)(2,1)}, bf16[4,16,16,512]{3,2,1,0:T(8,128)(2,1)}, u32[]{:S(2)}, u32[]{:S(2)}) collective-permute-start(bf16[4,16,16,512]{3,2,1,0:T(8,128)(2,1)} %copy-done.4), channel_id=1, source_target_pairs={{0,1},{1,0},{2,3},{3,2},{4,5},{5,4},{6,7},{7,6},{8,9},{9,8},{10,11... | collective-permute-start | bytes 3145736 | tf_op jit(solution)/shard_map/ppermute | solution.py:37
  49.2 13.1 %all-to-all-done = bf16[16,128,256]{2,1,0:T(8,128)(2,1)S(1)} async-done(((bf16[16,128,256]{2,1,0:T(8,128)(2,1)}), bf16[16,128,256]{2,1,0:T(8,128)(2,1)S(1)}, u32[]{:S(2)}, u32[]{:S(2)}) %all-to-all-start) | async-done | bytes 1048608 | tf_op jit(solution)/shard_map/all_to_all | solution.py:41
  62.2 0.0 copy-start.5
  62.2 0.1 select_bitcast_fusion
  62.3 1.1 copy-done.5
  63.5 0.5 convolution_bitcast_fusion.1
  63.9 0.0 collective-permute-done.3
  63.9 1.7 fusion.1
  65.7 31.9 %collective-permute-start.4 = (bf16[256,256]{1,0:T(8,128)(2,1)S(1)}, bf16[256,256]{1,0:T(8,128)(2,1)S(1)}, u32[]{:S(2)}, u32[]{:S(2)}) collective-permute-start(bf16[256,256]{1,0:T(8,128)(2,1)S(1)} %broadcast_select_fusion), channel_id=1, source_target_pairs={{0,8},{8,0},{1,9},{9,1},{2,10},{10,2},{3,11},{11,3},{4,12},{12,4},... | collective-permute-start | bytes 393224 | tf_op jit(solution)/shard_map/ppermute | solution.py:37
  97.6 5.5 %collective-permute-done.4 = bf16[256,256]{1,0:T(8,128)(2,1)S(1)} collective-permute-done((bf16[256,256]{1,0:T(8,128)(2,1)S(1)}, bf16[256,256]{1,0:T(8,128)(2,1)S(1)}, u32[]{:S(2)}, u32[]{:S(2)}) %collective-permute-start.4) | collective-permute-done | bytes 131104 | tf_op jit(solution)/shard_map/ppermute | solution.py:37
  103.1 0.1 add_convert_fusion.3
  103.1 8.8 %collective-permute-start.5 = (bf16[256,256]{1,0:T(8,128)(2,1)S(1)}, bf16[256,256]{1,0:T(8,128)(2,1)S(1)}, u32[]{:S(2)}, u32[]{:S(2)}) collective-permute-start(bf16[256,256]{1,0:T(8,128)(2,1)S(1)} %add_convert_fusion.3), channel_id=1, source_target_pairs={{0,256},{256,0},{512,768},{768,512},{1,257},{257,1},{513,769},{769... | collective-permute-start | bytes 393224 | tf_op jit(solution)/shard_map/ppermute | solution.py:37
  111.9 12.7 %collective-permute-done.5 = bf16[256,256]{1,0:T(8,128)(2,1)S(1)} collective-permute-done((bf16[256,256]{1,0:T(8,128)(2,1)S(1)}, bf16[256,256]{1,0:T(8,128)(2,1)S(1)}, u32[]{:S(2)}, u32[]{:S(2)}) %collective-permute-start.5) | collective-permute-done | bytes 131104 | tf_op jit(solution)/shard_map/ppermute | solution.py:37
  124.7 13.0 %collective-permute-start.6 = (bf16[256,256]{1,0:T(8,128)(2,1)S(1)}, bf16[256,256]{1,0:T(8,128)(2,1)S(1)}, u32[]{:S(2)}, u32[]{:S(2)}) collective-permute-start(bf16[256,256]{1,0:T(8,128)(2,1)S(1)} %add_convert_fusion.2), channel_id=1, source_target_pairs={{0,512},{256,768},{512,0},{768,256},{1,513},{257,769},{513,1},{769... | collective-permute-start | bytes 393224 | tf_op jit(solution)/shard_map/ppermute | solution.py:37
  137.7 17.7 %collective-permute-done.6 = bf16[256,256]{1,0:T(8,128)(2,1)S(1)} collective-permute-done((bf16[256,256]{1,0:T(8,128)(2,1)S(1)}, bf16[256,256]{1,0:T(8,128)(2,1)S(1)}, u32[]{:S(2)}, u32[]{:S(2)}) %collective-permute-start.6) | collective-permute-done | bytes 131104 | tf_op jit(solution)/shard_map/ppermute | solution.py:37
  155.5 0.0 copy-start.1
  155.5 0.0 copy-start.2
  155.5 0.0 copy-start.3
  155.5 22.3 %all_to_all.26 = bf16[4,256,256]{2,1,0:T(8,128)(2,1)S(1)} all-to-all(bf16[4,256,256]{2,1,0:T(8,128)(2,1)S(1)} %broadcast_in_dim.51), channel_id=1, replica_groups=mesh['za'=4,'zb'=4,'y'=4,'h'=2,'x'=4,'c'=2] {'zb'}, dimensions={0} | all-to-all | bytes 1048576 | tf_op jit(solution)/shard_map/all_to_all | solution.py:41
  177.8 0.2 fusion.2
  178.0 0.0 copy-done.1
  178.1 0.0 copy-done.2
  178.1 0.0 copy-done.3
  178.1 2.3 multiply_subtract_fusion
  180.3 8.7 %collective-permute-start = (bf16[1024,256]{1,0:T(8,128)(2,1)}, bf16[1024,256]{1,0:T(8,128)(2,1)}, u32[]{:S(2)}, u32[]{:S(2)}) collective-permute-start(bf16[1024,256]{1,0:T(8,128)(2,1)} %get-tuple-element.7), channel_id=1, source_target_pairs={{0,8},{8,0},{1,9},{9,1},{2,10},{10,2},{3,11},{11,3},{4,12},{12,4},... | collective-permute-start | bytes 1572872 | tf_op jit(solution)/shard_map/ppermute | solution.py:37
  189.1 101.3 %collective-permute-done = bf16[1024,256]{1,0:T(8,128)(2,1)} collective-permute-done((bf16[1024,256]{1,0:T(8,128)(2,1)}, bf16[1024,256]{1,0:T(8,128)(2,1)}, u32[]{:S(2)}, u32[]{:S(2)}) %collective-permute-start) | collective-permute-done | bytes 524320 | tf_op jit(solution)/shard_map/ppermute | solution.py:37
  290.4 1.5 convolution_convert_fusion
  291.9 2.4 collective-permute-start.1
  294.3 2.3 collective-permute-done.1
  296.6 1.5 add_convert_fusion
  298.1 17.1 %all_to_all.27 = bf16[4,128,1024]{2,1,0:T(8,128)(2,1)S(1)} all-to-all(bf16[4,128,1024]{2,1,0:T(8,128)(2,1)S(1)} %bitcast.33), channel_id=1, replica_groups=mesh['za'=4,'zb'=4,'y'=4,'h'=2,'x'=4,'c'=2] {'x'}, dimensions={0} | all-to-all | bytes 2097152 | tf_op jit(solution)/shard_map/all_to_all | solution.py:41
  315.2 0.2 reduce_sum.22
  315.4 6.4 %collective-permute-start.2 = (bf16[128,1024]{1,0:T(8,128)(2,1)S(1)}, bf16[128,1024]{1,0:T(8,128)(2,1)S(1)}, u32[]{:S(2)}, u32[]{:S(2)}) collective-permute-start(bf16[128,1024]{1,0:T(8,128)(2,1)S(1)} %reduce_sum.22), channel_id=1, source_target_pairs={{0,0},{2,16},{4,32},{6,48},{16,2},{18,18},{20,34},{22,50},{32,4},{... | collective-permute-start | bytes 786440 | tf_op jit(solution)/shard_map/ppermute | solution.py:122
  321.8 12.6 %collective-permute-done.2 = bf16[128,1024]{1,0:T(8,128)(2,1)S(1)} collective-permute-done((bf16[128,1024]{1,0:T(8,128)(2,1)S(1)}, bf16[128,1024]{1,0:T(8,128)(2,1)S(1)}, u32[]{:S(2)}, u32[]{:S(2)}) %collective-permute-start.2) | collective-permute-done | bytes 262176 | tf_op jit(solution)/shard_map/ppermute | solution.py:122
  334.4 0.7 copy.25
  (8 shorter events, 0.2 us)
Async XLA Ops:
  0.6 1.6 copy-start
  2.9 22.0 %copy-start.7 = (s32[2]{0:T(128)S(1)}, s32[2]{0:T(128)}, u32[]{:S(2)}) copy-start(s32[2]{0:T(128)} %param.8) | copy-start | bytes 28
  2.9 22.1 %copy-start.6 = (bf16[128,256]{1,0:T(8,128)(2,1)S(1)}, bf16[128,256]{1,0:T(8,128)(2,1)}, u32[]{:S(2)}) copy-start(bf16[128,256]{1,0:T(8,128)(2,1)} %param.7) | copy-start | bytes 196612
  20.7 12.2 %all-to-all-start.3 = ((bf16[4,16,16,512]{3,2,1,0:T(8,128)(2,1)}), bf16[4,16,16,512]{3,2,1,0:T(8,128)(2,1)S(1)}, u32[]{:S(2)}, u32[]{:S(2)}) async-start(bf16[4,16,16,512]{3,2,1,0:T(8,128)(2,1)} %broadcast_in_dim.50), calls=%async_computation.3 | async-start | bytes 2097152 | tf_op jit(solution)/shard_map/all_to_all | solution.py:41
  32.9 1.3 copy-start.4
  34.2 28.0 %all-to-all-start = ((bf16[16,128,256]{2,1,0:T(8,128)(2,1)}), bf16[16,128,256]{2,1,0:T(8,128)(2,1)S(1)}, u32[]{:S(2)}, u32[]{:S(2)}) async-start(bf16[16,128,256]{2,1,0:T(8,128)(2,1)} %broadcast_in_dim.49), calls=%async_computation | async-start | bytes 2097152 | tf_op jit(solution)/shard_map/all_to_all | solution.py:41
  38.8 25.1 %collective-permute-start.3 = (bf16[4,16,16,512]{3,2,1,0:T(8,128)(2,1)}, bf16[4,16,16,512]{3,2,1,0:T(8,128)(2,1)}, u32[]{:S(2)}, u32[]{:S(2)}) collective-permute-start(bf16[4,16,16,512]{3,2,1,0:T(8,128)(2,1)} %copy-done.4), channel_id=1, source_target_pairs={{0,1},{1,0},{2,3},{3,2},{4,5},{5,4},{6,7},{7,6},{8,9},{9,8},{10,11... | collective-permute-start | bytes 3145736 | tf_op jit(solution)/shard_map/ppermute | solution.py:37
  62.2 1.2 copy-start.5
  65.7 37.4 %collective-permute-start.4 = (bf16[256,256]{1,0:T(8,128)(2,1)S(1)}, bf16[256,256]{1,0:T(8,128)(2,1)S(1)}, u32[]{:S(2)}, u32[]{:S(2)}) collective-permute-start(bf16[256,256]{1,0:T(8,128)(2,1)S(1)} %broadcast_select_fusion), channel_id=1, source_target_pairs={{0,8},{8,0},{1,9},{9,1},{2,10},{10,2},{3,11},{11,3},{4,12},{12,4},... | collective-permute-start | bytes 393224 | tf_op jit(solution)/shard_map/ppermute | solution.py:37
  103.1 21.5 %collective-permute-start.5 = (bf16[256,256]{1,0:T(8,128)(2,1)S(1)}, bf16[256,256]{1,0:T(8,128)(2,1)S(1)}, u32[]{:S(2)}, u32[]{:S(2)}) collective-permute-start(bf16[256,256]{1,0:T(8,128)(2,1)S(1)} %add_convert_fusion.3), channel_id=1, source_target_pairs={{0,256},{256,0},{512,768},{768,512},{1,257},{257,1},{513,769},{769... | collective-permute-start | bytes 393224 | tf_op jit(solution)/shard_map/ppermute | solution.py:37
  124.7 30.8 %collective-permute-start.6 = (bf16[256,256]{1,0:T(8,128)(2,1)S(1)}, bf16[256,256]{1,0:T(8,128)(2,1)S(1)}, u32[]{:S(2)}, u32[]{:S(2)}) collective-permute-start(bf16[256,256]{1,0:T(8,128)(2,1)S(1)} %add_convert_fusion.2), channel_id=1, source_target_pairs={{0,512},{256,768},{512,0},{768,256},{1,513},{257,769},{513,1},{769... | collective-permute-start | bytes 393224 | tf_op jit(solution)/shard_map/ppermute | solution.py:37
  155.5 22.6 %copy-start.1 = (f32[1024,256]{1,0:T(8,128)S(1)}, f32[1024,256]{1,0:T(8,128)}, u32[]{:S(2)}) copy-start(f32[1024,256]{1,0:T(8,128)} %param.9) | copy-start | bytes 3145732
  155.5 22.6 %copy-start.2 = (f32[1024,256]{1,0:T(8,128)S(1)}, f32[1024,256]{1,0:T(8,128)}, u32[]{:S(2)}) copy-start(f32[1024,256]{1,0:T(8,128)} %param.10) | copy-start | bytes 3145732
  155.5 22.6 %copy-start.3 = (f32[1024,256]{1,0:T(8,128)S(1)}, f32[1024,256]{1,0:T(8,128)}, u32[]{:S(2)}) copy-start(f32[1024,256]{1,0:T(8,128)} %param.11) | copy-start | bytes 3145732
  180.3 110.0 %collective-permute-start = (bf16[1024,256]{1,0:T(8,128)(2,1)}, bf16[1024,256]{1,0:T(8,128)(2,1)}, u32[]{:S(2)}, u32[]{:S(2)}) collective-permute-start(bf16[1024,256]{1,0:T(8,128)(2,1)} %get-tuple-element.7), channel_id=1, source_target_pairs={{0,8},{8,0},{1,9},{9,1},{2,10},{10,2},{3,11},{11,3},{4,12},{12,4},... | collective-permute-start | bytes 1572872 | tf_op jit(solution)/shard_map/ppermute | solution.py:37
  291.9 4.7 %collective-permute-start.1 = (bf16[512,1024]{1,0:T(8,128)(2,1)S(1)}, bf16[512,1024]{1,0:T(8,128)(2,1)S(1)}, u32[]{:S(2)}, u32[]{:S(2)}) collective-permute-start(bf16[512,1024]{1,0:T(8,128)(2,1)S(1)} %convolution_convert_fusion), channel_id=1, source_target_pairs={{0,1},{1,0},{2,3},{3,2},{4,5},{5,4},{6,7},{7,6},{8,9},{9,8},{10,11... | collective-permute-start | bytes 3145736 | tf_op jit(solution)/shard_map/ppermute | solution.py:37
  315.4 19.0 %collective-permute-start.2 = (bf16[128,1024]{1,0:T(8,128)(2,1)S(1)}, bf16[128,1024]{1,0:T(8,128)(2,1)S(1)}, u32[]{:S(2)}, u32[]{:S(2)}) collective-permute-start(bf16[128,1024]{1,0:T(8,128)(2,1)S(1)} %reduce_sum.22), channel_id=1, source_target_pairs={{0,0},{2,16},{4,32},{6,48},{16,2},{18,18},{20,34},{22,50},{32,4},{... | collective-permute-start | bytes 786440 | tf_op jit(solution)/shard_map/ppermute | solution.py:122

commit v2 on v1

--- a/solution.py
+++ b/solution.py
@@ -3,6 +3,7 @@
 from jax import lax
 from jax.sharding import Mesh
 from jax.sharding import PartitionSpec as P
+
 
 AXES = ("za", "zb", "y", "h", "x", "c")
 ROWS = ("y", "h")
@@ -46,6 +47,13 @@
     return exchanged(jnp.broadcast_to(array[None], (count, *array.shape)), axes)
 
 
+def across(array):
+    count = lax.axis_size("za")
+    far = count // 2
+    pairs = [(2 * za + h, 2 * (za ^ far) + 1 - h) for za in range(count) for h in range(2)]
+    return lax.ppermute(array, ("za", "h"), pairs)
+
+
 def own_first(pair, index):
     flip = index == 0
     return jnp.where(flip, pair[0], pair[1]), jnp.where(flip, pair[1], pair[0])
@@ -61,8 +69,8 @@
     return jnp.where((index % seq_len < limit)[:, None], value_grads, jnp.zeros_like(value_grads))
 
 
-def local(activations, value_grads, lengths, master, moment_one, moment_two):
-    tok, width = activations.shape
+def step(activations, value_grads, lengths, master, moment_one, moment_two):
+    tok, _ = activations.shape
     rows, cols = master.shape
     nzb, ny, nx = lax.axis_size("zb"), lax.axis_size("y"), lax.axis_size("x")
     near = nzb * ny
@@ -71,18 +79,42 @@
     part = rows // nzb
     h, c, zb = lax.axis_index("h"), lax.axis_index("c"), lax.axis_index("zb")
 
-    weight = master.astype(BF16)
-    other_weight = swapped(weight, "h")
+    weight = lax.dynamic_slice_in_dim(master, zb * part, part, 0).astype(BF16)
+    other_weight = across(weight)
 
     mine = lax.dynamic_slice_in_dim(activations, lax.axis_index(COLS) * share, share, 0)
     mine = mine.reshape(share, ny, 2, nzb, part).transpose(3, 1, 0, 2, 4)
     mine = mine.reshape(near, share, 2 * part)
     act_share = exchanged(mine, NEAR)
-    act_own = gathered(act_share, "x")
+
+    masked = masked_grads(value_grads, lengths)
+    copies = jnp.broadcast_to(masked[None], (near, tok, cols))
+    copies, act_share = lax.optimization_barrier((copies, act_share))
+    grads = exchanged(copies, NEAR)
+
+    x = lax.axis_index("x")
+    act_own = jnp.zeros((nx, *act_share.shape), BF16)
+    act_own = lax.dynamic_update_index_in_dim(act_own, act_share, x, 0)
+    for k in range(1, nx):
+        piece = swapped(act_share, "x", k)
+        act_own = lax.dynamic_update_index_in_dim(act_own, piece, x ^ k, 0)
     act_other = swapped(act_own, "c")
 
-    masked = masked_grads(value_grads, lengths)
-    grads = gathered(masked, NEAR)
+    tokens = grads.reshape(near * tok, cols)
+    weight_keep, weight_send = own_first((weight, other_weight), h ^ c)
+
+    def product(w):
+        return lax.dot_general(
+            tokens, w, (((1,), (1,)), ((), ())), preferred_element_type=F32
+        )
+
+    sent = swapped(product(weight_send).astype(BF16), "c")
+    summed = (product(weight_keep) + sent.astype(F32)).astype(BF16)
+    arrived = exchanged(summed.reshape(nzb * nx, tok, part), ("zb", "x"))
+    block = arrived.astype(F32).reshape(nzb, nx, tok, part).sum(axis=1)
+    block = block.transpose(1, 0, 2).reshape(tok, rows).astype(BF16)
+    turn = [(y * nx + x, x * nx + y) for y in range(ny) for x in range(nx)]
+    input_grads = lax.ppermute(block, ("y", "x"), turn)
 
     by_core = grads.reshape(near, nx, 2, share, cols).transpose(2, 1, 0, 3, 4)
     grads_own, grads_other = own_first((by_core[0], by_core[1]), c)
@@ -98,28 +130,15 @@
     partial = outer(act_own, grads_own) + outer(act_other, grads_other)
     partial = partial.astype(BF16).reshape(2, part, cols)
     keep, send = own_first((partial[0], partial[1]), h)
-    total = (keep.astype(F32) + swapped(send, "h").astype(F32)).astype(BF16)
+    received = across(send)
+    total = (keep.astype(F32) + received.astype(F32)).astype(BF16)
     for bit in (1, 2):
         if bit < lax.axis_size("za"):
-            total = (total.astype(F32) + swapped(total, "za", bit).astype(F32)).astype(BF16)
+            received = swapped(total, "za", bit)
+            total = (total.astype(F32) + received.astype(F32)).astype(BF16)
     grad = gathered(total, "zb").reshape(rows, cols).astype(F32)
     count = float(tok * lax.axis_size(TOKENS))
     new_master, new_one, new_two = adamw(grad / count, master, moment_one, moment_two)
-
-    tokens = lax.dynamic_slice_in_dim(grads, zb * ny, ny, 0).reshape(ny * tok, cols)
-    weight_keep, weight_send = own_first((weight, other_weight), h ^ c)
-
-    def product(w):
-        return lax.dot_general(
-            tokens, w, (((1,), (1,)), ((), ())), preferred_element_type=F32
-        )
-
-    sent = swapped(product(weight_send).astype(BF16), "c")
-    summed = (product(weight_keep) + sent.astype(F32)).astype(BF16)
-    arrived = exchanged(summed.reshape(nx, tok, rows), "x")
-    block = arrived.astype(F32).sum(axis=0).astype(BF16)
-    turn = [(y * nx + x, x * nx + y) for y in range(ny) for x in range(nx)]
-    input_grads = lax.ppermute(block, ("y", "x"), turn)
     return (input_grads, new_master, new_one, new_two)
 
 
@@ -138,4 +157,6 @@
         P(ROWS, COLS),
     )
     out_specs = (P(TOKENS, COLS), P(ROWS, COLS), P(ROWS, COLS), P(ROWS, COLS))
-    return jax.shard_map(local, mesh=split, in_specs=in_specs, out_specs=out_specs, check_vma=False)
+    return jax.shard_map(
+        step, mesh=split, in_specs=in_specs, out_specs=out_specs, check_vma=False
+    )

time: 336 us -> 239 us (0.71)
  the two profiles are of different devices: /device:TPU:71 before, /device:TPU:216 now
where the time goes in v2:
time: 239 us; the launch traced here: 238 us
  waiting for transfers between devices  125 us (52%)
  starting transfers between devices  86.7 us (36%)
  local copies, waits for them, and re-layouts  11.7 us (5%)
  other arithmetic  7.68 us (3%)
  matrix products  5.31 us (2%)
    ppermute x2, waiting for transfers between devices, across(): return lax.ppermute(array, ('za', 'h'), pairs)  42 us
    ppermute x7, waiting for transfers between devices, swapped(): return lax.ppermute(array, axis, [(k, k ^ bit) for k in range(size)])  42 us
    all_to_all x4, starting transfers between devices, exchanged(): return lax.all_to_all(pieces, axes, split_axis=0, concat_axis=0, tiled=True)  31.9 us
    all_to_all x4, waiting for transfers between devices, exchanged(): return lax.all_to_all(pieces, axes, split_axis=0, concat_axis=0, tiled=True)  29.7 us
    ppermute x2, starting transfers between devices, across(): return lax.ppermute(array, ('za', 'h'), pairs)  28.2 us
    ppermute x7, starting transfers between devices, swapped(): return lax.ppermute(array, axis, [(k, k ^ bit) for k in range(size)])  24.8 us
    ppermute x1, waiting for transfers between devices, step(): input_grads = lax.ppermute(block, ('y', 'x'), turn)  11.6 us
  transfers between devices with their start and end apart: 14, of which 11 were waited for; matrix products, arithmetic and copies ran while one was open for 6% of the time, Pallas kernels for 0%

profile of v2, /device:TPU:216, one launch (start us, length us, event | category | flops | bytes accessed | tf_op | source)
XLA Modules:
  0.0 237.6 jit_solution(13504065002278890635)
XLA Ops:
  0.6 0.0 copy-start
  0.6 0.0 copy-start.2
  0.7 0.0 copy-start.1
  0.7 1.6 copy-done
  2.2 0.2 reshape.81
  2.4 0.2 copy.21
  2.7 0.9 reshape.82
  3.6 7.9 %all-to-all-start = ((bf16[16,16,512]{2,1,0:T(8,128)(2,1)}), bf16[16,16,512]{2,1,0:T(8,128)(2,1)S(1)}, u32[]{:S(2)}, u32[]{:S(2)}) async-start(bf16[16,16,512]{2,1,0:T(8,128)(2,1)} %reshape.82), calls=%async_computation | async-start | bytes 524288 | tf_op jit(solution)/shard_map/all_to_all | solution.py:42
  11.4 0.0 copy-done.2
  11.4 0.1 fusion.10
  11.5 0.0 copy-done.1
  11.5 0.1 broadcast_select_fusion.1
  11.6 6.2 %all-to-all-done = bf16[16,16,512]{2,1,0:T(8,128)(2,1)S(1)} async-done(((bf16[16,16,512]{2,1,0:T(8,128)(2,1)}), bf16[16,16,512]{2,1,0:T(8,128)(2,1)S(1)}, u32[]{:S(2)}, u32[]{:S(2)}) %all-to-all-start) | async-done | bytes 262176 | tf_op jit(solution)/shard_map/all_to_all | solution.py:42
  17.9 1.1 broadcast_in_dim.59
  18.9 8.0 %all-to-all-start.1 = ((bf16[16,128,256]{2,1,0:T(8,128)(2,1)}), bf16[16,128,256]{2,1,0:T(8,128)(2,1)S(1)}, u32[]{:S(2)}, u32[]{:S(2)}) async-start(bf16[16,128,256]{2,1,0:T(8,128)(2,1)} %broadcast_in_dim.59), calls=%async_computation.1 | async-start | bytes 2097152 | tf_op jit(solution)/shard_map/all_to_all | solution.py:42
  27.0 3.4 %collective-permute-start.3 = (bf16[16,16,512]{2,1,0:T(8,128)(2,1)S(1)}, bf16[16,16,512]{2,1,0:T(8,128)(2,1)}, u32[]{:S(2)}, u32[]{:S(2)}) collective-permute-start(bf16[16,16,512]{2,1,0:T(8,128)(2,1)S(1)} %all-to-all-done), channel_id=1, source_target_pairs={{0,2},{2,0},{4,6},{6,4},{1,3},{3,1},{5,7},{7,5},{8,10},{10,8},{12,... | collective-permute-start | bytes 786440 | tf_op jit(solution)/shard_map/ppermute | solution.py:38
  30.4 4.6 %collective-permute-start.4 = (bf16[16,16,512]{2,1,0:T(8,128)(2,1)S(1)}, bf16[16,16,512]{2,1,0:T(8,128)(2,1)S(1)}, u32[]{:S(2)}, u32[]{:S(2)}) collective-permute-start(bf16[16,16,512]{2,1,0:T(8,128)(2,1)S(1)} %all-to-all-done), channel_id=1, source_target_pairs={{0,4},{2,6},{4,0},{6,2},{1,5},{3,7},{5,1},{7,3},{8,12},{10,14},{12... | collective-permute-start | bytes 786440 | tf_op jit(solution)/shard_map/ppermute | solution.py:38
  35.0 2.4 %collective-permute-start.5 = (bf16[16,16,512]{2,1,0:T(8,128)(2,1)S(1)}, bf16[16,16,512]{2,1,0:T(8,128)(2,1)S(1)}, u32[]{:S(2)}, u32[]{:S(2)}) collective-permute-start(bf16[16,16,512]{2,1,0:T(8,128)(2,1)S(1)} %all-to-all-done), channel_id=1, source_target_pairs={{0,6},{2,4},{4,2},{6,0},{1,7},{3,5},{5,3},{7,1},{8,14},{10,12},{12... | collective-permute-start | bytes 786440 | tf_op jit(solution)/shard_map/ppermute | solution.py:38
  37.4 1.1 broadcast_in_dim.60
  38.5 0.7 bitcast_dynamic-update-slice_fusion.3
  39.2 0.0 collective-permute-done.3
  39.2 1.7 bitcast_dynamic-update-slice_fusion.2
  40.9 2.6 %collective-permute-done.4 = bf16[16,16,512]{2,1,0:T(8,128)(2,1)S(1)} collective-permute-done((bf16[16,16,512]{2,1,0:T(8,128)(2,1)S(1)}, bf16[16,16,512]{2,1,0:T(8,128)(2,1)S(1)}, u32[]{:S(2)}, u32[]{:S(2)}) %collective-permute-start.4) | collective-permute-done | bytes 262176 | tf_op jit(solution)/shard_map/ppermute | solution.py:38
  43.5 0.7 bitcast_dynamic-update-slice_fusion.1
  44.2 4.0 %collective-permute-done.5 = bf16[16,16,512]{2,1,0:T(8,128)(2,1)S(1)} collective-permute-done((bf16[16,16,512]{2,1,0:T(8,128)(2,1)S(1)}, bf16[16,16,512]{2,1,0:T(8,128)(2,1)S(1)}, u32[]{:S(2)}, u32[]{:S(2)}) %collective-permute-start.5) | collective-permute-done | bytes 262176 | tf_op jit(solution)/shard_map/ppermute | solution.py:38
  48.3 0.7 bitcast_dynamic-update-slice_fusion
  49.0 1.9 collective-permute-start.6
  50.9 0.0 all-to-all-done.1
  50.9 0.1 select_bitcast_fusion.1
  51.0 2.9 %collective-permute-done.6 = bf16[4,16,16,512]{3,2,1,0:T(8,128)(2,1)} collective-permute-done((bf16[4,16,16,512]{3,2,1,0:T(8,128)(2,1)}, bf16[4,16,16,512]{3,2,1,0:T(8,128)(2,1)}, u32[]{:S(2)}, u32[]{:S(2)}) %collective-permute-start.6) | collective-permute-done | bytes 1048608 | tf_op jit(solution)/shard_map/ppermute | solution.py:38
  53.9 1.7 convolution_bitcast_fusion
  55.6 1.7 fusion.2
  57.3 15.5 %collective-permute-start.7 = (bf16[256,256]{1,0:T(8,128)(2,1)S(1)}, bf16[256,256]{1,0:T(8,128)(2,1)S(1)}, u32[]{:S(2)}, u32[]{:S(2)}) collective-permute-start(bf16[256,256]{1,0:T(8,128)(2,1)S(1)} %broadcast_select_fusion), channel_id=1, source_target_pairs={{0,520},{8,512},{256,776},{264,768},{512,8},{520,0},{768,264},{776... | collective-permute-start | bytes 393224 | tf_op jit(solution)/shard_map/ppermute | solution.py:54
  72.8 20.7 %collective-permute-done.7 = bf16[256,256]{1,0:T(8,128)(2,1)S(1)} collective-permute-done((bf16[256,256]{1,0:T(8,128)(2,1)S(1)}, bf16[256,256]{1,0:T(8,128)(2,1)S(1)}, u32[]{:S(2)}, u32[]{:S(2)}) %collective-permute-start.7) | collective-permute-done | bytes 131104 | tf_op jit(solution)/shard_map/ppermute | solution.py:54
  93.6 0.1 add_convert_fusion.2
  93.6 1.9 collective-permute-start.8
  95.6 12.2 %collective-permute-done.8 = bf16[256,256]{1,0:T(8,128)(2,1)S(1)} collective-permute-done((bf16[256,256]{1,0:T(8,128)(2,1)S(1)}, bf16[256,256]{1,0:T(8,128)(2,1)S(1)}, u32[]{:S(2)}, u32[]{:S(2)}) %collective-permute-start.8) | collective-permute-done | bytes 131104 | tf_op jit(solution)/shard_map/ppermute | solution.py:38
  107.8 8.6 %collective-permute-start.9 = (bf16[256,256]{1,0:T(8,128)(2,1)S(1)}, bf16[256,256]{1,0:T(8,128)(2,1)S(1)}, u32[]{:S(2)}, u32[]{:S(2)}) collective-permute-start(bf16[256,256]{1,0:T(8,128)(2,1)S(1)} %add_convert_fusion.1), channel_id=1, source_target_pairs={{0,512},{256,768},{512,0},{768,256},{1,513},{257,769},{513,1},{769... | collective-permute-start | bytes 393224 | tf_op jit(solution)/shard_map/ppermute | solution.py:38
  116.4 17.6 %collective-permute-done.9 = bf16[256,256]{1,0:T(8,128)(2,1)S(1)} collective-permute-done((bf16[256,256]{1,0:T(8,128)(2,1)S(1)}, bf16[256,256]{1,0:T(8,128)(2,1)S(1)}, u32[]{:S(2)}, u32[]{:S(2)}) %collective-permute-start.9) | collective-permute-done | bytes 131104 | tf_op jit(solution)/shard_map/ppermute | solution.py:38
  134.1 0.8 broadcast_in_dim.65
  134.9 7.9 %all-to-all-start.3 = ((bf16[4,256,256]{2,1,0:T(8,128)(2,1)}), bf16[4,256,256]{2,1,0:T(8,128)(2,1)}, u32[]{:S(2)}, u32[]{:S(2)}) async-start(bf16[4,256,256]{2,1,0:T(8,128)(2,1)} %broadcast_in_dim.65), calls=%async_computation.3 | async-start | bytes 1048576 | tf_op jit(solution)/shard_map/all_to_all | solution.py:42
  142.8 1.0 dynamic-slice_convert_fusion
  143.7 12.7 %collective-permute-start = (bf16[256,256]{1,0:T(8,128)(2,1)S(1)}, bf16[256,256]{1,0:T(8,128)(2,1)S(1)}, u32[]{:S(2)}, u32[]{:S(2)}) collective-permute-start(bf16[256,256]{1,0:T(8,128)(2,1)S(1)} %dynamic-slice_convert_fusion), channel_id=1, source_target_pairs={{0,520},{8,512},{256,776},{264,768},{512,8},{520,0},{768,264},{776... | collective-permute-start | bytes 393224 | tf_op jit(solution)/shard_map/ppermute | solution.py:54
  156.4 21.3 %collective-permute-done = bf16[256,256]{1,0:T(8,128)(2,1)S(1)} collective-permute-done((bf16[256,256]{1,0:T(8,128)(2,1)S(1)}, bf16[256,256]{1,0:T(8,128)(2,1)S(1)}, u32[]{:S(2)}, u32[]{:S(2)}) %collective-permute-start) | collective-permute-done | bytes 131104 | tf_op jit(solution)/shard_map/ppermute | solution.py:54
  177.7 0.5 convolution_convert_fusion
  178.2 1.9 collective-permute-start.1
  180.1 2.6 %collective-permute-done.1 = bf16[2048,256]{1,0:T(8,128)(2,1)S(1)} collective-permute-done((bf16[2048,256]{1,0:T(8,128)(2,1)S(1)}, bf16[2048,256]{1,0:T(8,128)(2,1)S(1)}, u32[]{:S(2)}, u32[]{:S(2)}) %collective-permute-start.1) | collective-permute-done | bytes 1048608 | tf_op jit(solution)/shard_map/ppermute | solution.py:38
  182.7 1.4 fusion
  184.2 0.0 all-to-all-done.3
  184.2 8.1 %all-to-all-start.2 = ((bf16[16,128,256]{2,1,0:T(8,128)(2,1)}), bf16[16,128,256]{2,1,0:T(8,128)(2,1)S(1)}, u32[]{:S(2)}, u32[]{:S(2)}) async-start(bf16[16,128,256]{2,1,0:T(8,128)(2,1)} %bitcast.47), calls=%async_computation.2 | async-start | bytes 2097152 | tf_op jit(solution)/shard_map/all_to_all | solution.py:42
  192.3 2.6 %fusion.3 = (f32[4,256,256]{2,1,0:T(8,128)}, f32[4,256,256]{2,1,0:T(8,128)}) fusion(bf16[4,256,256]{2,1,0:T(8,128)(2,1)} %all-to-all-done.3), kind=kLoop, calls=%fused_computation.10 | loop fusion | flops 1310720 | bytes 2621440 | tf_op jit(solution)/shard_map/mul | solution.py:27
  194.9 23.5 %all-to-all-done.2 = bf16[16,128,256]{2,1,0:T(8,128)(2,1)S(1)} async-done(((bf16[16,128,256]{2,1,0:T(8,128)(2,1)}), bf16[16,128,256]{2,1,0:T(8,128)(2,1)S(1)}, u32[]{:S(2)}, u32[]{:S(2)}) %all-to-all-start.2) | async-done | bytes 1048608 | tf_op jit(solution)/shard_map/all_to_all | solution.py:42
  218.4 0.1 bitcast_reduce_fusion
  218.5 0.2 copy.22
  218.7 1.9 collective-permute-start.2
  220.6 4.6 %multiply_subtract_fusion = (f32[1024,256]{1,0:T(8,128)}, f32[1024,256]{1,0:T(8,128)}, f32[1024,256]{1,0:T(8,128)}) fusion(f32[1024,256]{1,0:T(8,128)} %param.9, f32[4,256,256]{2,1,0:T(8,128)} %get-tuple-element.22, f32[1024,256]{1,0:T(8,128)} %param.10, f32[4,256,256]{2,1,0:T(8,128)} %get-tuple-element.21, f32[1024,256]{1,0:T(8,128)} %param.11), kind=kLoop, calls=%fused_computation.14 | loop fusion | flops 3145728 | bytes 8388608 | tf_op jit(solution)/shard_map/sub | solution.py:30
  225.2 11.6 %collective-permute-done.2 = bf16[128,1024]{0,1:T(8,128)(2,1)S(1)} collective-permute-done((bf16[128,1024]{0,1:T(8,128)(2,1)S(1)}, bf16[128,1024]{0,1:T(8,128)(2,1)S(1)}, u32[]{:S(2)}, u32[]{:S(2)}) %collective-permute-start.2) | collective-permute-done | bytes 262176 | tf_op jit(solution)/shard_map/ppermute | solution.py:117
  236.8 0.8 copy.25
  (6 shorter events, 0.1 us)
Async XLA Ops:
  0.6 1.6 copy-start
  0.6 10.8 %copy-start.2 = (s32[2]{0:T(128)S(1)}, s32[2]{0:T(128)}, u32[]{:S(2)}) copy-start(s32[2]{0:T(128)} %param.8) | copy-start | bytes 28
  0.7 10.9 %copy-start.1 = (bf16[128,256]{1,0:T(8,128)(2,1)S(1)}, bf16[128,256]{1,0:T(8,128)(2,1)}, u32[]{:S(2)}) copy-start(bf16[128,256]{1,0:T(8,128)(2,1)} %param.7) | copy-start | bytes 196612
  3.6 14.3 %all-to-all-start = ((bf16[16,16,512]{2,1,0:T(8,128)(2,1)}), bf16[16,16,512]{2,1,0:T(8,128)(2,1)S(1)}, u32[]{:S(2)}, u32[]{:S(2)}) async-start(bf16[16,16,512]{2,1,0:T(8,128)(2,1)} %reshape.82), calls=%async_computation | async-start | bytes 524288 | tf_op jit(solution)/shard_map/all_to_all | solution.py:42
  18.9 32.0 %all-to-all-start.1 = ((bf16[16,128,256]{2,1,0:T(8,128)(2,1)}), bf16[16,128,256]{2,1,0:T(8,128)(2,1)S(1)}, u32[]{:S(2)}, u32[]{:S(2)}) async-start(bf16[16,128,256]{2,1,0:T(8,128)(2,1)} %broadcast_in_dim.59), calls=%async_computation.1 | async-start | bytes 2097152 | tf_op jit(solution)/shard_map/all_to_all | solution.py:42
  27.0 12.3 %collective-permute-start.3 = (bf16[16,16,512]{2,1,0:T(8,128)(2,1)S(1)}, bf16[16,16,512]{2,1,0:T(8,128)(2,1)}, u32[]{:S(2)}, u32[]{:S(2)}) collective-permute-start(bf16[16,16,512]{2,1,0:T(8,128)(2,1)S(1)} %all-to-all-done), channel_id=1, source_target_pairs={{0,2},{2,0},{4,6},{6,4},{1,3},{3,1},{5,7},{7,5},{8,10},{10,8},{12,... | collective-permute-start | bytes 786440 | tf_op jit(solution)/shard_map/ppermute | solution.py:38
  30.4 13.1 %collective-permute-start.4 = (bf16[16,16,512]{2,1,0:T(8,128)(2,1)S(1)}, bf16[16,16,512]{2,1,0:T(8,128)(2,1)S(1)}, u32[]{:S(2)}, u32[]{:S(2)}) collective-permute-start(bf16[16,16,512]{2,1,0:T(8,128)(2,1)S(1)} %all-to-all-done), channel_id=1, source_target_pairs={{0,4},{2,6},{4,0},{6,2},{1,5},{3,7},{5,1},{7,3},{8,12},{10,14},{12... | collective-permute-start | bytes 786440 | tf_op jit(solution)/shard_map/ppermute | solution.py:38
  35.0 13.3 %collective-permute-start.5 = (bf16[16,16,512]{2,1,0:T(8,128)(2,1)S(1)}, bf16[16,16,512]{2,1,0:T(8,128)(2,1)S(1)}, u32[]{:S(2)}, u32[]{:S(2)}) collective-permute-start(bf16[16,16,512]{2,1,0:T(8,128)(2,1)S(1)} %all-to-all-done), channel_id=1, source_target_pairs={{0,6},{2,4},{4,2},{6,0},{1,7},{3,5},{5,3},{7,1},{8,14},{10,12},{12... | collective-permute-start | bytes 786440 | tf_op jit(solution)/shard_map/ppermute | solution.py:38
  49.0 4.9 %collective-permute-start.6 = (bf16[4,16,16,512]{3,2,1,0:T(8,128)(2,1)}, bf16[4,16,16,512]{3,2,1,0:T(8,128)(2,1)}, u32[]{:S(2)}, u32[]{:S(2)}) collective-permute-start(bf16[4,16,16,512]{3,2,1,0:T(8,128)(2,1)} %bitcast_dynamic-update-slice_fusion), channel_id=1, source_target_pairs={{0,1},{1,0},{2,3},{3,2},{4,5},{5,4},{6,7},{7,6},{8,9},{9,8},{10,11... | collective-permute-start | bytes 3145736 | tf_op jit(solution)/shard_map/ppermute | solution.py:38
  57.3 36.2 %collective-permute-start.7 = (bf16[256,256]{1,0:T(8,128)(2,1)S(1)}, bf16[256,256]{1,0:T(8,128)(2,1)S(1)}, u32[]{:S(2)}, u32[]{:S(2)}) collective-permute-start(bf16[256,256]{1,0:T(8,128)(2,1)S(1)} %broadcast_select_fusion), channel_id=1, source_target_pairs={{0,520},{8,512},{256,776},{264,768},{512,8},{520,0},{768,264},{776... | collective-permute-start | bytes 393224 | tf_op jit(solution)/shard_map/ppermute | solution.py:54
  93.6 14.1 %collective-permute-start.8 = (bf16[256,256]{1,0:T(8,128)(2,1)S(1)}, bf16[256,256]{1,0:T(8,128)(2,1)S(1)}, u32[]{:S(2)}, u32[]{:S(2)}) collective-permute-start(bf16[256,256]{1,0:T(8,128)(2,1)S(1)} %add_convert_fusion.2), channel_id=1, source_target_pairs={{0,256},{256,0},{512,768},{768,512},{1,257},{257,1},{513,769},{769... | collective-permute-start | bytes 393224 | tf_op jit(solution)/shard_map/ppermute | solution.py:38
  107.8 26.3 %collective-permute-start.9 = (bf16[256,256]{1,0:T(8,128)(2,1)S(1)}, bf16[256,256]{1,0:T(8,128)(2,1)S(1)}, u32[]{:S(2)}, u32[]{:S(2)}) collective-permute-start(bf16[256,256]{1,0:T(8,128)(2,1)S(1)} %add_convert_fusion.1), channel_id=1, source_target_pairs={{0,512},{256,768},{512,0},{768,256},{1,513},{257,769},{513,1},{769... | collective-permute-start | bytes 393224 | tf_op jit(solution)/shard_map/ppermute | solution.py:38
  134.9 49.3 %all-to-all-start.3 = ((bf16[4,256,256]{2,1,0:T(8,128)(2,1)}), bf16[4,256,256]{2,1,0:T(8,128)(2,1)}, u32[]{:S(2)}, u32[]{:S(2)}) async-start(bf16[4,256,256]{2,1,0:T(8,128)(2,1)} %broadcast_in_dim.65), calls=%async_computation.3 | async-start | bytes 1048576 | tf_op jit(solution)/shard_map/all_to_all | solution.py:42
  143.7 34.0 %collective-permute-start = (bf16[256,256]{1,0:T(8,128)(2,1)S(1)}, bf16[256,256]{1,0:T(8,128)(2,1)S(1)}, u32[]{:S(2)}, u32[]{:S(2)}) collective-permute-start(bf16[256,256]{1,0:T(8,128)(2,1)S(1)} %dynamic-slice_convert_fusion), channel_id=1, source_target_pairs={{0,520},{8,512},{256,776},{264,768},{512,8},{520,0},{768,264},{776... | collective-permute-start | bytes 393224 | tf_op jit(solution)/shard_map/ppermute | solution.py:54
  178.2 4.6 %collective-permute-start.1 = (bf16[2048,256]{1,0:T(8,128)(2,1)S(1)}, bf16[2048,256]{1,0:T(8,128)(2,1)S(1)}, u32[]{:S(2)}, u32[]{:S(2)}) collective-permute-start(bf16[2048,256]{1,0:T(8,128)(2,1)S(1)} %convolution_convert_fusion), channel_id=1, source_target_pairs={{0,1},{1,0},{2,3},{3,2},{4,5},{5,4},{6,7},{7,6},{8,9},{9,8},{10,11... | collective-permute-start | bytes 3145736 | tf_op jit(solution)/shard_map/ppermute | solution.py:38
  184.2 34.2 %all-to-all-start.2 = ((bf16[16,128,256]{2,1,0:T(8,128)(2,1)}), bf16[16,128,256]{2,1,0:T(8,128)(2,1)S(1)}, u32[]{:S(2)}, u32[]{:S(2)}) async-start(bf16[16,128,256]{2,1,0:T(8,128)(2,1)} %bitcast.47), calls=%async_computation.2 | async-start | bytes 2097152 | tf_op jit(solution)/shard_map/all_to_all | solution.py:42
  218.7 18.1 %collective-permute-start.2 = (bf16[128,1024]{0,1:T(8,128)(2,1)S(1)}, bf16[128,1024]{0,1:T(8,128)(2,1)S(1)}, u32[]{:S(2)}, u32[]{:S(2)}) collective-permute-start(bf16[128,1024]{0,1:T(8,128)(2,1)S(1)} %bitcast.50), channel_id=1, source_target_pairs={{0,0},{2,16},{4,32},{6,48},{16,2},{18,18},{20,34},{22,50},{32,4},{... | collective-permute-start | bytes 786440 | tf_op jit(solution)/shard_map/ppermute | solution.py:117

commit v3 on v2

v3 whole, which is shorter than its diff:
```python
import functools

import jax
import jax.numpy as jnp
from jax import lax
from jax.experimental import pallas as pl
from jax.experimental.pallas import tpu as pltpu
from jax.sharding import Mesh
from jax.sharding import PartitionSpec as P


AXES = ("za", "zb", "y", "h", "x", "c")
ROWS = ("y", "h")
COLS = ("x", "c")
TOKENS = ("za", "zb", "y", "h")
NEAR = ("zb", "y")

beta_one = 0.9
beta_two = 0.95
learn_rate = 0.001
weight_decay = 0.1
adam_step = 10
epsilon = 1e-08

SMALL = 8 * 2**20

F32 = jnp.float32
BF16 = jnp.bfloat16


def adamw(grad, master, moment_one, moment_two):
    first = beta_one * moment_one + (1.0 - beta_one) * grad
    second = beta_two * moment_two + (1.0 - beta_two) * grad * grad
    first_hat = first / (1.0 - beta_one**adam_step)
    second_hat = second / (1.0 - beta_two**adam_step)
    updated = master - learn_rate * (
        first_hat / (jnp.sqrt(second_hat) + epsilon) + weight_decay * master
    )
    return (updated, first, second)


def swapped(array, axis, bit=1):
    size = lax.axis_size(axis)
    return lax.ppermute(array, axis, [(k, k ^ bit) for k in range(size)])


def exchanged(pieces, axes):
    return lax.all_to_all(pieces, axes, split_axis=0, concat_axis=0, tiled=True)


def gathered(array, axes):
    count = lax.axis_size(axes)
    return exchanged(jnp.broadcast_to(array[None], (count, *array.shape)), axes)


def across(array):
    count = lax.axis_size("za")
    far = count // 2
    pairs = [(2 * za + h, 2 * (za ^ far) + 1 - h) for za in range(count) for h in range(2)]
    return lax.ppermute(array, ("za", "h"), pairs)


def own_first(pair, index):
    flip = index == 0
    return jnp.where(flip, pair[0], pair[1]), jnp.where(flip, pair[1], pair[0])


def masked_grads(value_grads, lengths):
    tok_rows = value_grads.shape[0]
    seq_count = lengths.shape[0]
    seq_len = tok_rows // seq_count
    index = jnp.arange(tok_rows, dtype=jnp.int32)
    pick = (index // seq_len)[:, None] == jnp.arange(seq_count, dtype=jnp.int32)[None, :]
    limit = jnp.sum(jnp.where(pick, lengths[None, :], 0), axis=1)
    return jnp.where((index % seq_len < limit)[:, None], value_grads, jnp.zeros_like(value_grads))


def share_kernel(nzb, where_ref, act_ref, out_ref):
    near, _, width = out_ref.shape
    part = width // 2
    ny = act_ref.shape[1] // (2 * nzb * part)
    h = where_ref[1]
    for k in range(near):
        zb, y = k // ny, k % ny
        for side, half in enumerate((1 - h, h)):
            start = ((y * 2 + half) * nzb + zb) * part
            block = act_ref[:, pl.ds(pl.multiple_of(start, part), part)]
            out_ref[k, :, side * part : (side + 1) * part] = block


def share_of(activations, index, h, nzb, near, share, part):
    return pl.pallas_call(
        functools.partial(share_kernel, nzb),
        out_shape=jax.ShapeDtypeStruct((near, share, 2 * part), activations.dtype),
        grid_spec=pltpu.PrefetchScalarGridSpec(
            num_scalar_prefetch=1,
            grid=(1,),
            in_specs=[pl.BlockSpec((share, activations.shape[1]), lambda i, where: (where[0], 0))],
            out_specs=pl.BlockSpec((near, share, 2 * part), lambda i, where: (0, 0, 0)),
        ),
        name="share",
    )(jnp.stack([index, h]).astype(jnp.int32), activations)


def outer_kernel(half, x_ref, *refs):
    *pieces, grads_ref, out_ref = refs
    near, tok, _ = grads_ref.shape
    share = tok // len(pieces)
    cols = out_ref.shape[1]
    total = None
    for k, piece in enumerate(pieces):
        start = pl.multiple_of((x_ref[0] ^ k) * share, share)
        grads = grads_ref[:, pl.ds(start, share), half * cols : (half + 1) * cols]
        term = lax.dot_general(
            piece[...],
            grads.reshape(near * share, cols),
            (((0,), (0,)), ((), ())),
            preferred_element_type=F32,
        )
        total = term if total is None else total + term
    out_ref[...] = total.astype(out_ref.dtype)


def outer(x, pieces, grads, half, dtype):
    rows, cols = pieces[0].shape[1], grads.shape[2] // 2
    vmem = pl.BlockSpec(memory_space=pltpu.VMEM)
    depth = grads.shape[0] * grads.shape[1]
    return pl.pallas_call(
        functools.partial(outer_kernel, half),
        out_shape=jax.ShapeDtypeStruct((rows, cols), dtype),
        in_specs=[pl.BlockSpec(memory_space=pltpu.SMEM)] + [vmem] * (len(pieces) + 1),
        out_specs=vmem,
        cost_estimate=pl.CostEstimate(
            flops=2 * depth * rows * cols,
            bytes_accessed=2 * depth * (rows + cols),
            transcendentals=0,
        ),
        compiler_params=pltpu.CompilerParams(vmem_limit_bytes=SMALL),
    )(x.reshape(1), *pieces, grads)


def step(activations, value_grads, lengths, master, moment_one, moment_two):
    tok, _ = activations.shape
    rows, cols = master.shape
    nzb, ny, nx = lax.axis_size("zb"), lax.axis_size("y"), lax.axis_size("x")
    near = nzb * ny
    half = tok // 2
    share = half // nx
    part = rows // nzb
    h, c, zb = lax.axis_index("h"), lax.axis_index("c"), lax.axis_index("zb")
    x = lax.axis_index("x")

    masked = masked_grads(value_grads, lengths)
    vg_own, vg_send = own_first((masked[:half], masked[half:]), c)
    vg_other = swapped(vg_send, "c")
    vg_half = jnp.concatenate([vg_own, vg_other], axis=1)

    weight = lax.dynamic_slice_in_dim(master, zb * part, part, 0).astype(BF16)
    weight_far = across(weight)

    mine = share_of(activations, c * nx + x, h, nzb, near, share, part)
    act_share = exchanged(mine, NEAR)
    copies = jnp.broadcast_to(vg_half[None], (near, half, 2 * cols))
    copies, act_share = lax.optimization_barrier((copies, act_share))
    grads = exchanged(copies, NEAR)
    act_share = act_share.reshape(near * share, 2 * part)
    pieces = [act_share]
    for k in range(1, nx):
        pieces.append(swapped(act_share, "x", k))

    partial = outer(x, pieces, grads, 1, BF16)
    partial = swapped(partial, "c")
    partial = outer(x, pieces, grads, 0, F32) + partial.astype(F32)
    received = across(partial[:part].astype(BF16))
    total = (partial[part:] + received.astype(F32)).astype(BF16)
    for bit in (1, 2):
        if bit < lax.axis_size("za"):
            received = swapped(total, "za", bit)
            total = (total.astype(F32) + received.astype(F32)).astype(BF16)
    grad = gathered(total, "zb").reshape(rows, cols).astype(F32)
    count = float(tok * lax.axis_size(TOKENS))
    new_master, new_one, new_two = adamw(grad / count, master, moment_one, moment_two)

    both = jnp.concatenate(own_first((weight, weight_far), h), axis=0)
    both_other = swapped(both, "c")
    both = jnp.concatenate([both, both_other], axis=1)
    tokens = grads.reshape(near * half, 2 * cols)

    def product(w):
        out = lax.dot_general(tokens, w, (((1,), (1,)), ((), ())), preferred_element_type=F32)
        return out.astype(BF16).reshape(nzb, ny, half, part).transpose(1, 0, 2, 3)

    product = jnp.stack([product(both[:part]), product(both[part:])], axis=1)
    arrived = exchanged(product.reshape(ny * 2, nzb * half, part), COLS)
    block = arrived.reshape(nx, 2, nzb, half, part).astype(F32).sum(axis=0).astype(BF16)
    block = block.transpose(1, 0, 2, 3).reshape(nzb, tok, part)
    block = exchanged(block, "zb")
    block = block.transpose(1, 0, 2).reshape(tok, rows)
    turn = [(y * nx + x, x * nx + y) for y in range(ny) for x in range(nx)]
    input_grads = lax.ppermute(block, ("y", "x"), turn)
    return (input_grads, new_master, new_one, new_two)


def solution(mesh):
    replica, fsdp, tensor = (mesh.shape[a] for a in ("replica", "fsdp", "tensor"))
    near = 4 if replica == 16 else 2
    split = Mesh(
        mesh.devices.reshape(replica // near, near, fsdp // 2, 2, tensor // 2, 2), AXES
    )
    in_specs = (
        P(TOKENS, None),
        P(TOKENS, COLS),
        P(TOKENS),
        P(ROWS, COLS),
        P(ROWS, COLS),
        P(ROWS, COLS),
    )
    out_specs = (P(TOKENS, COLS), P(ROWS, COLS), P(ROWS, COLS), P(ROWS, COLS))
    return jax.shard_map(step, mesh=split, in_specs=in_specs, out_specs=out_specs, check_vma=False)
```

time: 239 us -> 236 us (0.987)
  the two profiles are of different devices: /device:TPU:216 before, /device:TPU:24 now
where the time goes in v3:
time: 236 us; the launch traced here: 235 us
  waiting for transfers between devices  113 us (48%)
  starting transfers between devices  103 us (44%)
  other arithmetic  7.18 us (3%)
  local copies, waits for them, and re-layouts  6.69 us (3%)
  Pallas kernels  3.31 us (1%)
    ppermute x8, waiting for transfers between devices, swapped(): return lax.ppermute(array, axis, [(k, k ^ bit) for k in range(size)])  52.3 us
    ppermute x2, waiting for transfers between devices, across(): return lax.ppermute(array, ('za', 'h'), pairs)  41 us
    all_to_all x5, starting transfers between devices, exchanged(): return lax.all_to_all(pieces, axes, split_axis=0, concat_axis=0, tiled=True)  40.3 us
    ppermute x8, starting transfers between devices, swapped(): return lax.ppermute(array, axis, [(k, k ^ bit) for k in range(size)])  35.2 us
    ppermute x2, starting transfers between devices, across(): return lax.ppermute(array, ('za', 'h'), pairs)  24.5 us
    ppermute x1, waiting for transfers between devices, step(): input_grads = lax.ppermute(block, ('y', 'x'), turn)  16.2 us
  transfers between devices with their start and end apart: 16, of which 9 were waited for; matrix products, arithmetic and copies ran while one was open for 3% of the time, Pallas kernels for 0%

profile of v3, /device:TPU:24, one launch (start us, length us, event | category | flops | bytes accessed | tf_op | source)
XLA Modules:
  0.0 234.8 jit_solution(9750592706329970944)
XLA Ops:
  0.6 0.0 copy-start.4
  0.6 0.0 copy-start.3
  0.7 0.6 pad_add_fusion.where_ref
  1.2 2.4 %share.1 = bf16[16,16,512]{2,1,0:T(8,128)(2,1)} custom-call(s32[2]{0:T(128)} %pad_add_fusion.where_ref, bf16[128,8192]{1,0:T(8,128)(2,1)} %act_ref.1), custom_call_target="tpu_custom_call" | custom-call | tf_op jit(solution)/shard_map/share/pallas_call | solution.py:92
  3.6 16.2 %all-to-all-start = ((bf16[16,16,512]{2,1,0:T(8,128)(2,1)}), bf16[16,16,512]{2,1,0:T(8,128)(2,1)S(1)}, u32[]{:S(2)}, u32[]{:S(2)}) async-start(bf16[16,16,512]{2,1,0:T(8,128)(2,1)} %share.1), calls=%async_computation | async-start | bytes 524288 | tf_op jit(solution)/shard_map/all_to_all | solution.py:48
  19.8 0.0 copy-done.4
  19.8 0.1 fusion.4
  19.9 0.0 copy-done.3
  19.9 0.1 broadcast_select_fusion.2
  20.0 1.9 collective-permute-start
  21.9 1.2 collective-permute-done
  23.1 3.3 %all-to-all-done = bf16[16,16,512]{2,1,0:T(8,128)(2,1)S(1)} async-done(((bf16[16,16,512]{2,1,0:T(8,128)(2,1)}), bf16[16,16,512]{2,1,0:T(8,128)(2,1)S(1)}, u32[]{:S(2)}, u32[]{:S(2)}) %all-to-all-start) | async-done | bytes 262176 | tf_op jit(solution)/shard_map/all_to_all | solution.py:48
  26.4 1.1 broadcast_in_dim.43
  27.5 7.0 %all-to-all-start.1 = ((bf16[16,64,512]{2,1,0:T(8,128)(2,1)}), bf16[16,64,512]{2,1,0:T(8,128)(2,1)S(1)}, u32[]{:S(2)}, u32[]{:S(2)}) async-start(bf16[16,64,512]{2,1,0:T(8,128)(2,1)} %broadcast_in_dim.43), calls=%async_computation.1 | async-start | bytes 2097152 | tf_op jit(solution)/shard_map/all_to_all | solution.py:48
  34.5 1.0 dynamic-slice_convert_fusion
  35.4 13.7 %collective-permute-start.1 = (bf16[256,256]{1,0:T(8,128)(2,1)S(1)}, bf16[256,256]{1,0:T(8,128)(2,1)S(1)}, u32[]{:S(2)}, u32[]{:S(2)}) collective-permute-start(bf16[256,256]{1,0:T(8,128)(2,1)S(1)} %dynamic-slice_convert_fusion), channel_id=1, source_target_pairs={{0,520},{8,512},{256,776},{264,768},{512,8},{520,0},{768,264},{776... | collective-permute-start | bytes 393224 | tf_op jit(solution)/shard_map/ppermute | solution.py:60
  49.2 18.2 %collective-permute-done.1 = bf16[256,256]{1,0:T(8,128)(2,1)S(1)} collective-permute-done((bf16[256,256]{1,0:T(8,128)(2,1)S(1)}, bf16[256,256]{1,0:T(8,128)(2,1)S(1)}, u32[]{:S(2)}, u32[]{:S(2)}) %collective-permute-start.1) | collective-permute-done | bytes 131104 | tf_op jit(solution)/shard_map/ppermute | solution.py:60
  67.4 1.0 broadcast_select_fusion.1
  68.4 1.9 collective-permute-start.2
  70.3 1.5 collective-permute-done.2
  71.9 0.0 all-to-all-done.1.refs_4_
  71.9 0.5 convolution_convert_fusion
  72.4 0.5 convolution_convert_fusion.1
  72.8 0.1 copy_bitcast_fusion
  72.9 1.1 pad_maximum_fusion
  74.0 7.3 %all-to-all-start.2 = ((bf16[8,256,256]{2,1,0:T(8,128)(2,1)}), bf16[8,256,256]{2,1,0:T(8,128)(2,1)S(1)}, u32[]{:S(2)}, u32[]{:S(2)}) async-start(bf16[8,256,256]{2,1,0:T(8,128)(2,1)} %bitcast.9), calls=%async_computation.2 | async-start | bytes 2097152 | tf_op jit(solution)/shard_map/all_to_all | solution.py:48
  81.3 5.1 %collective-permute-start.6 = (bf16[256,512]{1,0:T(8,128)(2,1)S(1)}, bf16[256,512]{1,0:T(8,128)(2,1)S(1)}, u32[]{:S(2)}, u32[]{:S(2)}) collective-permute-start(bf16[256,512]{1,0:T(8,128)(2,1)S(1)} %bitcast.32), channel_id=1, source_target_pairs={{0,6},{2,4},{4,2},{6,0},{1,7},{3,5},{5,3},{7,1},{8,14},{10,12},{12... | collective-permute-start | bytes 786440 | tf_op jit(solution)/shard_map/ppermute | solution.py:44
  86.5 2.8 %collective-permute-start.5 = (bf16[256,512]{1,0:T(8,128)(2,1)S(1)}, bf16[256,512]{1,0:T(8,128)(2,1)S(1)}, u32[]{:S(2)}, u32[]{:S(2)}) collective-permute-start(bf16[256,512]{1,0:T(8,128)(2,1)S(1)} %bitcast.33), channel_id=1, source_target_pairs={{0,4},{2,6},{4,0},{6,2},{1,5},{3,7},{5,1},{7,3},{8,12},{10,14},{12... | collective-permute-start | bytes 786440 | tf_op jit(solution)/shard_map/ppermute | solution.py:44
  89.2 1.9 collective-permute-start.4
  91.2 17.0 %collective-permute-done.6.refs_3_ = bf16[256,512]{1,0:T(8,128)(2,1)S(1)} collective-permute-done((bf16[256,512]{1,0:T(8,128)(2,1)S(1)}, bf16[256,512]{1,0:T(8,128)(2,1)S(1)}, u32[]{:S(2)}, u32[]{:S(2)}) %collective-permute-start.6) | collective-permute-done | bytes 262176 | tf_op jit(solution)/shard_map/ppermute | solution.py:44
  108.2 0.0 collective-permute-done.5.refs_2_
  108.2 0.0 collective-permute-done.4.refs_1_
  108.2 0.5 shard_map.94
  108.7 1.9 collective-permute-start.7
  110.6 0.0 all-to-all-done.2
  110.6 0.9 reduce_sum.22
  111.6 1.7 copy.21
  113.2 6.3 %all-to-all-start.3 = ((bf16[4,128,256]{2,1,0:T(8,128)(2,1)}), bf16[4,128,256]{2,1,0:T(8,128)(2,1)S(1)}, u32[]{:S(2)}, u32[]{:S(2)}) async-start(bf16[4,128,256]{2,1,0:T(8,128)(2,1)} %bitcast.12), calls=%async_computation.3 | async-start | bytes 524288 | tf_op jit(solution)/shard_map/all_to_all | solution.py:48
  119.5 0.5 shard_map.93
  120.0 0.0 collective-permute-done.7
  120.0 1.0 convert_add_fusion
  121.1 10.8 %collective-permute-start.8 = (bf16[256,256]{1,0:T(8,128)(2,1)S(1)}, bf16[256,256]{1,0:T(8,128)(2,1)S(1)}, u32[]{:S(2)}, u32[]{:S(2)}) collective-permute-start(bf16[256,256]{1,0:T(8,128)(2,1)S(1)} %slice.43), channel_id=1, source_target_pairs={{0,520},{8,512},{256,776},{264,768},{512,8},{520,0},{768,264},{776... | collective-permute-start | bytes 393224 | tf_op jit(solution)/shard_map/ppermute | solution.py:60
  131.8 22.8 %collective-permute-done.8 = bf16[256,256]{1,0:T(8,128)(2,1)S(1)} collective-permute-done((bf16[256,256]{1,0:T(8,128)(2,1)S(1)}, bf16[256,256]{1,0:T(8,128)(2,1)S(1)}, u32[]{:S(2)}, u32[]{:S(2)}) %collective-permute-start.8) | collective-permute-done | bytes 131104 | tf_op jit(solution)/shard_map/ppermute | solution.py:60
  154.6 1.9 collective-permute-start.9
  156.6 15.8 %collective-permute-done.9 = bf16[256,256]{1,0:T(8,128)(2,1)S(1)} collective-permute-done((bf16[256,256]{1,0:T(8,128)(2,1)S(1)}, bf16[256,256]{1,0:T(8,128)(2,1)S(1)}, u32[]{:S(2)}, u32[]{:S(2)}) %collective-permute-start.9) | collective-permute-done | bytes 131104 | tf_op jit(solution)/shard_map/ppermute | solution.py:44
  172.4 17.7 %collective-permute-start.10 = (bf16[256,256]{1,0:T(8,128)(2,1)S(1)}, bf16[256,256]{1,0:T(8,128)(2,1)S(1)}, u32[]{:S(2)}, u32[]{:S(2)}) collective-permute-start(bf16[256,256]{1,0:T(8,128)(2,1)S(1)} %add_convert_fusion.1), channel_id=1, source_target_pairs={{0,512},{256,768},{512,0},{768,256},{1,513},{257,769},{513,1},{769... | collective-permute-start | bytes 393224 | tf_op jit(solution)/shard_map/ppermute | solution.py:44
  190.1 16.8 %collective-permute-done.10 = bf16[256,256]{1,0:T(8,128)(2,1)S(1)} collective-permute-done((bf16[256,256]{1,0:T(8,128)(2,1)S(1)}, bf16[256,256]{1,0:T(8,128)(2,1)S(1)}, u32[]{:S(2)}, u32[]{:S(2)}) %collective-permute-start.10) | collective-permute-done | bytes 131104 | tf_op jit(solution)/shard_map/ppermute | solution.py:44
  206.9 0.0 all-to-all-done.3
  206.9 0.8 broadcast_in_dim.44
  207.8 3.5 %all-to-all-start.4 = ((bf16[4,256,256]{2,1,0:T(8,128)(2,1)}), bf16[4,256,256]{2,1,0:T(8,128)(2,1)S(1)}, u32[]{:S(2)}, u32[]{:S(2)}) async-start(bf16[4,256,256]{2,1,0:T(8,128)(2,1)} %broadcast_in_dim.44), calls=%async_computation.4 | async-start | bytes 1048576 | tf_op jit(solution)/shard_map/all_to_all | solution.py:48
  211.2 0.0 copy-start
  211.3 0.2 copy.22
  211.4 0.0 copy-start.1
  211.4 2.9 %collective-permute-start.3 = (bf16[128,1024]{0,1:T(8,128)(2,1)S(1)}, bf16[128,1024]{0,1:T(8,128)(2,1)S(1)}, u32[]{:S(2)}, u32[]{:S(2)}) collective-permute-start(bf16[128,1024]{0,1:T(8,128)(2,1)S(1)} %bitcast.41), channel_id=1, source_target_pairs={{0,0},{2,16},{4,32},{6,48},{16,2},{18,18},{20,34},{22,50},{32,4},{... | collective-permute-start | bytes 786440 | tf_op jit(solution)/shard_map/ppermute | solution.py:200
  214.4 16.2 %collective-permute-done.3 = bf16[128,1024]{0,1:T(8,128)(2,1)S(1)} collective-permute-done((bf16[128,1024]{0,1:T(8,128)(2,1)S(1)}, bf16[128,1024]{0,1:T(8,128)(2,1)S(1)}, u32[]{:S(2)}, u32[]{:S(2)}) %collective-permute-start.3) | collective-permute-done | bytes 262176 | tf_op jit(solution)/shard_map/ppermute | solution.py:200
  230.6 0.8 copy.23
  231.5 0.0 all-to-all-done.4
  231.5 0.0 copy-start.2
  231.5 0.2 fusion
  231.7 0.0 copy-done
  231.7 0.0 copy-done.1
  231.7 1.0 copy-done.2
  232.7 2.1 multiply_subtract_fusion
  (10 shorter events, 0.2 us)
Async XLA Ops:
  0.6 19.2 %copy-start.4 = (s32[2]{0:T(128)S(1)}, s32[2]{0:T(128)}, u32[]{:S(2)}) copy-start(s32[2]{0:T(128)} %param.8) | copy-start | bytes 28
  0.6 19.3 %copy-start.3 = (bf16[128,256]{1,0:T(8,128)(2,1)S(1)}, bf16[128,256]{1,0:T(8,128)(2,1)}, u32[]{:S(2)}) copy-start(bf16[128,256]{1,0:T(8,128)(2,1)} %param.7) | copy-start | bytes 196612
  3.6 22.8 %all-to-all-start = ((bf16[16,16,512]{2,1,0:T(8,128)(2,1)}), bf16[16,16,512]{2,1,0:T(8,128)(2,1)S(1)}, u32[]{:S(2)}, u32[]{:S(2)}) async-start(bf16[16,16,512]{2,1,0:T(8,128)(2,1)} %share.1), calls=%async_computation | async-start | bytes 524288 | tf_op jit(solution)/shard_map/all_to_all | solution.py:48
  20.0 3.1 %collective-permute-start = (bf16[64,256]{1,0:T(8,128)(2,1)S(1)}, bf16[64,256]{1,0:T(8,128)(2,1)S(1)}, u32[]{:S(2)}, u32[]{:S(2)}) collective-permute-start(bf16[64,256]{1,0:T(8,128)(2,1)S(1)} %get-tuple-element.24), channel_id=1, source_target_pairs={{0,1},{1,0},{2,3},{3,2},{4,5},{5,4},{6,7},{7,6},{8,9},{9,8},{10,11... | collective-permute-start | bytes 98312 | tf_op jit(solution)/shard_map/ppermute | solution.py:44
  27.5 44.4 %all-to-all-start.1 = ((bf16[16,64,512]{2,1,0:T(8,128)(2,1)}), bf16[16,64,512]{2,1,0:T(8,128)(2,1)S(1)}, u32[]{:S(2)}, u32[]{:S(2)}) async-start(bf16[16,64,512]{2,1,0:T(8,128)(2,1)} %broadcast_in_dim.43), calls=%async_computation.1 | async-start | bytes 2097152 | tf_op jit(solution)/shard_map/all_to_all | solution.py:48
  35.4 32.0 %collective-permute-start.1 = (bf16[256,256]{1,0:T(8,128)(2,1)S(1)}, bf16[256,256]{1,0:T(8,128)(2,1)S(1)}, u32[]{:S(2)}, u32[]{:S(2)}) collective-permute-start(bf16[256,256]{1,0:T(8,128)(2,1)S(1)} %dynamic-slice_convert_fusion), channel_id=1, source_target_pairs={{0,520},{8,512},{256,776},{264,768},{512,8},{520,0},{768,264},{776... | collective-permute-start | bytes 393224 | tf_op jit(solution)/shard_map/ppermute | solution.py:60
  68.4 3.4 %collective-permute-start.2 = (bf16[512,256]{1,0:T(8,128)(2,1)S(1)}, bf16[512,256]{1,0:T(8,128)(2,1)S(1)}, u32[]{:S(2)}, u32[]{:S(2)}) collective-permute-start(bf16[512,256]{1,0:T(8,128)(2,1)S(1)} %pad_maximum_fusion.2), channel_id=1, source_target_pairs={{0,1},{1,0},{2,3},{3,2},{4,5},{5,4},{6,7},{7,6},{8,9},{9,8},{10,11... | collective-permute-start | bytes 786440 | tf_op jit(solution)/shard_map/ppermute | solution.py:44
  74.0 36.6 %all-to-all-start.2 = ((bf16[8,256,256]{2,1,0:T(8,128)(2,1)}), bf16[8,256,256]{2,1,0:T(8,128)(2,1)S(1)}, u32[]{:S(2)}, u32[]{:S(2)}) async-start(bf16[8,256,256]{2,1,0:T(8,128)(2,1)} %bitcast.9), calls=%async_computation.2 | async-start | bytes 2097152 | tf_op jit(solution)/shard_map/all_to_all | solution.py:48
  81.3 26.9 %collective-permute-start.6 = (bf16[256,512]{1,0:T(8,128)(2,1)S(1)}, bf16[256,512]{1,0:T(8,128)(2,1)S(1)}, u32[]{:S(2)}, u32[]{:S(2)}) collective-permute-start(bf16[256,512]{1,0:T(8,128)(2,1)S(1)} %bitcast.32), channel_id=1, source_target_pairs={{0,6},{2,4},{4,2},{6,0},{1,7},{3,5},{5,3},{7,1},{8,14},{10,12},{12... | collective-permute-start | bytes 786440 | tf_op jit(solution)/shard_map/ppermute | solution.py:44
  86.5 21.7 %collective-permute-start.5 = (bf16[256,512]{1,0:T(8,128)(2,1)S(1)}, bf16[256,512]{1,0:T(8,128)(2,1)S(1)}, u32[]{:S(2)}, u32[]{:S(2)}) collective-permute-start(bf16[256,512]{1,0:T(8,128)(2,1)S(1)} %bitcast.33), channel_id=1, source_target_pairs={{0,4},{2,6},{4,0},{6,2},{1,5},{3,7},{5,1},{7,3},{8,12},{10,14},{12... | collective-permute-start | bytes 786440 | tf_op jit(solution)/shard_map/ppermute | solution.py:44
  89.2 19.0 %collective-permute-start.4 = (bf16[256,512]{1,0:T(8,128)(2,1)S(1)}, bf16[256,512]{1,0:T(8,128)(2,1)S(1)}, u32[]{:S(2)}, u32[]{:S(2)}) collective-permute-start(bf16[256,512]{1,0:T(8,128)(2,1)S(1)} %bitcast.34), channel_id=1, source_target_pairs={{0,2},{2,0},{4,6},{6,4},{1,3},{3,1},{5,7},{7,5},{8,10},{10,8},{12,... | collective-permute-start | bytes 786440 | tf_op jit(solution)/shard_map/ppermute | solution.py:44
  108.7 11.3 %collective-permute-start.7 = (bf16[512,256]{1,0:T(8,128)(2,1)S(1)}, bf16[512,256]{1,0:T(8,128)(2,1)}, u32[]{:S(2)}, u32[]{:S(2)}) collective-permute-start(bf16[512,256]{1,0:T(8,128)(2,1)S(1)} %shard_map.94), channel_id=1, source_target_pairs={{0,1},{1,0},{2,3},{3,2},{4,5},{5,4},{6,7},{7,6},{8,9},{9,8},{10,11... | collective-permute-start | bytes 786440 | tf_op jit(solution)/shard_map/ppermute | solution.py:44
  113.2 93.7 %all-to-all-start.3 = ((bf16[4,128,256]{2,1,0:T(8,128)(2,1)}), bf16[4,128,256]{2,1,0:T(8,128)(2,1)S(1)}, u32[]{:S(2)}, u32[]{:S(2)}) async-start(bf16[4,128,256]{2,1,0:T(8,128)(2,1)} %bitcast.12), calls=%async_computation.3 | async-start | bytes 524288 | tf_op jit(solution)/shard_map/all_to_all | solution.py:48
  121.1 33.5 %collective-permute-start.8 = (bf16[256,256]{1,0:T(8,128)(2,1)S(1)}, bf16[256,256]{1,0:T(8,128)(2,1)S(1)}, u32[]{:S(2)}, u32[]{:S(2)}) collective-permute-start(bf16[256,256]{1,0:T(8,128)(2,1)S(1)} %slice.43), channel_id=1, source_target_pairs={{0,520},{8,512},{256,776},{264,768},{512,8},{520,0},{768,264},{776... | collective-permute-start | bytes 393224 | tf_op jit(solution)/shard_map/ppermute | solution.py:60
  154.6 17.8 %collective-permute-start.9 = (bf16[256,256]{1,0:T(8,128)(2,1)S(1)}, bf16[256,256]{1,0:T(8,128)(2,1)S(1)}, u32[]{:S(2)}, u32[]{:S(2)}) collective-permute-start(bf16[256,256]{1,0:T(8,128)(2,1)S(1)} %fusion.1), channel_id=1, source_target_pairs={{0,256},{256,0},{512,768},{768,512},{1,257},{257,1},{513,769},{769... | collective-permute-start | bytes 393224 | tf_op jit(solution)/shard_map/ppermute | solution.py:44
  172.4 34.5 %collective-permute-start.10 = (bf16[256,256]{1,0:T(8,128)(2,1)S(1)}, bf16[256,256]{1,0:T(8,128)(2,1)S(1)}, u32[]{:S(2)}, u32[]{:S(2)}) collective-permute-start(bf16[256,256]{1,0:T(8,128)(2,1)S(1)} %add_convert_fusion.1), channel_id=1, source_target_pairs={{0,512},{256,768},{512,0},{768,256},{1,513},{257,769},{513,1},{769... | collective-permute-start | bytes 393224 | tf_op jit(solution)/shard_map/ppermute | solution.py:44
  207.8 23.7 %all-to-all-start.4 = ((bf16[4,256,256]{2,1,0:T(8,128)(2,1)}), bf16[4,256,256]{2,1,0:T(8,128)(2,1)S(1)}, u32[]{:S(2)}, u32[]{:S(2)}) async-start(bf16[4,256,256]{2,1,0:T(8,128)(2,1)} %broadcast_in_dim.44), calls=%async_computation.4 | async-start | bytes 1048576 | tf_op jit(solution)/shard_map/all_to_all | solution.py:48
  211.2 20.5 %copy-start = (f32[1024,256]{1,0:T(8,128)S(1)}, f32[1024,256]{1,0:T(8,128)}, u32[]{:S(2)}) copy-start(f32[1024,256]{1,0:T(8,128)} %param.9) | copy-start | bytes 3145732
  211.4 20.3 %copy-start.1 = (f32[1024,256]{1,0:T(8,128)S(1)}, f32[1024,256]{1,0:T(8,128)}, u32[]{:S(2)}) copy-start(f32[1024,256]{1,0:T(8,128)} %param.10) | copy-start | bytes 3145732
  211.4 19.2 %collective-permute-start.3 = (bf16[128,1024]{0,1:T(8,128)(2,1)S(1)}, bf16[128,1024]{0,1:T(8,128)(2,1)S(1)}, u32[]{:S(2)}, u32[]{:S(2)}) collective-permute-start(bf16[128,1024]{0,1:T(8,128)(2,1)S(1)} %bitcast.41), channel_id=1, source_target_pairs={{0,0},{2,16},{4,32},{6,48},{16,2},{18,18},{20,34},{22,50},{32,4},{... | collective-permute-start | bytes 786440 | tf_op jit(solution)/shard_map/ppermute | solution.py:200
  231.5 1.2 copy-start.2

commit v4 on v3

--- a/solution.py
+++ b/solution.py
@@ -104,16 +104,20 @@
 
 def outer_kernel(half, x_ref, *refs):
     *pieces, grads_ref, out_ref = refs
-    near, tok, _ = grads_ref.shape
+    ny, nzb, tok, _ = grads_ref.shape
     share = tok // len(pieces)
     cols = out_ref.shape[1]
     total = None
     for k, piece in enumerate(pieces):
         start = pl.multiple_of((x_ref[0] ^ k) * share, share)
-        grads = grads_ref[:, pl.ds(start, share), half * cols : (half + 1) * cols]
+        grads = [
+            grads_ref[y, zb, pl.ds(start, share), half * cols : (half + 1) * cols]
+            for zb in range(nzb)
+            for y in range(ny)
+        ]
         term = lax.dot_general(
             piece[...],
-            grads.reshape(near * share, cols),
+            jnp.concatenate(grads, axis=0),
             (((0,), (0,)), ((), ())),
             preferred_element_type=F32,
         )
@@ -122,9 +126,9 @@
 
 
 def outer(x, pieces, grads, half, dtype):
-    rows, cols = pieces[0].shape[1], grads.shape[2] // 2
+    rows, cols = pieces[0].shape[1], grads.shape[3] // 2
     vmem = pl.BlockSpec(memory_space=pltpu.VMEM)
-    depth = grads.shape[0] * grads.shape[1]
+    depth = sum(piece.shape[0] for piece in pieces)
     return pl.pallas_call(
         functools.partial(outer_kernel, half),
         out_shape=jax.ShapeDtypeStruct((rows, cols), dtype),
@@ -154,15 +158,16 @@
     vg_own, vg_send = own_first((masked[:half], masked[half:]), c)
     vg_other = swapped(vg_send, "c")
     vg_half = jnp.concatenate([vg_own, vg_other], axis=1)
+    vg_near = gathered(vg_half, "zb").reshape(nzb * half, 2 * cols)
 
     weight = lax.dynamic_slice_in_dim(master, zb * part, part, 0).astype(BF16)
     weight_far = across(weight)
 
     mine = share_of(activations, c * nx + x, h, nzb, near, share, part)
     act_share = exchanged(mine, NEAR)
-    copies = jnp.broadcast_to(vg_half[None], (near, half, 2 * cols))
+    copies = jnp.broadcast_to(vg_near[None], (ny, nzb * half, 2 * cols))
     copies, act_share = lax.optimization_barrier((copies, act_share))
-    grads = exchanged(copies, NEAR)
+    grads = exchanged(copies, "y").reshape(ny, nzb, half, 2 * cols)
     act_share = act_share.reshape(near * share, 2 * part)
     pieces = [act_share]
     for k in range(1, nx):
@@ -188,7 +193,7 @@
 
     def product(w):
         out = lax.dot_general(tokens, w, (((1,), (1,)), ((), ())), preferred_element_type=F32)
-        return out.astype(BF16).reshape(nzb, ny, half, part).transpose(1, 0, 2, 3)
+        return out.astype(BF16).reshape(ny, nzb, half, part)
 
     product = jnp.stack([product(both[:part]), product(both[part:])], axis=1)
     arrived = exchanged(product.reshape(ny * 2, nzb * half, part), COLS)

time: 236 us -> 230 us (0.975)
  the two profiles are of different devices: /device:TPU:24 before, /device:TPU:25 now
where the time goes in v4:
time: 230 us; the launch traced here: 229 us
  waiting for transfers between devices  117 us (51%)
  starting transfers between devices  90.8 us (39%)
  other arithmetic  8.68 us (4%)
  local copies, waits for them, and re-layouts  7.29 us (3%)
  Pallas kernels  3.32 us (1%)
    ppermute x8, waiting for transfers between devices, swapped(): return lax.ppermute(array, axis, [(k, k ^ bit) for k in range(size)])  57.4 us
    ppermute x2, waiting for transfers between devices, across(): return lax.ppermute(array, ('za', 'h'), pairs)  38.9 us
    all_to_all x6, starting transfers between devices, exchanged(): return lax.all_to_all(pieces, axes, split_axis=0, concat_axis=0, tiled=True)  35.2 us
    ppermute x8, starting transfers between devices, swapped(): return lax.ppermute(array, axis, [(k, k ^ bit) for k in range(size)])  27.8 us
    ppermute x2, starting transfers between devices, across(): return lax.ppermute(array, ('za', 'h'), pairs)  25.6 us
    ppermute x1, waiting for transfers between devices, step(): input_grads = lax.ppermute(block, ('y', 'x'), turn)  16.6 us
  transfers between devices with their start and end apart: 17, of which 9 were waited for; matrix products, arithmetic and copies ran while one was open for 4% of the time, Pallas kernels for 1%

profile of v4, /device:TPU:25, one launch (start us, length us, event | category | flops | bytes accessed | tf_op | source)
XLA Modules:
  0.0 229.3 jit_solution(7749662201399177861)
XLA Ops:
  0.6 0.7 fusion.4
  1.4 0.9 broadcast_select_fusion.2
  2.3 2.6 %collective-permute-start = (bf16[64,256]{1,0:T(8,128)(2,1)S(1)}, bf16[64,256]{1,0:T(8,128)(2,1)S(1)}, u32[]{:S(2)}, u32[]{:S(2)}) collective-permute-start(bf16[64,256]{1,0:T(8,128)(2,1)S(1)} %get-tuple-element.24), channel_id=1, source_target_pairs={{0,1},{1,0},{2,3},{3,2},{4,5},{5,4},{6,7},{7,6},{8,9},{9,8},{10,11... | collective-permute-start | bytes 98312 | tf_op jit(solution)/shard_map/ppermute | solution.py:44
  4.9 0.8 collective-permute-done
  5.8 0.7 broadcast_in_dim.50
  6.5 5.6 %all-to-all-start = ((bf16[4,64,512]{2,1,0:T(8,128)(2,1)}), bf16[4,64,512]{2,1,0:T(8,128)(2,1)S(1)}, u32[]{:S(2)}, u32[]{:S(2)}) async-start(bf16[4,64,512]{2,1,0:T(8,128)(2,1)} %broadcast_in_dim.50), calls=%async_computation | async-start | bytes 524288 | tf_op jit(solution)/shard_map/all_to_all | solution.py:48
  12.1 0.6 pad_add_fusion.where_ref
  12.7 2.4 %share.1 = bf16[16,16,512]{2,1,0:T(8,128)(2,1)} custom-call(s32[2]{0:T(128)} %pad_add_fusion.where_ref, bf16[128,8192]{1,0:T(8,128)(2,1)} %act_ref.1), custom_call_target="tpu_custom_call" | custom-call | tf_op jit(solution)/shard_map/share/pallas_call | solution.py:92
  15.1 4.5 %all-to-all-done = bf16[4,64,512]{2,1,0:T(8,128)(2,1)S(1)} async-done(((bf16[4,64,512]{2,1,0:T(8,128)(2,1)}), bf16[4,64,512]{2,1,0:T(8,128)(2,1)S(1)}, u32[]{:S(2)}, u32[]{:S(2)}) %all-to-all-start) | async-done | bytes 262176 | tf_op jit(solution)/shard_map/all_to_all | solution.py:48
  19.5 13.8 %all-to-all-start.1 = ((bf16[16,16,512]{2,1,0:T(8,128)(2,1)}), bf16[16,16,512]{2,1,0:T(8,128)(2,1)S(1)}, u32[]{:S(2)}, u32[]{:S(2)}) async-start(bf16[16,16,512]{2,1,0:T(8,128)(2,1)} %share.1), calls=%async_computation.1 | async-start | bytes 524288 | tf_op jit(solution)/shard_map/all_to_all | solution.py:48
  33.3 1.0 dynamic-slice_convert_fusion
  34.3 12.7 %collective-permute-start.1 = (bf16[256,256]{1,0:T(8,128)(2,1)S(1)}, bf16[256,256]{1,0:T(8,128)(2,1)S(1)}, u32[]{:S(2)}, u32[]{:S(2)}) collective-permute-start(bf16[256,256]{1,0:T(8,128)(2,1)S(1)} %dynamic-slice_convert_fusion), channel_id=1, source_target_pairs={{0,520},{8,512},{256,776},{264,768},{512,8},{520,0},{768,264},{776... | collective-permute-start | bytes 393224 | tf_op jit(solution)/shard_map/ppermute | solution.py:60
  47.0 0.0 all-to-all-done.1
  47.1 1.1 broadcast_in_dim.52
  48.1 4.2 %all-to-all-start.2 = ((bf16[4,256,512]{2,1,0:T(8,128)(2,1)}), bf16[4,256,512]{2,1,0:T(8,128)(2,1)S(1)}, u32[]{:S(2)}, u32[]{:S(2)}) async-start(bf16[4,256,512]{2,1,0:T(8,128)(2,1)} %broadcast_in_dim.52), calls=%async_computation.2 | async-start | bytes 2097152 | tf_op jit(solution)/shard_map/all_to_all | solution.py:48
  52.3 16.5 %collective-permute-done.1 = bf16[256,256]{1,0:T(8,128)(2,1)S(1)} collective-permute-done((bf16[256,256]{1,0:T(8,128)(2,1)S(1)}, bf16[256,256]{1,0:T(8,128)(2,1)S(1)}, u32[]{:S(2)}, u32[]{:S(2)}) %collective-permute-start.1) | collective-permute-done | bytes 131104 | tf_op jit(solution)/shard_map/ppermute | solution.py:60
  68.9 1.0 broadcast_select_fusion.1
  69.9 3.4 %collective-permute-start.2 = (bf16[512,256]{1,0:T(8,128)(2,1)S(1)}, bf16[512,256]{1,0:T(8,128)(2,1)S(1)}, u32[]{:S(2)}, u32[]{:S(2)}) collective-permute-start(bf16[512,256]{1,0:T(8,128)(2,1)S(1)} %pad_maximum_fusion.2), channel_id=1, source_target_pairs={{0,1},{1,0},{2,3},{3,2},{4,5},{5,4},{6,7},{7,6},{8,9},{9,8},{10,11... | collective-permute-start | bytes 786440 | tf_op jit(solution)/shard_map/ppermute | solution.py:44
  73.3 1.1 collective-permute-done.2
  74.5 0.0 all-to-all-done.2
  74.5 0.5 convolution_convert_fusion
  75.0 0.5 convolution_convert_fusion.1
  75.5 1.1 pad_maximum_fusion
  76.5 4.7 %all-to-all-start.3 = ((bf16[8,256,256]{2,1,0:T(8,128)(2,1)}), bf16[8,256,256]{2,1,0:T(8,128)(2,1)S(1)}, u32[]{:S(2)}, u32[]{:S(2)}) async-start(bf16[8,256,256]{2,1,0:T(8,128)(2,1)} %bitcast.8), calls=%async_computation.3 | async-start | bytes 2097152 | tf_op jit(solution)/shard_map/all_to_all | solution.py:48
  81.2 4.5 %collective-permute-start.6 = (bf16[256,512]{1,0:T(8,128)(2,1)S(1)}, bf16[256,512]{1,0:T(8,128)(2,1)S(1)}, u32[]{:S(2)}, u32[]{:S(2)}) collective-permute-start(bf16[256,512]{1,0:T(8,128)(2,1)S(1)} %bitcast.32), channel_id=1, source_target_pairs={{0,6},{2,4},{4,2},{6,0},{1,7},{3,5},{5,3},{7,1},{8,14},{10,12},{12... | collective-permute-start | bytes 786440 | tf_op jit(solution)/shard_map/ppermute | solution.py:44
  85.7 2.5 %collective-permute-start.5 = (bf16[256,512]{1,0:T(8,128)(2,1)S(1)}, bf16[256,512]{1,0:T(8,128)(2,1)S(1)}, u32[]{:S(2)}, u32[]{:S(2)}) collective-permute-start(bf16[256,512]{1,0:T(8,128)(2,1)S(1)} %bitcast.33), channel_id=1, source_target_pairs={{0,4},{2,6},{4,0},{6,2},{1,5},{3,7},{5,1},{7,3},{8,12},{10,14},{12... | collective-permute-start | bytes 786440 | tf_op jit(solution)/shard_map/ppermute | solution.py:44
  88.1 2.0 collective-permute-start.4
  90.2 17.1 %collective-permute-done.6.refs_3_ = bf16[256,512]{1,0:T(8,128)(2,1)S(1)} collective-permute-done((bf16[256,512]{1,0:T(8,128)(2,1)S(1)}, bf16[256,512]{1,0:T(8,128)(2,1)S(1)}, u32[]{:S(2)}, u32[]{:S(2)}) %collective-permute-start.6) | collective-permute-done | bytes 262176 | tf_op jit(solution)/shard_map/ppermute | solution.py:44
  107.3 0.0 collective-permute-done.5.refs_2_
  107.3 0.0 collective-permute-done.4.refs_1_
  107.3 0.5 shard_map.94
  107.8 2.7 %collective-permute-start.7 = (bf16[512,256]{1,0:T(8,128)(2,1)S(1)}, bf16[512,256]{1,0:T(8,128)(2,1)}, u32[]{:S(2)}, u32[]{:S(2)}) collective-permute-start(bf16[512,256]{1,0:T(8,128)(2,1)S(1)} %shard_map.94), channel_id=1, source_target_pairs={{0,1},{1,0},{2,3},{3,2},{4,5},{5,4},{6,7},{7,6},{8,9},{9,8},{10,11... | collective-permute-start | bytes 786440 | tf_op jit(solution)/shard_map/ppermute | solution.py:44
  110.5 0.0 all-to-all-done.3
  110.5 0.9 reduce_sum.22
  111.4 1.7 copy.21
  113.1 3.4 %all-to-all-start.4 = ((bf16[4,128,256]{2,1,0:T(8,128)(2,1)}), bf16[4,128,256]{2,1,0:T(8,128)(2,1)S(1)}, u32[]{:S(2)}, u32[]{:S(2)}) async-start(bf16[4,128,256]{2,1,0:T(8,128)(2,1)} %bitcast.11), calls=%async_computation.4 | async-start | bytes 524288 | tf_op jit(solution)/shard_map/all_to_all | solution.py:48
  116.5 0.5 shard_map.93
  117.0 0.0 collective-permute-done.7
  117.0 1.0 convert_add_fusion
  118.0 12.8 %collective-permute-start.8 = (bf16[256,256]{1,0:T(8,128)(2,1)S(1)}, bf16[256,256]{1,0:T(8,128)(2,1)S(1)}, u32[]{:S(2)}, u32[]{:S(2)}) collective-permute-start(bf16[256,256]{1,0:T(8,128)(2,1)S(1)} %slice.43), channel_id=1, source_target_pairs={{0,520},{8,512},{256,776},{264,768},{512,8},{520,0},{768,264},{776... | collective-permute-start | bytes 393224 | tf_op jit(solution)/shard_map/ppermute | solution.py:60
  130.9 22.3 %collective-permute-done.8 = bf16[256,256]{1,0:T(8,128)(2,1)S(1)} collective-permute-done((bf16[256,256]{1,0:T(8,128)(2,1)S(1)}, bf16[256,256]{1,0:T(8,128)(2,1)S(1)}, u32[]{:S(2)}, u32[]{:S(2)}) %collective-permute-start.8) | collective-permute-done | bytes 131104 | tf_op jit(solution)/shard_map/ppermute | solution.py:60
  153.2 1.9 collective-permute-start.9
  155.2 16.0 %collective-permute-done.9 = bf16[256,256]{1,0:T(8,128)(2,1)S(1)} collective-permute-done((bf16[256,256]{1,0:T(8,128)(2,1)S(1)}, bf16[256,256]{1,0:T(8,128)(2,1)S(1)}, u32[]{:S(2)}, u32[]{:S(2)}) %collective-permute-start.9) | collective-permute-done | bytes 131104 | tf_op jit(solution)/shard_map/ppermute | solution.py:44
  171.2 8.2 %collective-permute-start.10 = (bf16[256,256]{1,0:T(8,128)(2,1)S(1)}, bf16[256,256]{1,0:T(8,128)(2,1)S(1)}, u32[]{:S(2)}, u32[]{:S(2)}) collective-permute-start(bf16[256,256]{1,0:T(8,128)(2,1)S(1)} %add_convert_fusion.1), channel_id=1, source_target_pairs={{0,512},{256,768},{512,0},{768,256},{1,513},{257,769},{513,1},{769... | collective-permute-start | bytes 393224 | tf_op jit(solution)/shard_map/ppermute | solution.py:44
  179.3 22.4 %collective-permute-done.10 = bf16[256,256]{1,0:T(8,128)(2,1)S(1)} collective-permute-done((bf16[256,256]{1,0:T(8,128)(2,1)S(1)}, bf16[256,256]{1,0:T(8,128)(2,1)S(1)}, u32[]{:S(2)}, u32[]{:S(2)}) %collective-permute-start.10) | collective-permute-done | bytes 131104 | tf_op jit(solution)/shard_map/ppermute | solution.py:44
  201.8 0.0 all-to-all-done.4
  201.8 0.8 broadcast_in_dim.53
  202.6 3.5 %all-to-all-start.5 = ((bf16[4,256,256]{2,1,0:T(8,128)(2,1)}), bf16[4,256,256]{2,1,0:T(8,128)(2,1)S(1)}, u32[]{:S(2)}, u32[]{:S(2)}) async-start(bf16[4,256,256]{2,1,0:T(8,128)(2,1)} %broadcast_in_dim.53), calls=%async_computation.5 | async-start | bytes 1048576 | tf_op jit(solution)/shard_map/all_to_all | solution.py:48
  206.1 0.0 copy-start
  206.1 0.0 copy-start.1
  206.1 0.2 copy.22
  206.3 2.3 collective-permute-start.3
  208.6 16.6 %collective-permute-done.3 = bf16[128,1024]{0,1:T(8,128)(2,1)S(1)} collective-permute-done((bf16[128,1024]{0,1:T(8,128)(2,1)S(1)}, bf16[128,1024]{0,1:T(8,128)(2,1)S(1)}, u32[]{:S(2)}, u32[]{:S(2)}) %collective-permute-start.3) | collective-permute-done | bytes 262176 | tf_op jit(solution)/shard_map/ppermute | solution.py:205
  225.2 0.8 copy.23
  226.0 0.0 all-to-all-done.5
  226.0 0.0 copy-start.2
  226.0 0.2 fusion
  226.3 0.0 copy-done
  226.3 0.0 copy-done.1
  226.3 1.0 copy-done.2
  227.3 2.1 multiply_subtract_fusion
  (10 shorter events, 0.2 us)
Async XLA Ops:
  2.3 3.4 %collective-permute-start = (bf16[64,256]{1,0:T(8,128)(2,1)S(1)}, bf16[64,256]{1,0:T(8,128)(2,1)S(1)}, u32[]{:S(2)}, u32[]{:S(2)}) collective-permute-start(bf16[64,256]{1,0:T(8,128)(2,1)S(1)} %get-tuple-element.24), channel_id=1, source_target_pairs={{0,1},{1,0},{2,3},{3,2},{4,5},{5,4},{6,7},{7,6},{8,9},{9,8},{10,11... | collective-permute-start | bytes 98312 | tf_op jit(solution)/shard_map/ppermute | solution.py:44
  6.5 13.0 %all-to-all-start = ((bf16[4,64,512]{2,1,0:T(8,128)(2,1)}), bf16[4,64,512]{2,1,0:T(8,128)(2,1)S(1)}, u32[]{:S(2)}, u32[]{:S(2)}) async-start(bf16[4,64,512]{2,1,0:T(8,128)(2,1)} %broadcast_in_dim.50), calls=%async_computation | async-start | bytes 524288 | tf_op jit(solution)/shard_map/all_to_all | solution.py:48
  19.5 27.5 %all-to-all-start.1 = ((bf16[16,16,512]{2,1,0:T(8,128)(2,1)}), bf16[16,16,512]{2,1,0:T(8,128)(2,1)S(1)}, u32[]{:S(2)}, u32[]{:S(2)}) async-start(bf16[16,16,512]{2,1,0:T(8,128)(2,1)} %share.1), calls=%async_computation.1 | async-start | bytes 524288 | tf_op jit(solution)/shard_map/all_to_all | solution.py:48
  34.3 34.5 %collective-permute-start.1 = (bf16[256,256]{1,0:T(8,128)(2,1)S(1)}, bf16[256,256]{1,0:T(8,128)(2,1)S(1)}, u32[]{:S(2)}, u32[]{:S(2)}) collective-permute-start(bf16[256,256]{1,0:T(8,128)(2,1)S(1)} %dynamic-slice_convert_fusion), channel_id=1, source_target_pairs={{0,520},{8,512},{256,776},{264,768},{512,8},{520,0},{768,264},{776... | collective-permute-start | bytes 393224 | tf_op jit(solution)/shard_map/ppermute | solution.py:60
  48.1 26.4 %all-to-all-start.2 = ((bf16[4,256,512]{2,1,0:T(8,128)(2,1)}), bf16[4,256,512]{2,1,0:T(8,128)(2,1)S(1)}, u32[]{:S(2)}, u32[]{:S(2)}) async-start(bf16[4,256,512]{2,1,0:T(8,128)(2,1)} %broadcast_in_dim.52), calls=%async_computation.2 | async-start | bytes 2097152 | tf_op jit(solution)/shard_map/all_to_all | solution.py:48
  69.9 4.6 %collective-permute-start.2 = (bf16[512,256]{1,0:T(8,128)(2,1)S(1)}, bf16[512,256]{1,0:T(8,128)(2,1)S(1)}, u32[]{:S(2)}, u32[]{:S(2)}) collective-permute-start(bf16[512,256]{1,0:T(8,128)(2,1)S(1)} %pad_maximum_fusion.2), channel_id=1, source_target_pairs={{0,1},{1,0},{2,3},{3,2},{4,5},{5,4},{6,7},{7,6},{8,9},{9,8},{10,11... | collective-permute-start | bytes 786440 | tf_op jit(solution)/shard_map/ppermute | solution.py:44
  76.5 34.0 %all-to-all-start.3 = ((bf16[8,256,256]{2,1,0:T(8,128)(2,1)}), bf16[8,256,256]{2,1,0:T(8,128)(2,1)S(1)}, u32[]{:S(2)}, u32[]{:S(2)}) async-start(bf16[8,256,256]{2,1,0:T(8,128)(2,1)} %bitcast.8), calls=%async_computation.3 | async-start | bytes 2097152 | tf_op jit(solution)/shard_map/all_to_all | solution.py:48
  81.2 26.1 %collective-permute-start.6 = (bf16[256,512]{1,0:T(8,128)(2,1)S(1)}, bf16[256,512]{1,0:T(8,128)(2,1)S(1)}, u32[]{:S(2)}, u32[]{:S(2)}) collective-permute-start(bf16[256,512]{1,0:T(8,128)(2,1)S(1)} %bitcast.32), channel_id=1, source_target_pairs={{0,6},{2,4},{4,2},{6,0},{1,7},{3,5},{5,3},{7,1},{8,14},{10,12},{12... | collective-permute-start | bytes 786440 | tf_op jit(solution)/shard_map/ppermute | solution.py:44
  85.7 21.6 %collective-permute-start.5 = (bf16[256,512]{1,0:T(8,128)(2,1)S(1)}, bf16[256,512]{1,0:T(8,128)(2,1)S(1)}, u32[]{:S(2)}, u32[]{:S(2)}) collective-permute-start(bf16[256,512]{1,0:T(8,128)(2,1)S(1)} %bitcast.33), channel_id=1, source_target_pairs={{0,4},{2,6},{4,0},{6,2},{1,5},{3,7},{5,1},{7,3},{8,12},{10,14},{12... | collective-permute-start | bytes 786440 | tf_op jit(solution)/shard_map/ppermute | solution.py:44
  88.1 19.1 %collective-permute-start.4 = (bf16[256,512]{1,0:T(8,128)(2,1)S(1)}, bf16[256,512]{1,0:T(8,128)(2,1)S(1)}, u32[]{:S(2)}, u32[]{:S(2)}) collective-permute-start(bf16[256,512]{1,0:T(8,128)(2,1)S(1)} %bitcast.34), channel_id=1, source_target_pairs={{0,2},{2,0},{4,6},{6,4},{1,3},{3,1},{5,7},{7,5},{8,10},{10,8},{12,... | collective-permute-start | bytes 786440 | tf_op jit(solution)/shard_map/ppermute | solution.py:44
  107.8 9.2 %collective-permute-start.7 = (bf16[512,256]{1,0:T(8,128)(2,1)S(1)}, bf16[512,256]{1,0:T(8,128)(2,1)}, u32[]{:S(2)}, u32[]{:S(2)}) collective-permute-start(bf16[512,256]{1,0:T(8,128)(2,1)S(1)} %shard_map.94), channel_id=1, source_target_pairs={{0,1},{1,0},{2,3},{3,2},{4,5},{5,4},{6,7},{7,6},{8,9},{9,8},{10,11... | collective-permute-start | bytes 786440 | tf_op jit(solution)/shard_map/ppermute | solution.py:44
  113.1 88.7 %all-to-all-start.4 = ((bf16[4,128,256]{2,1,0:T(8,128)(2,1)}), bf16[4,128,256]{2,1,0:T(8,128)(2,1)S(1)}, u32[]{:S(2)}, u32[]{:S(2)}) async-start(bf16[4,128,256]{2,1,0:T(8,128)(2,1)} %bitcast.11), calls=%async_computation.4 | async-start | bytes 524288 | tf_op jit(solution)/shard_map/all_to_all | solution.py:48
  118.0 35.2 %collective-permute-start.8 = (bf16[256,256]{1,0:T(8,128)(2,1)S(1)}, bf16[256,256]{1,0:T(8,128)(2,1)S(1)}, u32[]{:S(2)}, u32[]{:S(2)}) collective-permute-start(bf16[256,256]{1,0:T(8,128)(2,1)S(1)} %slice.43), channel_id=1, source_target_pairs={{0,520},{8,512},{256,776},{264,768},{512,8},{520,0},{768,264},{776... | collective-permute-start | bytes 393224 | tf_op jit(solution)/shard_map/ppermute | solution.py:60
  153.2 17.9 %collective-permute-start.9 = (bf16[256,256]{1,0:T(8,128)(2,1)S(1)}, bf16[256,256]{1,0:T(8,128)(2,1)S(1)}, u32[]{:S(2)}, u32[]{:S(2)}) collective-permute-start(bf16[256,256]{1,0:T(8,128)(2,1)S(1)} %fusion.1), channel_id=1, source_target_pairs={{0,256},{256,0},{512,768},{768,512},{1,257},{257,1},{513,769},{769... | collective-permute-start | bytes 393224 | tf_op jit(solution)/shard_map/ppermute | solution.py:44
  171.2 30.6 %collective-permute-start.10 = (bf16[256,256]{1,0:T(8,128)(2,1)S(1)}, bf16[256,256]{1,0:T(8,128)(2,1)S(1)}, u32[]{:S(2)}, u32[]{:S(2)}) collective-permute-start(bf16[256,256]{1,0:T(8,128)(2,1)S(1)} %add_convert_fusion.1), channel_id=1, source_target_pairs={{0,512},{256,768},{512,0},{768,256},{1,513},{257,769},{513,1},{769... | collective-permute-start | bytes 393224 | tf_op jit(solution)/shard_map/ppermute | solution.py:44
  202.6 23.4 %all-to-all-start.5 = ((bf16[4,256,256]{2,1,0:T(8,128)(2,1)}), bf16[4,256,256]{2,1,0:T(8,128)(2,1)S(1)}, u32[]{:S(2)}, u32[]{:S(2)}) async-start(bf16[4,256,256]{2,1,0:T(8,128)(2,1)} %broadcast_in_dim.53), calls=%async_computation.5 | async-start | bytes 1048576 | tf_op jit(solution)/shard_map/all_to_all | solution.py:48
  206.1 20.2 %copy-start = (f32[1024,256]{1,0:T(8,128)S(1)}, f32[1024,256]{1,0:T(8,128)}, u32[]{:S(2)}) copy-start(f32[1024,256]{1,0:T(8,128)} %param.9) | copy-start | bytes 3145732
  206.1 20.2 %copy-start.1 = (f32[1024,256]{1,0:T(8,128)S(1)}, f32[1024,256]{1,0:T(8,128)}, u32[]{:S(2)}) copy-start(f32[1024,256]{1,0:T(8,128)} %param.10) | copy-start | bytes 3145732
  206.3 18.9 %collective-permute-start.3 = (bf16[128,1024]{0,1:T(8,128)(2,1)S(1)}, bf16[128,1024]{0,1:T(8,128)(2,1)S(1)}, u32[]{:S(2)}, u32[]{:S(2)}) collective-permute-start(bf16[128,1024]{0,1:T(8,128)(2,1)S(1)} %bitcast.42), channel_id=1, source_target_pairs={{0,0},{2,16},{4,32},{6,48},{16,2},{18,18},{20,34},{22,50},{32,4},{... | collective-permute-start | bytes 786440 | tf_op jit(solution)/shard_map/ppermute | solution.py:205
  226.0 1.2 copy-start.2

commit v5 on v4

--- a/solution.py
+++ b/solution.py
@@ -13,7 +13,6 @@
 ROWS = ("y", "h")
 COLS = ("x", "c")
 TOKENS = ("za", "zb", "y", "h")
-NEAR = ("zb", "y")
 
 beta_one = 0.9
 beta_two = 0.95
@@ -65,41 +64,48 @@
     return jnp.where(flip, pair[0], pair[1]), jnp.where(flip, pair[1], pair[0])
 
 
-def masked_grads(value_grads, lengths):
-    tok_rows = value_grads.shape[0]
-    seq_count = lengths.shape[0]
-    seq_len = tok_rows // seq_count
-    index = jnp.arange(tok_rows, dtype=jnp.int32)
-    pick = (index // seq_len)[:, None] == jnp.arange(seq_count, dtype=jnp.int32)[None, :]
-    limit = jnp.sum(jnp.where(pick, lengths[None, :], 0), axis=1)
-    return jnp.where((index % seq_len < limit)[:, None], value_grads, jnp.zeros_like(value_grads))
-
-
-def share_kernel(nzb, where_ref, act_ref, out_ref):
-    near, _, width = out_ref.shape
-    part = width // 2
-    ny = act_ref.shape[1] // (2 * nzb * part)
-    h = where_ref[1]
-    for k in range(near):
-        zb, y = k // ny, k % ny
-        for side, half in enumerate((1 - h, h)):
-            start = ((y * 2 + half) * nzb + zb) * part
-            block = act_ref[:, pl.ds(pl.multiple_of(start, part), part)]
-            out_ref[k, :, side * part : (side + 1) * part] = block
-
-
-def share_of(activations, index, h, nzb, near, share, part):
+def share_kernel(nzb, seq_len, where_ref, lengths_ref, act_ref, own_ref, other_ref, out_ref):
+    _, height, width = out_ref.shape
+    share, half, part = act_ref.shape[0], own_ref.shape[0], width // 2
+    ny = (height - half) // share
+    h, c = where_ref[1], where_ref[2]
+    index = c * half + lax.broadcasted_iota(jnp.int32, (half, part), 0)
+    live = None
+    for k in range(lengths_ref.shape[0]):
+        inside = (index >= k * seq_len) & (index < k * seq_len + lengths_ref[k])
+        live = inside if live is None else live | inside
+    for zb in range(nzb):
+        for y in range(ny):
+            for side, far in enumerate((1 - h, h)):
+                start = ((y * 2 + far) * nzb + zb) * part
+                block = act_ref[:, pl.ds(pl.multiple_of(start, part), part)]
+                out_ref[zb, y * share : (y + 1) * share, side * part : (side + 1) * part] = block
+    for side, ref in enumerate((own_ref, other_ref)):
+        block = ref[...].astype(F32)
+        block = jnp.where(live, block, jnp.zeros_like(block)).astype(out_ref.dtype)
+        for zb in range(nzb):
+            out_ref[zb, ny * share :, side * part : (side + 1) * part] = block
+
+
+def near_pieces(where, lengths, activations, value_grads, other, nzb, ny, share):
+    tok, width = activations.shape
+    half, cols = other.shape
+    shape = (nzb, ny * share + half, 2 * cols)
     return pl.pallas_call(
-        functools.partial(share_kernel, nzb),
-        out_shape=jax.ShapeDtypeStruct((near, share, 2 * part), activations.dtype),
+        functools.partial(share_kernel, nzb, tok // lengths.shape[0]),
+        out_shape=jax.ShapeDtypeStruct(shape, activations.dtype),
         grid_spec=pltpu.PrefetchScalarGridSpec(
-            num_scalar_prefetch=1,
+            num_scalar_prefetch=2,
             grid=(1,),
-            in_specs=[pl.BlockSpec((share, activations.shape[1]), lambda i, where: (where[0], 0))],
-            out_specs=pl.BlockSpec((near, share, 2 * part), lambda i, where: (0, 0, 0)),
+            in_specs=[
+                pl.BlockSpec((share, width), lambda i, where, lengths: (where[0], 0)),
+                pl.BlockSpec((half, cols), lambda i, where, lengths: (where[2], 0)),
+                pl.BlockSpec((half, cols), lambda i, where, lengths: (0, 0)),
+            ],
+            out_specs=pl.BlockSpec(shape, lambda i, where, lengths: (0, 0, 0)),
         ),
         name="share",
-    )(jnp.stack([index, h]).astype(jnp.int32), activations)
+    )(where, lengths, activations, value_grads, other)
 
 
 def outer_kernel(half, x_ref, *refs):
@@ -112,8 +118,8 @@
         start = pl.multiple_of((x_ref[0] ^ k) * share, share)
         grads = [
             grads_ref[y, zb, pl.ds(start, share), half * cols : (half + 1) * cols]
+            for y in range(ny)
             for zb in range(nzb)
-            for y in range(ny)
         ]
         term = lax.dot_general(
             piece[...],
@@ -154,18 +160,19 @@
     h, c, zb = lax.axis_index("h"), lax.axis_index("c"), lax.axis_index("zb")
     x = lax.axis_index("x")
 
-    masked = masked_grads(value_grads, lengths)
-    vg_own, vg_send = own_first((masked[:half], masked[half:]), c)
-    vg_other = swapped(vg_send, "c")
-    vg_half = jnp.concatenate([vg_own, vg_other], axis=1)
-    vg_near = gathered(vg_half, "zb").reshape(nzb * half, 2 * cols)
+    send = lax.dynamic_slice_in_dim(value_grads, (1 - c) * half, half, 0)
+    vg_other = swapped(send, "c")
 
     weight = lax.dynamic_slice_in_dim(master, zb * part, part, 0).astype(BF16)
     weight_far = across(weight)
 
-    mine = share_of(activations, c * nx + x, h, nzb, near, share, part)
-    act_share = exchanged(mine, NEAR)
-    copies = jnp.broadcast_to(vg_near[None], (ny, nzb * half, 2 * cols))
+    where = jnp.stack([c * nx + x, h, c]).astype(jnp.int32)
+    mine = near_pieces(where, lengths, activations, value_grads, vg_other, nzb, ny, share)
+    arrived = exchanged(mine, "zb")
+    mine = arrived[:, : ny * share].reshape(nzb, ny, share, 2 * part).transpose(1, 0, 2, 3)
+    act_share = exchanged(mine.reshape(ny, nzb * share, 2 * part), "y")
+    copies = arrived[:, ny * share :].reshape(nzb * half, 2 * cols)
+    copies = jnp.broadcast_to(copies[None], (ny, nzb * half, 2 * cols))
     copies, act_share = lax.optimization_barrier((copies, act_share))
     grads = exchanged(copies, "y").reshape(ny, nzb, half, 2 * cols)
     act_share = act_share.reshape(near * share, 2 * part)

time: 230 us -> 231 us (level)
  the two profiles are of different devices: /device:TPU:25 before, /device:TPU:24 now
where the time goes in v5:
time: 231 us; the launch traced here: 230 us
  waiting for transfers between devices  117 us (51%)
  starting transfers between devices  92 us (40%)
  local copies, waits for them, and re-layouts  8.7 us (4%)
  other arithmetic  7.06 us (3%)
  Pallas kernels  3.47 us (2%)
    ppermute x8, waiting for transfers between devices, swapped(): return lax.ppermute(array, axis, [(k, k ^ bit) for k in range(size)])  56.7 us
    all_to_all x6, starting transfers between devices, exchanged(): return lax.all_to_all(pieces, axes, split_axis=0, concat_axis=0, tiled=True)  35.9 us
    ppermute x8, starting transfers between devices, swapped(): return lax.ppermute(array, axis, [(k, k ^ bit) for k in range(size)])  28.9 us
    ppermute x2, waiting for transfers between devices, across(): return lax.ppermute(array, ('za', 'h'), pairs)  28.5 us
    ppermute x2, starting transfers between devices, across(): return lax.ppermute(array, ('za', 'h'), pairs)  24.6 us
    ppermute x1, waiting for transfers between devices, step(): input_grads = lax.ppermute(block, ('y', 'x'), turn)  16.5 us
    all_to_all x6, waiting for transfers between devices, exchanged(): return lax.all_to_all(pieces, axes, split_axis=0, concat_axis=0, tiled=True)  14.8 us
  transfers between devices with their start and end apart: 17, of which 9 were waited for; matrix products, arithmetic and copies ran while one was open for 4% of the time, Pallas kernels for 0%

profile of v5, /device:TPU:24, one launch (start us, length us, event | category | flops | bytes accessed | tf_op | source)
XLA Modules:
  0.0 229.7 jit_solution(1139849073170160331)
XLA Ops:
  0.6 0.8 constant_dynamic-slice_fusion
  1.4 1.9 collective-permute-start
  3.3 0.7 pad_add_fusion.where_ref
  4.0 0.5 collective-permute-done.other_ref
  4.5 0.0 copy-start.3
  4.5 0.6 copy-done.3
  5.1 2.5 %share.1 = bf16[4,128,512]{2,1,0:T(8,128)(2,1)} custom-call(s32[3]{0:T(128)} %pad_add_fusion.where_ref, s32[2]{0:T(128)} %lengths_ref.1, bf16[128,8192]{1,0:T(8,128)(2,1)} %act_ref.1, bf16[128,256]{1,0:T(8,128)(2,1)} %own_ref.1, bf16[64,256]{1,0:T(8,128)(2,1)} %copy-done.3), custom_call_target="tpu_custom_call" | custom-call | tf_op jit(solution)/shard_map/share/pallas_call | solution.py:94
  7.6 5.9 %all-to-all-start = ((bf16[4,128,512]{2,1,0:T(8,128)(2,1)}), bf16[4,128,512]{2,1,0:T(8,128)(2,1)S(1)}, u32[]{:S(2)}, u32[]{:S(2)}) async-start(bf16[4,128,512]{2,1,0:T(8,128)(2,1)} %share.1), calls=%async_computation | async-start | bytes 1048576 | tf_op jit(solution)/shard_map/all_to_all | solution.py:47
  13.5 14.8 %all-to-all-done = bf16[4,128,512]{2,1,0:T(8,128)(2,1)S(1)} async-done(((bf16[4,128,512]{2,1,0:T(8,128)(2,1)}), bf16[4,128,512]{2,1,0:T(8,128)(2,1)S(1)}, u32[]{:S(2)}, u32[]{:S(2)}) %all-to-all-start) | async-done | bytes 524320 | tf_op jit(solution)/shard_map/all_to_all | solution.py:47
  28.4 0.7 copy.17
  29.1 14.1 %all-to-all-start.1 = ((bf16[4,64,512]{2,1,0:T(8,128)(2,1)}), bf16[4,64,512]{2,1,0:T(8,128)(2,1)S(1)}, u32[]{:S(2)}, u32[]{:S(2)}) async-start(bf16[4,64,512]{2,1,0:T(8,128)(2,1)} %bitcast.6), calls=%async_computation.1 | async-start | bytes 524288 | tf_op jit(solution)/shard_map/all_to_all | solution.py:47
  43.1 1.0 dynamic-slice_convert_fusion
  44.1 11.5 %collective-permute-start.1 = (bf16[256,256]{1,0:T(8,128)(2,1)S(1)}, bf16[256,256]{1,0:T(8,128)(2,1)S(1)}, u32[]{:S(2)}, u32[]{:S(2)}) collective-permute-start(bf16[256,256]{1,0:T(8,128)(2,1)S(1)} %dynamic-slice_convert_fusion), channel_id=1, source_target_pairs={{0,520},{8,512},{256,776},{264,768},{512,8},{520,0},{768,264},{776... | collective-permute-start | bytes 393224 | tf_op jit(solution)/shard_map/ppermute | solution.py:59
  55.6 0.0 all-to-all-done.1
  55.6 1.1 broadcast_in_dim.14
  56.6 4.8 %all-to-all-start.2 = ((bf16[4,256,512]{2,1,0:T(8,128)(2,1)}), bf16[4,256,512]{2,1,0:T(8,128)(2,1)S(1)}, u32[]{:S(2)}, u32[]{:S(2)}) async-start(bf16[4,256,512]{2,1,0:T(8,128)(2,1)} %broadcast_in_dim.14), calls=%async_computation.2 | async-start | bytes 2097152 | tf_op jit(solution)/shard_map/all_to_all | solution.py:47
  61.4 13.6 %collective-permute-done.1 = bf16[256,256]{1,0:T(8,128)(2,1)S(1)} collective-permute-done((bf16[256,256]{1,0:T(8,128)(2,1)S(1)}, bf16[256,256]{1,0:T(8,128)(2,1)S(1)}, u32[]{:S(2)}, u32[]{:S(2)}) %collective-permute-start.1) | collective-permute-done | bytes 131104 | tf_op jit(solution)/shard_map/ppermute | solution.py:59
  75.1 1.0 broadcast_select_fusion.1
  76.1 1.9 collective-permute-start.2
  78.0 1.5 collective-permute-done.2
  79.5 0.0 all-to-all-done.2
  79.6 0.5 convolution_convert_fusion
  80.0 0.5 convolution_convert_fusion.1
  80.5 1.1 pad_maximum_fusion
  81.6 4.3 %all-to-all-start.3 = ((bf16[8,256,256]{2,1,0:T(8,128)(2,1)}), bf16[8,256,256]{2,1,0:T(8,128)(2,1)S(1)}, u32[]{:S(2)}, u32[]{:S(2)}) async-start(bf16[8,256,256]{2,1,0:T(8,128)(2,1)} %bitcast.12), calls=%async_computation.3 | async-start | bytes 2097152 | tf_op jit(solution)/shard_map/all_to_all | solution.py:47
  85.9 5.1 %collective-permute-start.6 = (bf16[256,512]{1,0:T(8,128)(2,1)S(1)}, bf16[256,512]{1,0:T(8,128)(2,1)S(1)}, u32[]{:S(2)}, u32[]{:S(2)}) collective-permute-start(bf16[256,512]{1,0:T(8,128)(2,1)S(1)} %bitcast.37), channel_id=1, source_target_pairs={{0,6},{2,4},{4,2},{6,0},{1,7},{3,5},{5,3},{7,1},{8,14},{10,12},{12... | collective-permute-start | bytes 786440 | tf_op jit(solution)/shard_map/ppermute | solution.py:43
  91.0 2.8 %collective-permute-start.5 = (bf16[256,512]{1,0:T(8,128)(2,1)S(1)}, bf16[256,512]{1,0:T(8,128)(2,1)S(1)}, u32[]{:S(2)}, u32[]{:S(2)}) collective-permute-start(bf16[256,512]{1,0:T(8,128)(2,1)S(1)} %bitcast.38), channel_id=1, source_target_pairs={{0,4},{2,6},{4,0},{6,2},{1,5},{3,7},{5,1},{7,3},{8,12},{10,14},{12... | collective-permute-start | bytes 786440 | tf_op jit(solution)/shard_map/ppermute | solution.py:43
  93.8 1.9 collective-permute-start.4
  95.7 17.0 %collective-permute-done.6.refs_3_ = bf16[256,512]{1,0:T(8,128)(2,1)S(1)} collective-permute-done((bf16[256,512]{1,0:T(8,128)(2,1)S(1)}, bf16[256,512]{1,0:T(8,128)(2,1)S(1)}, u32[]{:S(2)}, u32[]{:S(2)}) %collective-permute-start.6) | collective-permute-done | bytes 262176 | tf_op jit(solution)/shard_map/ppermute | solution.py:43
  112.7 0.0 collective-permute-done.5.refs_2_
  112.7 0.0 collective-permute-done.4.refs_1_
  112.7 0.5 shard_map.94
  113.2 1.9 collective-permute-start.7
  115.2 0.0 all-to-all-done.3
  115.2 0.9 reduce_sum.12
  116.1 1.7 copy.20
  117.8 3.4 %all-to-all-start.4 = ((bf16[4,128,256]{2,1,0:T(8,128)(2,1)}), bf16[4,128,256]{2,1,0:T(8,128)(2,1)S(1)}, u32[]{:S(2)}, u32[]{:S(2)}) async-start(bf16[4,128,256]{2,1,0:T(8,128)(2,1)} %bitcast.15), calls=%async_computation.4 | async-start | bytes 524288 | tf_op jit(solution)/shard_map/all_to_all | solution.py:47
  121.2 0.5 shard_map.93
  121.7 0.0 collective-permute-done.7
  121.7 1.0 convert_add_fusion
  122.7 13.1 %collective-permute-start.8 = (bf16[256,256]{1,0:T(8,128)(2,1)S(1)}, bf16[256,256]{1,0:T(8,128)(2,1)S(1)}, u32[]{:S(2)}, u32[]{:S(2)}) collective-permute-start(bf16[256,256]{1,0:T(8,128)(2,1)S(1)} %slice.39), channel_id=1, source_target_pairs={{0,520},{8,512},{256,776},{264,768},{512,8},{520,0},{768,264},{776... | collective-permute-start | bytes 393224 | tf_op jit(solution)/shard_map/ppermute | solution.py:59
  135.8 14.8 %collective-permute-done.8 = bf16[256,256]{1,0:T(8,128)(2,1)S(1)} collective-permute-done((bf16[256,256]{1,0:T(8,128)(2,1)S(1)}, bf16[256,256]{1,0:T(8,128)(2,1)S(1)}, u32[]{:S(2)}, u32[]{:S(2)}) %collective-permute-start.8) | collective-permute-done | bytes 131104 | tf_op jit(solution)/shard_map/ppermute | solution.py:59
  150.7 1.9 collective-permute-start.9
  152.6 17.7 %collective-permute-done.9 = bf16[256,256]{1,0:T(8,128)(2,1)S(1)} collective-permute-done((bf16[256,256]{1,0:T(8,128)(2,1)S(1)}, bf16[256,256]{1,0:T(8,128)(2,1)S(1)}, u32[]{:S(2)}, u32[]{:S(2)}) %collective-permute-start.9) | collective-permute-done | bytes 131104 | tf_op jit(solution)/shard_map/ppermute | solution.py:43
  170.4 11.4 %collective-permute-start.10 = (bf16[256,256]{1,0:T(8,128)(2,1)S(1)}, bf16[256,256]{1,0:T(8,128)(2,1)S(1)}, u32[]{:S(2)}, u32[]{:S(2)}) collective-permute-start(bf16[256,256]{1,0:T(8,128)(2,1)S(1)} %add_convert_fusion.1), channel_id=1, source_target_pairs={{0,512},{256,768},{512,0},{768,256},{1,513},{257,769},{513,1},{769... | collective-permute-start | bytes 393224 | tf_op jit(solution)/shard_map/ppermute | solution.py:43
  181.8 19.9 %collective-permute-done.10 = bf16[256,256]{1,0:T(8,128)(2,1)S(1)} collective-permute-done((bf16[256,256]{1,0:T(8,128)(2,1)S(1)}, bf16[256,256]{1,0:T(8,128)(2,1)S(1)}, u32[]{:S(2)}, u32[]{:S(2)}) %collective-permute-start.10) | collective-permute-done | bytes 131104 | tf_op jit(solution)/shard_map/ppermute | solution.py:43
  201.8 0.0 all-to-all-done.4
  201.8 0.8 broadcast_in_dim.15
  202.6 3.5 %all-to-all-start.5 = ((bf16[4,256,256]{2,1,0:T(8,128)(2,1)}), bf16[4,256,256]{2,1,0:T(8,128)(2,1)S(1)}, u32[]{:S(2)}, u32[]{:S(2)}) async-start(bf16[4,256,256]{2,1,0:T(8,128)(2,1)} %broadcast_in_dim.15), calls=%async_computation.5 | async-start | bytes 1048576 | tf_op jit(solution)/shard_map/all_to_all | solution.py:47
  206.1 0.0 copy-start
  206.1 0.0 copy-start.1
  206.1 0.2 copy.21
  206.3 2.7 %collective-permute-start.3 = (bf16[128,1024]{0,1:T(8,128)(2,1)S(1)}, bf16[128,1024]{0,1:T(8,128)(2,1)S(1)}, u32[]{:S(2)}, u32[]{:S(2)}) collective-permute-start(bf16[128,1024]{0,1:T(8,128)(2,1)S(1)} %bitcast.48), channel_id=1, source_target_pairs={{0,0},{2,16},{4,32},{6,48},{16,2},{18,18},{20,34},{22,50},{32,4},{... | collective-permute-start | bytes 786440 | tf_op jit(solution)/shard_map/ppermute | solution.py:212
  209.0 16.5 %collective-permute-done.3 = bf16[128,1024]{0,1:T(8,128)(2,1)S(1)} collective-permute-done((bf16[128,1024]{0,1:T(8,128)(2,1)S(1)}, bf16[128,1024]{0,1:T(8,128)(2,1)S(1)}, u32[]{:S(2)}, u32[]{:S(2)}) %collective-permute-start.3) | collective-permute-done | bytes 262176 | tf_op jit(solution)/shard_map/ppermute | solution.py:212
  225.5 0.8 copy.22
  226.4 0.0 all-to-all-done.5
  226.4 0.0 copy-start.2
  226.4 0.2 fusion
  226.6 0.0 copy-done
  226.6 0.0 copy-done.1
  226.6 1.0 copy-done.2
  227.6 2.1 multiply_subtract_fusion
  (7 shorter events, 0.2 us)
Async XLA Ops:
  1.4 3.1 %collective-permute-start = (bf16[64,256]{1,0:T(8,128)(2,1)S(1)}, bf16[64,256]{1,0:T(8,128)(2,1)S(1)}, u32[]{:S(2)}, u32[]{:S(2)}) collective-permute-start(bf16[64,256]{1,0:T(8,128)(2,1)S(1)} %constant_dynamic-slice_fusion), channel_id=1, source_target_pairs={{0,1},{1,0},{2,3},{3,2},{4,5},{5,4},{6,7},{7,6},{8,9},{9,8},{10,11... | collective-permute-start | bytes 98312 | tf_op jit(solution)/shard_map/ppermute | solution.py:43
  4.5 0.6 copy-start.3
  7.6 20.7 %all-to-all-start = ((bf16[4,128,512]{2,1,0:T(8,128)(2,1)}), bf16[4,128,512]{2,1,0:T(8,128)(2,1)S(1)}, u32[]{:S(2)}, u32[]{:S(2)}) async-start(bf16[4,128,512]{2,1,0:T(8,128)(2,1)} %share.1), calls=%async_computation | async-start | bytes 1048576 | tf_op jit(solution)/shard_map/all_to_all | solution.py:47
  29.1 26.5 %all-to-all-start.1 = ((bf16[4,64,512]{2,1,0:T(8,128)(2,1)}), bf16[4,64,512]{2,1,0:T(8,128)(2,1)S(1)}, u32[]{:S(2)}, u32[]{:S(2)}) async-start(bf16[4,64,512]{2,1,0:T(8,128)(2,1)} %bitcast.6), calls=%async_computation.1 | async-start | bytes 524288 | tf_op jit(solution)/shard_map/all_to_all | solution.py:47
  44.1 31.0 %collective-permute-start.1 = (bf16[256,256]{1,0:T(8,128)(2,1)S(1)}, bf16[256,256]{1,0:T(8,128)(2,1)S(1)}, u32[]{:S(2)}, u32[]{:S(2)}) collective-permute-start(bf16[256,256]{1,0:T(8,128)(2,1)S(1)} %dynamic-slice_convert_fusion), channel_id=1, source_target_pairs={{0,520},{8,512},{256,776},{264,768},{512,8},{520,0},{768,264},{776... | collective-permute-start | bytes 393224 | tf_op jit(solution)/shard_map/ppermute | solution.py:59
  56.6 22.9 %all-to-all-start.2 = ((bf16[4,256,512]{2,1,0:T(8,128)(2,1)}), bf16[4,256,512]{2,1,0:T(8,128)(2,1)S(1)}, u32[]{:S(2)}, u32[]{:S(2)}) async-start(bf16[4,256,512]{2,1,0:T(8,128)(2,1)} %broadcast_in_dim.14), calls=%async_computation.2 | async-start | bytes 2097152 | tf_op jit(solution)/shard_map/all_to_all | solution.py:47
  76.1 3.4 %collective-permute-start.2 = (bf16[512,256]{1,0:T(8,128)(2,1)S(1)}, bf16[512,256]{1,0:T(8,128)(2,1)S(1)}, u32[]{:S(2)}, u32[]{:S(2)}) collective-permute-start(bf16[512,256]{1,0:T(8,128)(2,1)S(1)} %pad_maximum_fusion.2), channel_id=1, source_target_pairs={{0,1},{1,0},{2,3},{3,2},{4,5},{5,4},{6,7},{7,6},{8,9},{9,8},{10,11... | collective-permute-start | bytes 786440 | tf_op jit(solution)/shard_map/ppermute | solution.py:43
  81.6 33.6 %all-to-all-start.3 = ((bf16[8,256,256]{2,1,0:T(8,128)(2,1)}), bf16[8,256,256]{2,1,0:T(8,128)(2,1)S(1)}, u32[]{:S(2)}, u32[]{:S(2)}) async-start(bf16[8,256,256]{2,1,0:T(8,128)(2,1)} %bitcast.12), calls=%async_computation.3 | async-start | bytes 2097152 | tf_op jit(solution)/shard_map/all_to_all | solution.py:47
  85.9 26.9 %collective-permute-start.6 = (bf16[256,512]{1,0:T(8,128)(2,1)S(1)}, bf16[256,512]{1,0:T(8,128)(2,1)S(1)}, u32[]{:S(2)}, u32[]{:S(2)}) collective-permute-start(bf16[256,512]{1,0:T(8,128)(2,1)S(1)} %bitcast.37), channel_id=1, source_target_pairs={{0,6},{2,4},{4,2},{6,0},{1,7},{3,5},{5,3},{7,1},{8,14},{10,12},{12... | collective-permute-start | bytes 786440 | tf_op jit(solution)/shard_map/ppermute | solution.py:43
  91.0 21.7 %collective-permute-start.5 = (bf16[256,512]{1,0:T(8,128)(2,1)S(1)}, bf16[256,512]{1,0:T(8,128)(2,1)S(1)}, u32[]{:S(2)}, u32[]{:S(2)}) collective-permute-start(bf16[256,512]{1,0:T(8,128)(2,1)S(1)} %bitcast.38), channel_id=1, source_target_pairs={{0,4},{2,6},{4,0},{6,2},{1,5},{3,7},{5,1},{7,3},{8,12},{10,14},{12... | collective-permute-start | bytes 786440 | tf_op jit(solution)/shard_map/ppermute | solution.py:43
  93.8 19.0 %collective-permute-start.4 = (bf16[256,512]{1,0:T(8,128)(2,1)S(1)}, bf16[256,512]{1,0:T(8,128)(2,1)S(1)}, u32[]{:S(2)}, u32[]{:S(2)}) collective-permute-start(bf16[256,512]{1,0:T(8,128)(2,1)S(1)} %bitcast.39), channel_id=1, source_target_pairs={{0,2},{2,0},{4,6},{6,4},{1,3},{3,1},{5,7},{7,5},{8,10},{10,8},{12,... | collective-permute-start | bytes 786440 | tf_op jit(solution)/shard_map/ppermute | solution.py:43
  113.2 8.4 %collective-permute-start.7 = (bf16[512,256]{1,0:T(8,128)(2,1)S(1)}, bf16[512,256]{1,0:T(8,128)(2,1)}, u32[]{:S(2)}, u32[]{:S(2)}) collective-permute-start(bf16[512,256]{1,0:T(8,128)(2,1)S(1)} %shard_map.94), channel_id=1, source_target_pairs={{0,1},{1,0},{2,3},{3,2},{4,5},{5,4},{6,7},{7,6},{8,9},{9,8},{10,11... | collective-permute-start | bytes 786440 | tf_op jit(solution)/shard_map/ppermute | solution.py:43
  117.8 84.0 %all-to-all-start.4 = ((bf16[4,128,256]{2,1,0:T(8,128)(2,1)}), bf16[4,128,256]{2,1,0:T(8,128)(2,1)S(1)}, u32[]{:S(2)}, u32[]{:S(2)}) async-start(bf16[4,128,256]{2,1,0:T(8,128)(2,1)} %bitcast.15), calls=%async_computation.4 | async-start | bytes 524288 | tf_op jit(solution)/shard_map/all_to_all | solution.py:47
  122.7 27.9 %collective-permute-start.8 = (bf16[256,256]{1,0:T(8,128)(2,1)S(1)}, bf16[256,256]{1,0:T(8,128)(2,1)S(1)}, u32[]{:S(2)}, u32[]{:S(2)}) collective-permute-start(bf16[256,256]{1,0:T(8,128)(2,1)S(1)} %slice.39), channel_id=1, source_target_pairs={{0,520},{8,512},{256,776},{264,768},{512,8},{520,0},{768,264},{776... | collective-permute-start | bytes 393224 | tf_op jit(solution)/shard_map/ppermute | solution.py:59
  150.7 19.7 %collective-permute-start.9 = (bf16[256,256]{1,0:T(8,128)(2,1)S(1)}, bf16[256,256]{1,0:T(8,128)(2,1)S(1)}, u32[]{:S(2)}, u32[]{:S(2)}) collective-permute-start(bf16[256,256]{1,0:T(8,128)(2,1)S(1)} %fusion.1), channel_id=1, source_target_pairs={{0,256},{256,0},{512,768},{768,512},{1,257},{257,1},{513,769},{769... | collective-permute-start | bytes 393224 | tf_op jit(solution)/shard_map/ppermute | solution.py:43
  170.4 31.4 %collective-permute-start.10 = (bf16[256,256]{1,0:T(8,128)(2,1)S(1)}, bf16[256,256]{1,0:T(8,128)(2,1)S(1)}, u32[]{:S(2)}, u32[]{:S(2)}) collective-permute-start(bf16[256,256]{1,0:T(8,128)(2,1)S(1)} %add_convert_fusion.1), channel_id=1, source_target_pairs={{0,512},{256,768},{512,0},{768,256},{1,513},{257,769},{513,1},{769... | collective-permute-start | bytes 393224 | tf_op jit(solution)/shard_map/ppermute | solution.py:43
  202.6 23.7 %all-to-all-start.5 = ((bf16[4,256,256]{2,1,0:T(8,128)(2,1)}), bf16[4,256,256]{2,1,0:T(8,128)(2,1)S(1)}, u32[]{:S(2)}, u32[]{:S(2)}) async-start(bf16[4,256,256]{2,1,0:T(8,128)(2,1)} %broadcast_in_dim.15), calls=%async_computation.5 | async-start | bytes 1048576 | tf_op jit(solution)/shard_map/all_to_all | solution.py:47
  206.1 20.5 %copy-start = (f32[1024,256]{1,0:T(8,128)S(1)}, f32[1024,256]{1,0:T(8,128)}, u32[]{:S(2)}) copy-start(f32[1024,256]{1,0:T(8,128)} %param.9) | copy-start | bytes 3145732
  206.1 20.5 %copy-start.1 = (f32[1024,256]{1,0:T(8,128)S(1)}, f32[1024,256]{1,0:T(8,128)}, u32[]{:S(2)}) copy-start(f32[1024,256]{1,0:T(8,128)} %param.10) | copy-start | bytes 3145732
  206.3 19.2 %collective-permute-start.3 = (bf16[128,1024]{0,1:T(8,128)(2,1)S(1)}, bf16[128,1024]{0,1:T(8,128)(2,1)S(1)}, u32[]{:S(2)}, u32[]{:S(2)}) collective-permute-start(bf16[128,1024]{0,1:T(8,128)(2,1)S(1)} %bitcast.48), channel_id=1, source_target_pairs={{0,0},{2,16},{4,32},{6,48},{16,2},{18,18},{20,34},{22,50},{32,4},{... | collective-permute-start | bytes 786440 | tf_op jit(solution)/shard_map/ppermute | solution.py:212
  226.4 1.2 copy-start.2

commit v6 on v5

--- a/solution.py
+++ b/solution.py
@@ -13,6 +13,7 @@
 ROWS = ("y", "h")
 COLS = ("x", "c")
 TOKENS = ("za", "zb", "y", "h")
+NEAR = ("zb", "y")
 
 beta_one = 0.9
 beta_two = 0.95
@@ -64,36 +65,39 @@
     return jnp.where(flip, pair[0], pair[1]), jnp.where(flip, pair[1], pair[0])
 
 
-def share_kernel(nzb, seq_len, where_ref, lengths_ref, act_ref, own_ref, other_ref, out_ref):
-    _, height, width = out_ref.shape
-    share, half, part = act_ref.shape[0], own_ref.shape[0], width // 2
-    ny = (height - half) // share
+def share_kernel(
+    nzb, seq_len, where_ref, lengths_ref, act_ref, own_ref, other_ref, mine_ref, copies_ref
+):
+    near, _, width = mine_ref.shape
+    half, part = own_ref.shape[0], width // 2
+    cols = own_ref.shape[1]
+    ny = near // nzb
     h, c = where_ref[1], where_ref[2]
-    index = c * half + lax.broadcasted_iota(jnp.int32, (half, part), 0)
+    for k in range(near):
+        zb, y = k // ny, k % ny
+        for side, far in enumerate((1 - h, h)):
+            start = ((y * 2 + far) * nzb + zb) * part
+            block = act_ref[:, pl.ds(pl.multiple_of(start, part), part)]
+            mine_ref[k, :, side * part : (side + 1) * part] = block
+    index = c * half + lax.broadcasted_iota(jnp.int32, (half, cols), 0)
     live = None
     for k in range(lengths_ref.shape[0]):
         inside = (index >= k * seq_len) & (index < k * seq_len + lengths_ref[k])
         live = inside if live is None else live | inside
-    for zb in range(nzb):
-        for y in range(ny):
-            for side, far in enumerate((1 - h, h)):
-                start = ((y * 2 + far) * nzb + zb) * part
-                block = act_ref[:, pl.ds(pl.multiple_of(start, part), part)]
-                out_ref[zb, y * share : (y + 1) * share, side * part : (side + 1) * part] = block
     for side, ref in enumerate((own_ref, other_ref)):
         block = ref[...].astype(F32)
-        block = jnp.where(live, block, jnp.zeros_like(block)).astype(out_ref.dtype)
-        for zb in range(nzb):
-            out_ref[zb, ny * share :, side * part : (side + 1) * part] = block
-
-
-def near_pieces(where, lengths, activations, value_grads, other, nzb, ny, share):
+        block = jnp.where(live, block, jnp.zeros_like(block)).astype(copies_ref.dtype)
+        for k in range(near):
+            copies_ref[k, :, side * cols : (side + 1) * cols] = block
+
+
+def near_pieces(where, lengths, activations, value_grads, other, nzb, ny, share, part):
     tok, width = activations.shape
     half, cols = other.shape
-    shape = (nzb, ny * share + half, 2 * cols)
+    shapes = ((nzb * ny, share, 2 * part), (nzb * ny, half, 2 * cols))
     return pl.pallas_call(
         functools.partial(share_kernel, nzb, tok // lengths.shape[0]),
-        out_shape=jax.ShapeDtypeStruct(shape, activations.dtype),
+        out_shape=[jax.ShapeDtypeStruct(shape, activations.dtype) for shape in shapes],
         grid_spec=pltpu.PrefetchScalarGridSpec(
             num_scalar_prefetch=2,
             grid=(1,),
@@ -102,7 +106,7 @@
                 pl.BlockSpec((half, cols), lambda i, where, lengths: (where[2], 0)),
                 pl.BlockSpec((half, cols), lambda i, where, lengths: (0, 0)),
             ],
-            out_specs=pl.BlockSpec(shape, lambda i, where, lengths: (0, 0, 0)),
+            out_specs=[pl.BlockSpec(shape, lambda i, where, lengths: (0, 0, 0)) for shape in shapes],
         ),
         name="share",
     )(where, lengths, activations, value_grads, other)
@@ -110,20 +114,16 @@
 
 def outer_kernel(half, x_ref, *refs):
     *pieces, grads_ref, out_ref = refs
-    ny, nzb, tok, _ = grads_ref.shape
+    near, tok, _ = grads_ref.shape
     share = tok // len(pieces)
     cols = out_ref.shape[1]
     total = None
     for k, piece in enumerate(pieces):
         start = pl.multiple_of((x_ref[0] ^ k) * share, share)
-        grads = [
-            grads_ref[y, zb, pl.ds(start, share), half * cols : (half + 1) * cols]
-            for y in range(ny)
-            for zb in range(nzb)
-        ]
+        grads = grads_ref[:, pl.ds(start, share), half * cols : (half + 1) * cols]
         term = lax.dot_general(
             piece[...],
-            jnp.concatenate(grads, axis=0),
+            grads.reshape(near * share, cols),
             (((0,), (0,)), ((), ())),
             preferred_element_type=F32,
         )
@@ -132,7 +132,7 @@
 
 
 def outer(x, pieces, grads, half, dtype):
-    rows, cols = pieces[0].shape[1], grads.shape[3] // 2
+    rows, cols = pieces[0].shape[1], grads.shape[2] // 2
     vmem = pl.BlockSpec(memory_space=pltpu.VMEM)
     depth = sum(piece.shape[0] for piece in pieces)
     return pl.pallas_call(
@@ -167,14 +167,12 @@
     weight_far = across(weight)
 
     where = jnp.stack([c * nx + x, h, c]).astype(jnp.int32)
-    mine = near_pieces(where, lengths, activations, value_grads, vg_other, nzb, ny, share)
-    arrived = exchanged(mine, "zb")
-    mine = arrived[:, : ny * share].reshape(nzb, ny, share, 2 * part).transpose(1, 0, 2, 3)
-    act_share = exchanged(mine.reshape(ny, nzb * share, 2 * part), "y")
-    copies = arrived[:, ny * share :].reshape(nzb * half, 2 * cols)
-    copies = jnp.broadcast_to(copies[None], (ny, nzb * half, 2 * cols))
+    mine, copies = near_pieces(
+        where, lengths, activations, value_grads, vg_other, nzb, ny, share, part
+    )
+    act_share = exchanged(mine, NEAR)
     copies, act_share = lax.optimization_barrier((copies, act_share))
-    grads = exchanged(copies, "y").reshape(ny, nzb, half, 2 * cols)
+    grads = exchanged(copies, NEAR)
     act_share = act_share.reshape(near * share, 2 * part)
     pieces = [act_share]
     for k in range(1, nx):
@@ -200,7 +198,7 @@
 
     def product(w):
         out = lax.dot_general(tokens, w, (((1,), (1,)), ((), ())), preferred_element_type=F32)
-        return out.astype(BF16).reshape(ny, nzb, half, part)
+        return out.astype(BF16).reshape(nzb, ny, half, part).transpose(1, 0, 2, 3)
 
     product = jnp.stack([product(both[:part]), product(both[part:])], axis=1)
     arrived = exchanged(product.reshape(ny * 2, nzb * half, part), COLS)
@@ -228,4 +226,6 @@
         P(ROWS, COLS),
     )
     out_specs = (P(TOKENS, COLS), P(ROWS, COLS), P(ROWS, COLS), P(ROWS, COLS))
-    return jax.shard_map(step, mesh=split, in_specs=in_specs, out_specs=out_specs, check_vma=False)
+    return jax.shard_map(
+        step, mesh=split, in_specs=in_specs, out_specs=out_specs, check_vma=False
+    )

time: 231 us -> 240 us (1.039)
  blocking collectives: 0 us -> 25.1 us
  starting transfers between devices: 92 us -> 81 us
  waiting for transfers between devices: 117 us -> 113 us
    all_to_all x0 -> x1, blocking collectives: none -> 25.1 us  [exchanged(): return lax.all_to_all(pieces, axes, split_axis=0, concat_axis=0, tiled=True)]
    all_to_all x6 -> x4, starting transfers between devices: 35.9 us -> 22.8 us  [exchanged(): return lax.all_to_all(pieces, axes, split_axis=0, concat_axis=0, tiled=True)]
    all_to_all x6 -> x4, waiting for transfers between devices: 14.8 us -> 2.65 us  [exchanged(): return lax.all_to_all(pieces, axes, split_axis=0, concat_axis=0, tiled=True)]
    ppermute x2, waiting for transfers between devices: 28.5 us -> 39.6 us  [across(): return lax.ppermute(array, ('za', 'h'), pairs)]
  transfers between devices with their start and end apart: 17 -> 15, of which waited for: 9 -> 9; matrix products, arithmetic and copies ran while one was open for 4% -> 3% of each run, Pallas kernels for 0% -> 0%
where the time goes in v6:
time: 240 us; the launch traced here: 239 us
  waiting for transfers between devices  113 us (47%)
  starting transfers between devices  81 us (34%)
  blocking collectives  25.1 us (10%)
  other arithmetic  7.06 us (3%)
  local copies, waits for them, and re-layouts  6.99 us (3%)
  Pallas kernels  3.73 us (2%)
    ppermute x8, waiting for transfers between devices, swapped(): return lax.ppermute(array, axis, [(k, k ^ bit) for k in range(size)])  54.5 us
    ppermute x2, waiting for transfers between devices, across(): return lax.ppermute(array, ('za', 'h'), pairs)  39.6 us
    ppermute x8, starting transfers between devices, swapped(): return lax.ppermute(array, axis, [(k, k ^ bit) for k in range(size)])  29.5 us
    ppermute x2, starting transfers between devices, across(): return lax.ppermute(array, ('za', 'h'), pairs)  25.8 us
    all_to_all x1, blocking collectives, exchanged(): return lax.all_to_all(pieces, axes, split_axis=0, concat_axis=0, tiled=True)  25.1 us
    all_to_all x4, starting transfers between devices, exchanged(): return lax.all_to_all(pieces, axes, split_axis=0, concat_axis=0, tiled=True)  22.8 us
    ppermute x1, waiting for transfers between devices, step(): input_grads = lax.ppermute(block, ('y', 'x'), turn)  16.3 us
  transfers between devices with their start and end apart: 15, of which 9 were waited for; matrix products, arithmetic and copies ran while one was open for 3% of the time, Pallas kernels for 0%

profile of v6, /device:TPU:24, one launch (start us, length us, event | category | flops | bytes accessed | tf_op | source)
XLA Modules:
  0.0 238.8 jit_solution(16178853237478749225)
XLA Ops:
  0.6 0.8 constant_dynamic-slice_fusion
  1.4 1.9 collective-permute-start
  3.3 0.7 pad_add_fusion.where_ref
  4.0 0.5 collective-permute-done.other_ref
  4.5 0.0 copy-start.3
  4.5 0.6 copy-done.3
  5.1 2.8 %share.1 = (bf16[16,16,512]{2,1,0:T(8,128)(2,1)}, bf16[16,64,512]{2,1,0:T(8,128)(2,1)}) custom-call(s32[3]{0:T(128)} %pad_add_fusion.where_ref, s32[2]{0:T(128)} %lengths_ref.1, bf16[128,8192]{1,0:T(8,128)(2,1)} %act_ref.1, bf16[128,256]{1,0:T(8,128)(2,1)} %own_ref.1, bf16[64,256]{1,0:T(8,128)(2,1)} %copy-done.3), custom_call_target="tpu_custom_call" | custom-call | tf_op jit(solution)/shard_map/share/pallas_call | solution.py:98
  7.9 25.1 %all_to_all.25 = bf16[16,16,512]{2,1,0:T(8,128)(2,1)S(1)} all-to-all(bf16[16,16,512]{2,1,0:T(8,128)(2,1)} %get-tuple-element.9), channel_id=1, replica_groups=mesh['za'=4,'zb'=4,'y'=4,'h'=2,'x'=4,'c'=2] {'zb','y'}, dimensions={0} | all-to-all | bytes 524288 | tf_op jit(solution)/shard_map/all_to_all | solution.py:48
  32.9 6.2 %all-to-all-start.1 = ((bf16[16,64,512]{2,1,0:T(8,128)(2,1)}), bf16[16,64,512]{2,1,0:T(8,128)(2,1)S(1)}, u32[]{:S(2)}, u32[]{:S(2)}) async-start(bf16[16,64,512]{2,1,0:T(8,128)(2,1)} %get-tuple-element.10), calls=%async_computation.1 | async-start | bytes 2097152 | tf_op jit(solution)/shard_map/all_to_all | solution.py:48
  39.1 1.0 dynamic-slice_convert_fusion
  40.1 12.6 %collective-permute-start.1 = (bf16[256,256]{1,0:T(8,128)(2,1)S(1)}, bf16[256,256]{1,0:T(8,128)(2,1)S(1)}, u32[]{:S(2)}, u32[]{:S(2)}) collective-permute-start(bf16[256,256]{1,0:T(8,128)(2,1)S(1)} %dynamic-slice_convert_fusion), channel_id=1, source_target_pairs={{0,520},{8,512},{256,776},{264,768},{512,8},{520,0},{768,264},{776... | collective-permute-start | bytes 393224 | tf_op jit(solution)/shard_map/ppermute | solution.py:60
  52.7 16.9 %collective-permute-done.1 = bf16[256,256]{1,0:T(8,128)(2,1)S(1)} collective-permute-done((bf16[256,256]{1,0:T(8,128)(2,1)S(1)}, bf16[256,256]{1,0:T(8,128)(2,1)S(1)}, u32[]{:S(2)}, u32[]{:S(2)}) %collective-permute-start.1) | collective-permute-done | bytes 131104 | tf_op jit(solution)/shard_map/ppermute | solution.py:60
  69.6 1.0 broadcast_select_fusion.1
  70.6 1.9 collective-permute-start.2
  72.5 1.5 collective-permute-done.2
  74.0 2.6 %all-to-all-done.1.refs_4_ = bf16[16,64,512]{2,1,0:T(8,128)(2,1)S(1)} async-done(((bf16[16,64,512]{2,1,0:T(8,128)(2,1)}), bf16[16,64,512]{2,1,0:T(8,128)(2,1)S(1)}, u32[]{:S(2)}, u32[]{:S(2)}) %all-to-all-start.1) | async-done | bytes 1048608 | tf_op jit(solution)/shard_map/all_to_all | solution.py:48
  76.7 0.5 convolution_convert_fusion
  77.2 0.5 convolution_convert_fusion.1
  77.6 0.1 copy_bitcast_fusion
  77.7 1.1 pad_maximum_fusion
  78.8 6.5 %all-to-all-start.2 = ((bf16[8,256,256]{2,1,0:T(8,128)(2,1)}), bf16[8,256,256]{2,1,0:T(8,128)(2,1)S(1)}, u32[]{:S(2)}, u32[]{:S(2)}) async-start(bf16[8,256,256]{2,1,0:T(8,128)(2,1)} %bitcast.10), calls=%async_computation.2 | async-start | bytes 2097152 | tf_op jit(solution)/shard_map/all_to_all | solution.py:48
  85.3 5.1 %collective-permute-start.6 = (bf16[256,512]{1,0:T(8,128)(2,1)S(1)}, bf16[256,512]{1,0:T(8,128)(2,1)S(1)}, u32[]{:S(2)}, u32[]{:S(2)}) collective-permute-start(bf16[256,512]{1,0:T(8,128)(2,1)S(1)} %bitcast.33), channel_id=1, source_target_pairs={{0,6},{2,4},{4,2},{6,0},{1,7},{3,5},{5,3},{7,1},{8,14},{10,12},{12... | collective-permute-start | bytes 786440 | tf_op jit(solution)/shard_map/ppermute | solution.py:44
  90.4 2.8 %collective-permute-start.5 = (bf16[256,512]{1,0:T(8,128)(2,1)S(1)}, bf16[256,512]{1,0:T(8,128)(2,1)S(1)}, u32[]{:S(2)}, u32[]{:S(2)}) collective-permute-start(bf16[256,512]{1,0:T(8,128)(2,1)S(1)} %bitcast.34), channel_id=1, source_target_pairs={{0,4},{2,6},{4,0},{6,2},{1,5},{3,7},{5,1},{7,3},{8,12},{10,14},{12... | collective-permute-start | bytes 786440 | tf_op jit(solution)/shard_map/ppermute | solution.py:44
  93.2 1.9 collective-permute-start.4
  95.1 17.0 %collective-permute-done.6.refs_3_ = bf16[256,512]{1,0:T(8,128)(2,1)S(1)} collective-permute-done((bf16[256,512]{1,0:T(8,128)(2,1)S(1)}, bf16[256,512]{1,0:T(8,128)(2,1)S(1)}, u32[]{:S(2)}, u32[]{:S(2)}) %collective-permute-start.6) | collective-permute-done | bytes 262176 | tf_op jit(solution)/shard_map/ppermute | solution.py:44
  112.2 0.0 collective-permute-done.5.refs_2_
  112.2 0.0 collective-permute-done.4.refs_1_
  112.2 0.5 shard_map.94
  112.7 1.9 collective-permute-start.7
  114.6 0.0 all-to-all-done.2
  114.6 0.9 reduce_sum.12
  115.5 1.7 copy.16
  117.2 6.7 %all-to-all-start.3 = ((bf16[4,128,256]{2,1,0:T(8,128)(2,1)}), bf16[4,128,256]{2,1,0:T(8,128)(2,1)S(1)}, u32[]{:S(2)}, u32[]{:S(2)}) async-start(bf16[4,128,256]{2,1,0:T(8,128)(2,1)} %bitcast.13), calls=%async_computation.3 | async-start | bytes 524288 | tf_op jit(solution)/shard_map/all_to_all | solution.py:48
  123.9 0.5 shard_map.93
  124.3 0.0 collective-permute-done.7
  124.4 1.0 convert_add_fusion
  125.4 13.2 %collective-permute-start.8 = (bf16[256,256]{1,0:T(8,128)(2,1)S(1)}, bf16[256,256]{1,0:T(8,128)(2,1)S(1)}, u32[]{:S(2)}, u32[]{:S(2)}) collective-permute-start(bf16[256,256]{1,0:T(8,128)(2,1)S(1)} %slice.29), channel_id=1, source_target_pairs={{0,520},{8,512},{256,776},{264,768},{512,8},{520,0},{768,264},{776... | collective-permute-start | bytes 393224 | tf_op jit(solution)/shard_map/ppermute | solution.py:60
  138.6 22.8 %collective-permute-done.8 = bf16[256,256]{1,0:T(8,128)(2,1)S(1)} collective-permute-done((bf16[256,256]{1,0:T(8,128)(2,1)S(1)}, bf16[256,256]{1,0:T(8,128)(2,1)S(1)}, u32[]{:S(2)}, u32[]{:S(2)}) %collective-permute-start.8) | collective-permute-done | bytes 131104 | tf_op jit(solution)/shard_map/ppermute | solution.py:60
  161.4 1.9 collective-permute-start.9
  163.3 15.6 %collective-permute-done.9 = bf16[256,256]{1,0:T(8,128)(2,1)S(1)} collective-permute-done((bf16[256,256]{1,0:T(8,128)(2,1)S(1)}, bf16[256,256]{1,0:T(8,128)(2,1)S(1)}, u32[]{:S(2)}, u32[]{:S(2)}) %collective-permute-start.9) | collective-permute-done | bytes 131104 | tf_op jit(solution)/shard_map/ppermute | solution.py:44
  179.0 12.0 %collective-permute-start.10 = (bf16[256,256]{1,0:T(8,128)(2,1)S(1)}, bf16[256,256]{1,0:T(8,128)(2,1)S(1)}, u32[]{:S(2)}, u32[]{:S(2)}) collective-permute-start(bf16[256,256]{1,0:T(8,128)(2,1)S(1)} %add_convert_fusion.1), channel_id=1, source_target_pairs={{0,512},{256,768},{512,0},{768,256},{1,513},{257,769},{513,1},{769... | collective-permute-start | bytes 393224 | tf_op jit(solution)/shard_map/ppermute | solution.py:44
  191.0 19.9 %collective-permute-done.10 = bf16[256,256]{1,0:T(8,128)(2,1)S(1)} collective-permute-done((bf16[256,256]{1,0:T(8,128)(2,1)S(1)}, bf16[256,256]{1,0:T(8,128)(2,1)S(1)}, u32[]{:S(2)}, u32[]{:S(2)}) %collective-permute-start.10) | collective-permute-done | bytes 131104 | tf_op jit(solution)/shard_map/ppermute | solution.py:44
  210.9 0.0 all-to-all-done.3
  210.9 0.8 broadcast_in_dim.2
  211.7 3.5 %all-to-all-start.4 = ((bf16[4,256,256]{2,1,0:T(8,128)(2,1)}), bf16[4,256,256]{2,1,0:T(8,128)(2,1)S(1)}, u32[]{:S(2)}, u32[]{:S(2)}) async-start(bf16[4,256,256]{2,1,0:T(8,128)(2,1)} %broadcast_in_dim.2), calls=%async_computation.4 | async-start | bytes 1048576 | tf_op jit(solution)/shard_map/all_to_all | solution.py:48
  215.2 0.0 copy-start
  215.2 0.0 copy-start.1
  215.2 0.2 copy.17
  215.4 2.9 %collective-permute-start.3 = (bf16[128,1024]{0,1:T(8,128)(2,1)S(1)}, bf16[128,1024]{0,1:T(8,128)(2,1)S(1)}, u32[]{:S(2)}, u32[]{:S(2)}) collective-permute-start(bf16[128,1024]{0,1:T(8,128)(2,1)S(1)} %bitcast.42), channel_id=1, source_target_pairs={{0,0},{2,16},{4,32},{6,48},{16,2},{18,18},{20,34},{22,50},{32,4},{... | collective-permute-start | bytes 786440 | tf_op jit(solution)/shard_map/ppermute | solution.py:210
  218.3 16.3 %collective-permute-done.3 = bf16[128,1024]{0,1:T(8,128)(2,1)S(1)} collective-permute-done((bf16[128,1024]{0,1:T(8,128)(2,1)S(1)}, bf16[128,1024]{0,1:T(8,128)(2,1)S(1)}, u32[]{:S(2)}, u32[]{:S(2)}) %collective-permute-start.3) | collective-permute-done | bytes 262176 | tf_op jit(solution)/shard_map/ppermute | solution.py:210
  234.6 0.8 copy.18
  235.5 0.0 all-to-all-done.4
  235.5 0.0 copy-start.2
  235.5 0.2 fusion
  235.7 0.0 copy-done
  235.7 0.0 copy-done.1
  235.7 1.0 copy-done.2
  236.7 2.1 multiply_subtract_fusion
  (6 shorter events, 0.2 us)
Async XLA Ops:
  1.4 3.1 %collective-permute-start = (bf16[64,256]{1,0:T(8,128)(2,1)S(1)}, bf16[64,256]{1,0:T(8,128)(2,1)S(1)}, u32[]{:S(2)}, u32[]{:S(2)}) collective-permute-start(bf16[64,256]{1,0:T(8,128)(2,1)S(1)} %constant_dynamic-slice_fusion), channel_id=1, source_target_pairs={{0,1},{1,0},{2,3},{3,2},{4,5},{5,4},{6,7},{7,6},{8,9},{9,8},{10,11... | collective-permute-start | bytes 98312 | tf_op jit(solution)/shard_map/ppermute | solution.py:44
  4.5 0.6 copy-start.3
  32.9 43.8 %all-to-all-start.1 = ((bf16[16,64,512]{2,1,0:T(8,128)(2,1)}), bf16[16,64,512]{2,1,0:T(8,128)(2,1)S(1)}, u32[]{:S(2)}, u32[]{:S(2)}) async-start(bf16[16,64,512]{2,1,0:T(8,128)(2,1)} %get-tuple-element.10), calls=%async_computation.1 | async-start | bytes 2097152 | tf_op jit(solution)/shard_map/all_to_all | solution.py:48
  40.1 29.5 %collective-permute-start.1 = (bf16[256,256]{1,0:T(8,128)(2,1)S(1)}, bf16[256,256]{1,0:T(8,128)(2,1)S(1)}, u32[]{:S(2)}, u32[]{:S(2)}) collective-permute-start(bf16[256,256]{1,0:T(8,128)(2,1)S(1)} %dynamic-slice_convert_fusion), channel_id=1, source_target_pairs={{0,520},{8,512},{256,776},{264,768},{512,8},{520,0},{768,264},{776... | collective-permute-start | bytes 393224 | tf_op jit(solution)/shard_map/ppermute | solution.py:60
  70.6 3.4 %collective-permute-start.2 = (bf16[512,256]{1,0:T(8,128)(2,1)S(1)}, bf16[512,256]{1,0:T(8,128)(2,1)S(1)}, u32[]{:S(2)}, u32[]{:S(2)}) collective-permute-start(bf16[512,256]{1,0:T(8,128)(2,1)S(1)} %pad_maximum_fusion.2), channel_id=1, source_target_pairs={{0,1},{1,0},{2,3},{3,2},{4,5},{5,4},{6,7},{7,6},{8,9},{9,8},{10,11... | collective-permute-start | bytes 786440 | tf_op jit(solution)/shard_map/ppermute | solution.py:44
  78.8 35.8 %all-to-all-start.2 = ((bf16[8,256,256]{2,1,0:T(8,128)(2,1)}), bf16[8,256,256]{2,1,0:T(8,128)(2,1)S(1)}, u32[]{:S(2)}, u32[]{:S(2)}) async-start(bf16[8,256,256]{2,1,0:T(8,128)(2,1)} %bitcast.10), calls=%async_computation.2 | async-start | bytes 2097152 | tf_op jit(solution)/shard_map/all_to_all | solution.py:48
  85.3 26.9 %collective-permute-start.6 = (bf16[256,512]{1,0:T(8,128)(2,1)S(1)}, bf16[256,512]{1,0:T(8,128)(2,1)S(1)}, u32[]{:S(2)}, u32[]{:S(2)}) collective-permute-start(bf16[256,512]{1,0:T(8,128)(2,1)S(1)} %bitcast.33), channel_id=1, source_target_pairs={{0,6},{2,4},{4,2},{6,0},{1,7},{3,5},{5,3},{7,1},{8,14},{10,12},{12... | collective-permute-start | bytes 786440 | tf_op jit(solution)/shard_map/ppermute | solution.py:44
  90.4 21.7 %collective-permute-start.5 = (bf16[256,512]{1,0:T(8,128)(2,1)S(1)}, bf16[256,512]{1,0:T(8,128)(2,1)S(1)}, u32[]{:S(2)}, u32[]{:S(2)}) collective-permute-start(bf16[256,512]{1,0:T(8,128)(2,1)S(1)} %bitcast.34), channel_id=1, source_target_pairs={{0,4},{2,6},{4,0},{6,2},{1,5},{3,7},{5,1},{7,3},{8,12},{10,14},{12... | collective-permute-start | bytes 786440 | tf_op jit(solution)/shard_map/ppermute | solution.py:44
  93.2 19.0 %collective-permute-start.4 = (bf16[256,512]{1,0:T(8,128)(2,1)S(1)}, bf16[256,512]{1,0:T(8,128)(2,1)S(1)}, u32[]{:S(2)}, u32[]{:S(2)}) collective-permute-start(bf16[256,512]{1,0:T(8,128)(2,1)S(1)} %bitcast.35), channel_id=1, source_target_pairs={{0,2},{2,0},{4,6},{6,4},{1,3},{3,1},{5,7},{7,5},{8,10},{10,8},{12,... | collective-permute-start | bytes 786440 | tf_op jit(solution)/shard_map/ppermute | solution.py:44
  112.7 11.7 %collective-permute-start.7 = (bf16[512,256]{1,0:T(8,128)(2,1)S(1)}, bf16[512,256]{1,0:T(8,128)(2,1)}, u32[]{:S(2)}, u32[]{:S(2)}) collective-permute-start(bf16[512,256]{1,0:T(8,128)(2,1)S(1)} %shard_map.94), channel_id=1, source_target_pairs={{0,1},{1,0},{2,3},{3,2},{4,5},{5,4},{6,7},{7,6},{8,9},{9,8},{10,11... | collective-permute-start | bytes 786440 | tf_op jit(solution)/shard_map/ppermute | solution.py:44
  117.2 93.7 %all-to-all-start.3 = ((bf16[4,128,256]{2,1,0:T(8,128)(2,1)}), bf16[4,128,256]{2,1,0:T(8,128)(2,1)S(1)}, u32[]{:S(2)}, u32[]{:S(2)}) async-start(bf16[4,128,256]{2,1,0:T(8,128)(2,1)} %bitcast.13), calls=%async_computation.3 | async-start | bytes 524288 | tf_op jit(solution)/shard_map/all_to_all | solution.py:48
  125.4 36.0 %collective-permute-start.8 = (bf16[256,256]{1,0:T(8,128)(2,1)S(1)}, bf16[256,256]{1,0:T(8,128)(2,1)S(1)}, u32[]{:S(2)}, u32[]{:S(2)}) collective-permute-start(bf16[256,256]{1,0:T(8,128)(2,1)S(1)} %slice.29), channel_id=1, source_target_pairs={{0,520},{8,512},{256,776},{264,768},{512,8},{520,0},{768,264},{776... | collective-permute-start | bytes 393224 | tf_op jit(solution)/shard_map/ppermute | solution.py:60
  161.4 17.6 %collective-permute-start.9 = (bf16[256,256]{1,0:T(8,128)(2,1)S(1)}, bf16[256,256]{1,0:T(8,128)(2,1)S(1)}, u32[]{:S(2)}, u32[]{:S(2)}) collective-permute-start(bf16[256,256]{1,0:T(8,128)(2,1)S(1)} %fusion.1), channel_id=1, source_target_pairs={{0,256},{256,0},{512,768},{768,512},{1,257},{257,1},{513,769},{769... | collective-permute-start | bytes 393224 | tf_op jit(solution)/shard_map/ppermute | solution.py:44
  179.0 31.9 %collective-permute-start.10 = (bf16[256,256]{1,0:T(8,128)(2,1)S(1)}, bf16[256,256]{1,0:T(8,128)(2,1)S(1)}, u32[]{:S(2)}, u32[]{:S(2)}) collective-permute-start(bf16[256,256]{1,0:T(8,128)(2,1)S(1)} %add_convert_fusion.1), channel_id=1, source_target_pairs={{0,512},{256,768},{512,0},{768,256},{1,513},{257,769},{513,1},{769... | collective-permute-start | bytes 393224 | tf_op jit(solution)/shard_map/ppermute | solution.py:44
  211.7 23.7 %all-to-all-start.4 = ((bf16[4,256,256]{2,1,0:T(8,128)(2,1)}), bf16[4,256,256]{2,1,0:T(8,128)(2,1)S(1)}, u32[]{:S(2)}, u32[]{:S(2)}) async-start(bf16[4,256,256]{2,1,0:T(8,128)(2,1)} %broadcast_in_dim.2), calls=%async_computation.4 | async-start | bytes 1048576 | tf_op jit(solution)/shard_map/all_to_all | solution.py:48
  215.2 20.5 %copy-start = (f32[1024,256]{1,0:T(8,128)S(1)}, f32[1024,256]{1,0:T(8,128)}, u32[]{:S(2)}) copy-start(f32[1024,256]{1,0:T(8,128)} %param.9) | copy-start | bytes 3145732
  215.2 20.5 %copy-start.1 = (f32[1024,256]{1,0:T(8,128)S(1)}, f32[1024,256]{1,0:T(8,128)}, u32[]{:S(2)}) copy-start(f32[1024,256]{1,0:T(8,128)} %param.10) | copy-start | bytes 3145732
  215.4 19.2 %collective-permute-start.3 = (bf16[128,1024]{0,1:T(8,128)(2,1)S(1)}, bf16[128,1024]{0,1:T(8,128)(2,1)S(1)}, u32[]{:S(2)}, u32[]{:S(2)}) collective-permute-start(bf16[128,1024]{0,1:T(8,128)(2,1)S(1)} %bitcast.42), channel_id=1, source_target_pairs={{0,0},{2,16},{4,32},{6,48},{16,2},{18,18},{20,34},{22,50},{32,4},{... | collective-permute-start | bytes 786440 | tf_op jit(solution)/shard_map/ppermute | solution.py:210
  235.5 1.2 copy-start.2

commit v7 on v6

--- a/solution.py
+++ b/solution.py
@@ -65,21 +65,36 @@
     return jnp.where(flip, pair[0], pair[1]), jnp.where(flip, pair[1], pair[0])
 
 
-def share_kernel(
-    nzb, seq_len, where_ref, lengths_ref, act_ref, own_ref, other_ref, mine_ref, copies_ref
-):
+def share_kernel(nzb, where_ref, act_ref, mine_ref):
     near, _, width = mine_ref.shape
-    half, part = own_ref.shape[0], width // 2
-    cols = own_ref.shape[1]
-    ny = near // nzb
-    h, c = where_ref[1], where_ref[2]
+    part, ny = width // 2, near // nzb
+    h = where_ref[1]
     for k in range(near):
         zb, y = k // ny, k % ny
         for side, far in enumerate((1 - h, h)):
             start = ((y * 2 + far) * nzb + zb) * part
             block = act_ref[:, pl.ds(pl.multiple_of(start, part), part)]
             mine_ref[k, :, side * part : (side + 1) * part] = block
-    index = c * half + lax.broadcasted_iota(jnp.int32, (half, cols), 0)
+
+
+def share_of(where, activations, nzb, ny, share, part):
+    shape = (nzb * ny, share, 2 * part)
+    return pl.pallas_call(
+        functools.partial(share_kernel, nzb),
+        out_shape=jax.ShapeDtypeStruct(shape, activations.dtype),
+        grid_spec=pltpu.PrefetchScalarGridSpec(
+            num_scalar_prefetch=1,
+            grid=(1,),
+            in_specs=[pl.BlockSpec((share, activations.shape[1]), lambda i, where: (where[0], 0))],
+            out_specs=pl.BlockSpec(shape, lambda i, where: (0, 0, 0)),
+        ),
+        name="share",
+    )(where, activations)
+
+
+def copies_kernel(seq_len, where_ref, lengths_ref, own_ref, other_ref, copies_ref):
+    half, cols = own_ref.shape
+    index = where_ref[2] * half + lax.broadcasted_iota(jnp.int32, (half, cols), 0)
     live = None
     for k in range(lengths_ref.shape[0]):
         inside = (index >= k * seq_len) & (index < k * seq_len + lengths_ref[k])
@@ -87,43 +102,45 @@
     for side, ref in enumerate((own_ref, other_ref)):
         block = ref[...].astype(F32)
         block = jnp.where(live, block, jnp.zeros_like(block)).astype(copies_ref.dtype)
-        for k in range(near):
+        for k in range(copies_ref.shape[0]):
             copies_ref[k, :, side * cols : (side + 1) * cols] = block
 
 
-def near_pieces(where, lengths, activations, value_grads, other, nzb, ny, share, part):
-    tok, width = activations.shape
+def copies_of(where, lengths, value_grads, other, count):
     half, cols = other.shape
-    shapes = ((nzb * ny, share, 2 * part), (nzb * ny, half, 2 * cols))
+    shape = (count, half, 2 * cols)
     return pl.pallas_call(
-        functools.partial(share_kernel, nzb, tok // lengths.shape[0]),
-        out_shape=[jax.ShapeDtypeStruct(shape, activations.dtype) for shape in shapes],
+        functools.partial(copies_kernel, value_grads.shape[0] // lengths.shape[0]),
+        out_shape=jax.ShapeDtypeStruct(shape, value_grads.dtype),
         grid_spec=pltpu.PrefetchScalarGridSpec(
             num_scalar_prefetch=2,
             grid=(1,),
             in_specs=[
-                pl.BlockSpec((share, width), lambda i, where, lengths: (where[0], 0)),
                 pl.BlockSpec((half, cols), lambda i, where, lengths: (where[2], 0)),
                 pl.BlockSpec((half, cols), lambda i, where, lengths: (0, 0)),
             ],
-            out_specs=[pl.BlockSpec(shape, lambda i, where, lengths: (0, 0, 0)) for shape in shapes],
+            out_specs=pl.BlockSpec(shape, lambda i, where, lengths: (0, 0, 0)),
         ),
-        name="share",
-    )(where, lengths, activations, value_grads, other)
+        name="copies",
+    )(where, lengths, value_grads, other)
 
 
 def outer_kernel(half, x_ref, *refs):
     *pieces, grads_ref, out_ref = refs
-    near, tok, _ = grads_ref.shape
+    ny, nzb, tok, _ = grads_ref.shape
     share = tok // len(pieces)
     cols = out_ref.shape[1]
     total = None
     for k, piece in enumerate(pieces):
         start = pl.multiple_of((x_ref[0] ^ k) * share, share)
-        grads = grads_ref[:, pl.ds(start, share), half * cols : (half + 1) * cols]
+        grads = [
+            grads_ref[y, zb, pl.ds(start, share), half * cols : (half + 1) * cols]
+            for zb in range(nzb)
+            for y in range(ny)
+        ]
         term = lax.dot_general(
             piece[...],
-            grads.reshape(near * share, cols),
+            jnp.concatenate(grads, axis=0),
             (((0,), (0,)), ((), ())),
             preferred_element_type=F32,
         )
@@ -132,7 +149,7 @@
 
 
 def outer(x, pieces, grads, half, dtype):
-    rows, cols = pieces[0].shape[1], grads.shape[2] // 2
+    rows, cols = pieces[0].shape[1], grads.shape[3] // 2
     vmem = pl.BlockSpec(memory_space=pltpu.VMEM)
     depth = sum(piece.shape[0] for piece in pieces)
     return pl.pallas_call(
@@ -167,12 +184,12 @@
     weight_far = across(weight)
 
     where = jnp.stack([c * nx + x, h, c]).astype(jnp.int32)
-    mine, copies = near_pieces(
-        where, lengths, activations, value_grads, vg_other, nzb, ny, share, part
-    )
+    mine = share_of(where, activations, nzb, ny, share, part)
     act_share = exchanged(mine, NEAR)
+    copies = copies_of(where, lengths, value_grads, vg_other, nzb)
     copies, act_share = lax.optimization_barrier((copies, act_share))
-    grads = exchanged(copies, NEAR)
+    vg_near = exchanged(copies, "zb").reshape(nzb * half, 2 * cols)
+    grads = gathered(vg_near, "y").reshape(ny, nzb, half, 2 * cols)
     act_share = act_share.reshape(near * share, 2 * part)
     pieces = [act_share]
     for k in range(1, nx):
@@ -198,7 +215,7 @@
 
     def product(w):
         out = lax.dot_general(tokens, w, (((1,), (1,)), ((), ())), preferred_element_type=F32)
-        return out.astype(BF16).reshape(nzb, ny, half, part).transpose(1, 0, 2, 3)
+        return out.astype(BF16).reshape(ny, nzb, half, part)
 
     product = jnp.stack([product(both[:part]), product(both[part:])], axis=1)
     arrived = exchanged(product.reshape(ny * 2, nzb * half, part), COLS)

time: 240 us -> 228 us (0.950)
  the two profiles are of different devices: /device:TPU:24 before, /device:TPU:6 now
where the time goes in v7:
time: 228 us; the launch traced here: 226 us
  waiting for transfers between devices  114 us (50%)
  starting transfers between devices  90.7 us (40%)
  local copies, waits for them, and re-layouts  7.2 us (3%)
  other arithmetic  7.06 us (3%)
  Pallas kernels  5.5 us (2%)
    ppermute x8, waiting for transfers between devices, swapped(): return lax.ppermute(array, axis, [(k, k ^ bit) for k in range(size)])  55.5 us
    ppermute x2, waiting for transfers between devices, across(): return lax.ppermute(array, ('za', 'h'), pairs)  39.5 us
    ppermute x2, starting transfers between devices, across(): return lax.ppermute(array, ('za', 'h'), pairs)  33.4 us
    all_to_all x6, starting transfers between devices, exchanged(): return lax.all_to_all(pieces, axes, split_axis=0, concat_axis=0, tiled=True)  27.2 us
    ppermute x8, starting transfers between devices, swapped(): return lax.ppermute(array, axis, [(k, k ^ bit) for k in range(size)])  25.2 us
    ppermute x1, waiting for transfers between devices, step(): input_grads = lax.ppermute(block, ('y', 'x'), turn)  14.3 us
    ppermute x1, starting transfers between devices, step(): input_grads = lax.ppermute(block, ('y', 'x'), turn)  4.89 us
    all_to_all x6, waiting for transfers between devices, exchanged(): return lax.all_to_all(pieces, axes, split_axis=0, concat_axis=0, tiled=True)  4.76 us
  transfers between devices with their start and end apart: 17, of which 10 were waited for; matrix products, arithmetic and copies ran while one was open for 3% of the time, Pallas kernels for 1%

profile of v7, /device:TPU:6, one launch (start us, length us, event | category | flops | bytes accessed | tf_op | source)
XLA Modules:
  0.0 226.5 jit_solution(618844739402584454)
XLA Ops:
  0.6 0.0 copy-start.3
  0.7 0.7 pad_add_fusion.where_ref
  1.3 2.4 %share.1 = bf16[16,16,512]{2,1,0:T(8,128)(2,1)} custom-call(s32[3]{0:T(128)} %pad_add_fusion.where_ref, bf16[128,8192]{1,0:T(8,128)(2,1)} %act_ref.1), custom_call_target="tpu_custom_call" | custom-call | tf_op jit(solution)/shard_map/share/pallas_call | solution.py:82
  3.7 8.6 %all-to-all-start = ((bf16[16,16,512]{2,1,0:T(8,128)(2,1)}), bf16[16,16,512]{2,1,0:T(8,128)(2,1)S(1)}, u32[]{:S(2)}, u32[]{:S(2)}) async-start(bf16[16,16,512]{2,1,0:T(8,128)(2,1)} %share.1), calls=%async_computation | async-start | bytes 524288 | tf_op jit(solution)/shard_map/all_to_all | solution.py:48
  12.3 0.0 copy-done.3
  12.4 1.9 collective-permute-start
  14.3 1.2 collective-permute-done.other_ref
  15.5 0.0 copy-start.4
  15.5 0.6 copy-done.4
  16.1 2.2 copies.1
  18.2 4.7 %all-to-all-done = bf16[16,16,512]{2,1,0:T(8,128)(2,1)S(1)} async-done(((bf16[16,16,512]{2,1,0:T(8,128)(2,1)}), bf16[16,16,512]{2,1,0:T(8,128)(2,1)S(1)}, u32[]{:S(2)}, u32[]{:S(2)}) %all-to-all-start) | async-done | bytes 262176 | tf_op jit(solution)/shard_map/all_to_all | solution.py:48
  23.0 3.4 %all-to-all-start.1 = ((bf16[4,64,512]{2,1,0:T(8,128)(2,1)}), bf16[4,64,512]{2,1,0:T(8,128)(2,1)S(1)}, u32[]{:S(2)}, u32[]{:S(2)}) async-start(bf16[4,64,512]{2,1,0:T(8,128)(2,1)} %copies.1), calls=%async_computation.1 | async-start | bytes 524288 | tf_op jit(solution)/shard_map/all_to_all | solution.py:48
  26.4 1.0 dynamic-slice_convert_fusion
  27.4 20.3 %collective-permute-start.1 = (bf16[256,256]{1,0:T(8,128)(2,1)S(1)}, bf16[256,256]{1,0:T(8,128)(2,1)S(1)}, u32[]{:S(2)}, u32[]{:S(2)}) collective-permute-start(bf16[256,256]{1,0:T(8,128)(2,1)S(1)} %dynamic-slice_convert_fusion), channel_id=1, source_target_pairs={{0,520},{8,512},{256,776},{264,768},{512,8},{520,0},{768,264},{776... | collective-permute-start | bytes 393224 | tf_op jit(solution)/shard_map/ppermute | solution.py:60
  47.7 0.0 all-to-all-done.1
  47.7 1.1 broadcast_in_dim.14
  48.8 3.5 %all-to-all-start.2 = ((bf16[4,256,512]{2,1,0:T(8,128)(2,1)}), bf16[4,256,512]{2,1,0:T(8,128)(2,1)S(1)}, u32[]{:S(2)}, u32[]{:S(2)}) async-start(bf16[4,256,512]{2,1,0:T(8,128)(2,1)} %broadcast_in_dim.14), calls=%async_computation.2 | async-start | bytes 2097152 | tf_op jit(solution)/shard_map/all_to_all | solution.py:48
  52.3 16.4 %collective-permute-done.1 = bf16[256,256]{1,0:T(8,128)(2,1)S(1)} collective-permute-done((bf16[256,256]{1,0:T(8,128)(2,1)S(1)}, bf16[256,256]{1,0:T(8,128)(2,1)S(1)}, u32[]{:S(2)}, u32[]{:S(2)}) %collective-permute-start.1) | collective-permute-done | bytes 131104 | tf_op jit(solution)/shard_map/ppermute | solution.py:60
  68.7 1.0 broadcast_select_fusion.1
  69.7 1.9 collective-permute-start.2
  71.7 1.5 collective-permute-done.2
  73.2 0.0 all-to-all-done.2
  73.2 0.5 convolution_convert_fusion
  73.7 0.5 convolution_convert_fusion.1
  74.2 1.1 pad_maximum_fusion
  75.2 4.8 %all-to-all-start.3 = ((bf16[8,256,256]{2,1,0:T(8,128)(2,1)}), bf16[8,256,256]{2,1,0:T(8,128)(2,1)S(1)}, u32[]{:S(2)}, u32[]{:S(2)}) async-start(bf16[8,256,256]{2,1,0:T(8,128)(2,1)} %bitcast.9), calls=%async_computation.3 | async-start | bytes 2097152 | tf_op jit(solution)/shard_map/all_to_all | solution.py:48
  80.0 1.9 collective-permute-start.6
  81.9 4.8 %collective-permute-start.5 = (bf16[256,512]{1,0:T(8,128)(2,1)S(1)}, bf16[256,512]{1,0:T(8,128)(2,1)S(1)}, u32[]{:S(2)}, u32[]{:S(2)}) collective-permute-start(bf16[256,512]{1,0:T(8,128)(2,1)S(1)} %bitcast.34), channel_id=1, source_target_pairs={{0,4},{2,6},{4,0},{6,2},{1,5},{3,7},{5,1},{7,3},{8,12},{10,14},{12... | collective-permute-start | bytes 786440 | tf_op jit(solution)/shard_map/ppermute | solution.py:44
  86.7 3.1 %collective-permute-start.4 = (bf16[256,512]{1,0:T(8,128)(2,1)S(1)}, bf16[256,512]{1,0:T(8,128)(2,1)S(1)}, u32[]{:S(2)}, u32[]{:S(2)}) collective-permute-start(bf16[256,512]{1,0:T(8,128)(2,1)S(1)} %bitcast.35), channel_id=1, source_target_pairs={{0,2},{2,0},{4,6},{6,4},{1,3},{3,1},{5,7},{7,5},{8,10},{10,8},{12,... | collective-permute-start | bytes 786440 | tf_op jit(solution)/shard_map/ppermute | solution.py:44
  89.8 14.2 %collective-permute-done.6.refs_3_ = bf16[256,512]{1,0:T(8,128)(2,1)S(1)} collective-permute-done((bf16[256,512]{1,0:T(8,128)(2,1)S(1)}, bf16[256,512]{1,0:T(8,128)(2,1)S(1)}, u32[]{:S(2)}, u32[]{:S(2)}) %collective-permute-start.6) | collective-permute-done | bytes 262176 | tf_op jit(solution)/shard_map/ppermute | solution.py:44
  104.0 0.0 collective-permute-done.5.refs_2_
  104.0 0.5 collective-permute-done.4.refs_1_
  104.5 0.5 shard_map.94
  105.0 1.9 collective-permute-start.7
  107.0 0.0 all-to-all-done.3
  107.0 0.9 reduce_sum.12
  107.9 1.7 copy.16
  109.6 3.4 %all-to-all-start.4 = ((bf16[4,128,256]{2,1,0:T(8,128)(2,1)}), bf16[4,128,256]{2,1,0:T(8,128)(2,1)S(1)}, u32[]{:S(2)}, u32[]{:S(2)}) async-start(bf16[4,128,256]{2,1,0:T(8,128)(2,1)} %bitcast.12), calls=%async_computation.4 | async-start | bytes 524288 | tf_op jit(solution)/shard_map/all_to_all | solution.py:48
  113.0 0.5 shard_map.93
  113.5 0.0 collective-permute-done.7
  113.5 1.0 convert_add_fusion
  114.5 13.1 %collective-permute-start.8 = (bf16[256,256]{1,0:T(8,128)(2,1)S(1)}, bf16[256,256]{1,0:T(8,128)(2,1)S(1)}, u32[]{:S(2)}, u32[]{:S(2)}) collective-permute-start(bf16[256,256]{1,0:T(8,128)(2,1)S(1)} %slice.29), channel_id=1, source_target_pairs={{0,520},{8,512},{256,776},{264,768},{512,8},{520,0},{768,264},{776... | collective-permute-start | bytes 393224 | tf_op jit(solution)/shard_map/ppermute | solution.py:60
  127.6 23.1 %collective-permute-done.8 = bf16[256,256]{1,0:T(8,128)(2,1)S(1)} collective-permute-done((bf16[256,256]{1,0:T(8,128)(2,1)S(1)}, bf16[256,256]{1,0:T(8,128)(2,1)S(1)}, u32[]{:S(2)}, u32[]{:S(2)}) %collective-permute-start.8) | collective-permute-done | bytes 131104 | tf_op jit(solution)/shard_map/ppermute | solution.py:60
  150.7 1.9 collective-permute-start.9
  152.6 15.4 %collective-permute-done.9 = bf16[256,256]{1,0:T(8,128)(2,1)S(1)} collective-permute-done((bf16[256,256]{1,0:T(8,128)(2,1)S(1)}, bf16[256,256]{1,0:T(8,128)(2,1)S(1)}, u32[]{:S(2)}, u32[]{:S(2)}) %collective-permute-start.9) | collective-permute-done | bytes 131104 | tf_op jit(solution)/shard_map/ppermute | solution.py:44
  168.1 7.8 %collective-permute-start.10 = (bf16[256,256]{1,0:T(8,128)(2,1)S(1)}, bf16[256,256]{1,0:T(8,128)(2,1)S(1)}, u32[]{:S(2)}, u32[]{:S(2)}) collective-permute-start(bf16[256,256]{1,0:T(8,128)(2,1)S(1)} %add_convert_fusion.1), channel_id=1, source_target_pairs={{0,512},{256,768},{512,0},{768,256},{1,513},{257,769},{513,1},{769... | collective-permute-start | bytes 393224 | tf_op jit(solution)/shard_map/ppermute | solution.py:44
  175.9 22.7 %collective-permute-done.10 = bf16[256,256]{1,0:T(8,128)(2,1)S(1)} collective-permute-done((bf16[256,256]{1,0:T(8,128)(2,1)S(1)}, bf16[256,256]{1,0:T(8,128)(2,1)S(1)}, u32[]{:S(2)}, u32[]{:S(2)}) %collective-permute-start.10) | collective-permute-done | bytes 131104 | tf_op jit(solution)/shard_map/ppermute | solution.py:44
  198.6 0.0 all-to-all-done.4
  198.6 0.8 broadcast_in_dim.15
  199.4 3.5 %all-to-all-start.5 = ((bf16[4,256,256]{2,1,0:T(8,128)(2,1)}), bf16[4,256,256]{2,1,0:T(8,128)(2,1)S(1)}, u32[]{:S(2)}, u32[]{:S(2)}) async-start(bf16[4,256,256]{2,1,0:T(8,128)(2,1)} %broadcast_in_dim.15), calls=%async_computation.5 | async-start | bytes 1048576 | tf_op jit(solution)/shard_map/all_to_all | solution.py:48
  202.9 0.0 copy-start
  202.9 0.0 copy-start.1
  202.9 0.2 copy.17
  203.1 4.9 %collective-permute-start.3 = (bf16[128,1024]{0,1:T(8,128)(2,1)S(1)}, bf16[128,1024]{0,1:T(8,128)(2,1)S(1)}, u32[]{:S(2)}, u32[]{:S(2)}) collective-permute-start(bf16[128,1024]{0,1:T(8,128)(2,1)S(1)} %bitcast.43), channel_id=1, source_target_pairs={{0,0},{2,16},{4,32},{6,48},{16,2},{18,18},{20,34},{22,50},{32,4},{... | collective-permute-start | bytes 786440 | tf_op jit(solution)/shard_map/ppermute | solution.py:227
  208.0 14.3 %collective-permute-done.3 = bf16[128,1024]{0,1:T(8,128)(2,1)S(1)} collective-permute-done((bf16[128,1024]{0,1:T(8,128)(2,1)S(1)}, bf16[128,1024]{0,1:T(8,128)(2,1)S(1)}, u32[]{:S(2)}, u32[]{:S(2)}) %collective-permute-start.3) | collective-permute-done | bytes 262176 | tf_op jit(solution)/shard_map/ppermute | solution.py:227
  222.3 0.8 copy.18
  223.2 0.0 all-to-all-done.5
  223.2 0.0 copy-start.2
  223.2 0.2 fusion
  223.4 0.0 copy-done
  223.4 0.0 copy-done.1
  223.4 1.0 copy-done.2
  224.4 2.1 multiply_subtract_fusion
  (7 shorter events, 0.2 us)
Async XLA Ops:
  0.6 11.7 %copy-start.3 = (bf16[128,256]{1,0:T(8,128)(2,1)S(1)}, bf16[128,256]{1,0:T(8,128)(2,1)}, u32[]{:S(2)}) copy-start(bf16[128,256]{1,0:T(8,128)(2,1)} %own_ref.1) | copy-start | bytes 196612
  3.7 19.3 %all-to-all-start = ((bf16[16,16,512]{2,1,0:T(8,128)(2,1)}), bf16[16,16,512]{2,1,0:T(8,128)(2,1)S(1)}, u32[]{:S(2)}, u32[]{:S(2)}) async-start(bf16[16,16,512]{2,1,0:T(8,128)(2,1)} %share.1), calls=%async_computation | async-start | bytes 524288 | tf_op jit(solution)/shard_map/all_to_all | solution.py:48
  12.4 3.1 %collective-permute-start = (bf16[64,256]{1,0:T(8,128)(2,1)S(1)}, bf16[64,256]{1,0:T(8,128)(2,1)S(1)}, u32[]{:S(2)}, u32[]{:S(2)}) collective-permute-start(bf16[64,256]{1,0:T(8,128)(2,1)S(1)} %constant_dynamic-slice_fusion), channel_id=1, source_target_pairs={{0,1},{1,0},{2,3},{3,2},{4,5},{5,4},{6,7},{7,6},{8,9},{9,8},{10,11... | collective-permute-start | bytes 98312 | tf_op jit(solution)/shard_map/ppermute | solution.py:44
  15.5 0.6 copy-start.4
  23.0 24.7 %all-to-all-start.1 = ((bf16[4,64,512]{2,1,0:T(8,128)(2,1)}), bf16[4,64,512]{2,1,0:T(8,128)(2,1)S(1)}, u32[]{:S(2)}, u32[]{:S(2)}) async-start(bf16[4,64,512]{2,1,0:T(8,128)(2,1)} %copies.1), calls=%async_computation.1 | async-start | bytes 524288 | tf_op jit(solution)/shard_map/all_to_all | solution.py:48
  27.4 41.3 %collective-permute-start.1 = (bf16[256,256]{1,0:T(8,128)(2,1)S(1)}, bf16[256,256]{1,0:T(8,128)(2,1)S(1)}, u32[]{:S(2)}, u32[]{:S(2)}) collective-permute-start(bf16[256,256]{1,0:T(8,128)(2,1)S(1)} %dynamic-slice_convert_fusion), channel_id=1, source_target_pairs={{0,520},{8,512},{256,776},{264,768},{512,8},{520,0},{768,264},{776... | collective-permute-start | bytes 393224 | tf_op jit(solution)/shard_map/ppermute | solution.py:60
  48.8 24.4 %all-to-all-start.2 = ((bf16[4,256,512]{2,1,0:T(8,128)(2,1)}), bf16[4,256,512]{2,1,0:T(8,128)(2,1)S(1)}, u32[]{:S(2)}, u32[]{:S(2)}) async-start(bf16[4,256,512]{2,1,0:T(8,128)(2,1)} %broadcast_in_dim.14), calls=%async_computation.2 | async-start | bytes 2097152 | tf_op jit(solution)/shard_map/all_to_all | solution.py:48
  69.7 3.4 %collective-permute-start.2 = (bf16[512,256]{1,0:T(8,128)(2,1)S(1)}, bf16[512,256]{1,0:T(8,128)(2,1)S(1)}, u32[]{:S(2)}, u32[]{:S(2)}) collective-permute-start(bf16[512,256]{1,0:T(8,128)(2,1)S(1)} %pad_maximum_fusion.2), channel_id=1, source_target_pairs={{0,1},{1,0},{2,3},{3,2},{4,5},{5,4},{6,7},{7,6},{8,9},{9,8},{10,11... | collective-permute-start | bytes 786440 | tf_op jit(solution)/shard_map/ppermute | solution.py:44
  75.2 31.7 %all-to-all-start.3 = ((bf16[8,256,256]{2,1,0:T(8,128)(2,1)}), bf16[8,256,256]{2,1,0:T(8,128)(2,1)S(1)}, u32[]{:S(2)}, u32[]{:S(2)}) async-start(bf16[8,256,256]{2,1,0:T(8,128)(2,1)} %bitcast.9), calls=%async_computation.3 | async-start | bytes 2097152 | tf_op jit(solution)/shard_map/all_to_all | solution.py:48
  80.0 24.0 %collective-permute-start.6 = (bf16[256,512]{1,0:T(8,128)(2,1)S(1)}, bf16[256,512]{1,0:T(8,128)(2,1)S(1)}, u32[]{:S(2)}, u32[]{:S(2)}) collective-permute-start(bf16[256,512]{1,0:T(8,128)(2,1)S(1)} %bitcast.33), channel_id=1, source_target_pairs={{0,6},{2,4},{4,2},{6,0},{1,7},{3,5},{5,3},{7,1},{8,14},{10,12},{12... | collective-permute-start | bytes 786440 | tf_op jit(solution)/shard_map/ppermute | solution.py:44
  81.9 22.1 %collective-permute-start.5 = (bf16[256,512]{1,0:T(8,128)(2,1)S(1)}, bf16[256,512]{1,0:T(8,128)(2,1)S(1)}, u32[]{:S(2)}, u32[]{:S(2)}) collective-permute-start(bf16[256,512]{1,0:T(8,128)(2,1)S(1)} %bitcast.34), channel_id=1, source_target_pairs={{0,4},{2,6},{4,0},{6,2},{1,5},{3,7},{5,1},{7,3},{8,12},{10,14},{12... | collective-permute-start | bytes 786440 | tf_op jit(solution)/shard_map/ppermute | solution.py:44
  86.7 17.8 %collective-permute-start.4 = (bf16[256,512]{1,0:T(8,128)(2,1)S(1)}, bf16[256,512]{1,0:T(8,128)(2,1)S(1)}, u32[]{:S(2)}, u32[]{:S(2)}) collective-permute-start(bf16[256,512]{1,0:T(8,128)(2,1)S(1)} %bitcast.35), channel_id=1, source_target_pairs={{0,2},{2,0},{4,6},{6,4},{1,3},{3,1},{5,7},{7,5},{8,10},{10,8},{12,... | collective-permute-start | bytes 786440 | tf_op jit(solution)/shard_map/ppermute | solution.py:44
  105.0 8.4 %collective-permute-start.7 = (bf16[512,256]{1,0:T(8,128)(2,1)S(1)}, bf16[512,256]{1,0:T(8,128)(2,1)}, u32[]{:S(2)}, u32[]{:S(2)}) collective-permute-start(bf16[512,256]{1,0:T(8,128)(2,1)S(1)} %shard_map.94), channel_id=1, source_target_pairs={{0,1},{1,0},{2,3},{3,2},{4,5},{5,4},{6,7},{7,6},{8,9},{9,8},{10,11... | collective-permute-start | bytes 786440 | tf_op jit(solution)/shard_map/ppermute | solution.py:44
  109.6 89.0 %all-to-all-start.4 = ((bf16[4,128,256]{2,1,0:T(8,128)(2,1)}), bf16[4,128,256]{2,1,0:T(8,128)(2,1)S(1)}, u32[]{:S(2)}, u32[]{:S(2)}) async-start(bf16[4,128,256]{2,1,0:T(8,128)(2,1)} %bitcast.12), calls=%async_computation.4 | async-start | bytes 524288 | tf_op jit(solution)/shard_map/all_to_all | solution.py:48
  114.5 36.2 %collective-permute-start.8 = (bf16[256,256]{1,0:T(8,128)(2,1)S(1)}, bf16[256,256]{1,0:T(8,128)(2,1)S(1)}, u32[]{:S(2)}, u32[]{:S(2)}) collective-permute-start(bf16[256,256]{1,0:T(8,128)(2,1)S(1)} %slice.29), channel_id=1, source_target_pairs={{0,520},{8,512},{256,776},{264,768},{512,8},{520,0},{768,264},{776... | collective-permute-start | bytes 393224 | tf_op jit(solution)/shard_map/ppermute | solution.py:60
  150.7 17.4 %collective-permute-start.9 = (bf16[256,256]{1,0:T(8,128)(2,1)S(1)}, bf16[256,256]{1,0:T(8,128)(2,1)S(1)}, u32[]{:S(2)}, u32[]{:S(2)}) collective-permute-start(bf16[256,256]{1,0:T(8,128)(2,1)S(1)} %fusion.1), channel_id=1, source_target_pairs={{0,256},{256,0},{512,768},{768,512},{1,257},{257,1},{513,769},{769... | collective-permute-start | bytes 393224 | tf_op jit(solution)/shard_map/ppermute | solution.py:44
  168.1 30.4 %collective-permute-start.10 = (bf16[256,256]{1,0:T(8,128)(2,1)S(1)}, bf16[256,256]{1,0:T(8,128)(2,1)S(1)}, u32[]{:S(2)}, u32[]{:S(2)}) collective-permute-start(bf16[256,256]{1,0:T(8,128)(2,1)S(1)} %add_convert_fusion.1), channel_id=1, source_target_pairs={{0,512},{256,768},{512,0},{768,256},{1,513},{257,769},{513,1},{769... | collective-permute-start | bytes 393224 | tf_op jit(solution)/shard_map/ppermute | solution.py:44
  199.4 23.7 %all-to-all-start.5 = ((bf16[4,256,256]{2,1,0:T(8,128)(2,1)}), bf16[4,256,256]{2,1,0:T(8,128)(2,1)S(1)}, u32[]{:S(2)}, u32[]{:S(2)}) async-start(bf16[4,256,256]{2,1,0:T(8,128)(2,1)} %broadcast_in_dim.15), calls=%async_computation.5 | async-start | bytes 1048576 | tf_op jit(solution)/shard_map/all_to_all | solution.py:48
  202.9 20.5 %copy-start = (f32[1024,256]{1,0:T(8,128)S(1)}, f32[1024,256]{1,0:T(8,128)}, u32[]{:S(2)}) copy-start(f32[1024,256]{1,0:T(8,128)} %param.9) | copy-start | bytes 3145732
  202.9 20.5 %copy-start.1 = (f32[1024,256]{1,0:T(8,128)S(1)}, f32[1024,256]{1,0:T(8,128)}, u32[]{:S(2)}) copy-start(f32[1024,256]{1,0:T(8,128)} %param.10) | copy-start | bytes 3145732
  203.1 19.2 %collective-permute-start.3 = (bf16[128,1024]{0,1:T(8,128)(2,1)S(1)}, bf16[128,1024]{0,1:T(8,128)(2,1)S(1)}, u32[]{:S(2)}, u32[]{:S(2)}) collective-permute-start(bf16[128,1024]{0,1:T(8,128)(2,1)S(1)} %bitcast.43), channel_id=1, source_target_pairs={{0,0},{2,16},{4,32},{6,48},{16,2},{18,18},{20,34},{22,50},{32,4},{... | collective-permute-start | bytes 786440 | tf_op jit(solution)/shard_map/ppermute | solution.py:227
  223.2 1.2 copy-start.2
